TPU v7x, 32 devices: a whole 2x2x4 slice. The times are simulated.
32 devices in a mesh: ctx: 8 (over z, y), wsh: 4 (over x, core).
Axes of the slice: x: 2, y: 2, z: 4, core: 2. Of those that a mesh axis runs over, the one named last changes fastest.
Arguments:
- tokens: bfloat16 [4, 8192, 768], P('wsh', 'ctx'), may hold values from -6 to 6
- cotangent: bfloat16 [4, 8192, 768], P('wsh', 'ctx'), may hold values from -6 to 6
- random_blocks: int32 [4, 128, 3], P('wsh'), may hold values from 16 to 111, as said below
- query_weight: bfloat16 [768, 768], P('wsh'), may hold values from -0.21875 to 0.21875
- query_bias: bfloat16 [768], P('wsh'), may hold values from -3 to 3
- key_weight: bfloat16 [768, 768], P('wsh'), may hold values from -0.21875 to 0.21875
- value_weight: bfloat16 [768, 768], P('wsh'), may hold values from -0.21875 to 0.21875
- value_bias: bfloat16 [768], P('wsh'), may hold values from -1.1953125 to 1.1953125
- output_weight: bfloat16 [768, 768], P('wsh'), may hold values from -1.75 to 1.75
- output_bias: bfloat16 [768], P('wsh'), may hold values from -1.796875 to 1.796875
- first_gain: bfloat16 [768], P('wsh'), may hold values from 0.5 to 1.5
- first_shift: bfloat16 [768], P('wsh'), may hold values from -1.1953125 to 1.1953125
- inner_weight: bfloat16 [768, 3072], P('wsh'), may hold values from -0.21875 to 0.21875
- inner_bias: bfloat16 [3072], P('wsh'), may hold values from -1.796875 to 1.796875
- outer_weight: bfloat16 [3072, 768], P('wsh'), may hold values from -0.109375 to 0.109375
- outer_bias: bfloat16 [768], P('wsh'), may hold values from -1.796875 to 1.796875
- second_gain: bfloat16 [768], P('wsh'), may hold values from 0.5 to 1.5
- second_shift: bfloat16 [768], P('wsh'), may hold values from -1.1953125 to 1.1953125
Outputs:
- layer_output: bfloat16 [4, 8192, 768], P('wsh', 'ctx')
- tokens_grad: bfloat16 [4, 8192, 768], P('wsh', 'ctx')
- query_weight_grad: float32 [768, 768], P('wsh')
- query_bias_grad: float32 [768], P('wsh')
- key_weight_grad: float32 [768, 768], P('wsh')
- value_weight_grad: float32 [768, 768], P('wsh')
- value_bias_grad: float32 [768], P('wsh')
- output_weight_grad: float32 [768, 768], P('wsh')
- output_bias_grad: float32 [768], P('wsh')
- first_gain_grad: float32 [768], P('wsh')
- first_shift_grad: float32 [768], P('wsh')
- inner_weight_grad: float32 [768, 3072], P('wsh')
- inner_bias_grad: float32 [3072], P('wsh')
- outer_weight_grad: float32 [3072, 768], P('wsh')
- outer_bias_grad: float32 [768], P('wsh')
- second_gain_grad: float32 [768], P('wsh')
- second_shift_grad: float32 [768], P('wsh')
- stream_rms: float32 [2], replicated
Inputs may be any that keep to these rules, and one draw needn't show every extreme that they name: `random_blocks`: of the 48 random blocks of one device's 16 query blocks, at most 8 lie in the 1024 tokens of any one index of ctx, and exactly 8 for some; none lies in the first or the last 1024 tokens of the sequence.
All inputs are finite; a program needn't handle non-finite values.
Results may differ from a plain program's by a relative error of at most 0.018.
Values may be sent and summed in bfloat16 or wider, within the bound.
A program may use at most 576 MiB of HBM per device.

v0:
```python
import math

import jax
import jax.numpy as jnp
from jax import lax
from jax.sharding import PartitionSpec as P

HD = 64
BLK = 64


EPSILON = 1e-06
NEG_FILL = -1e30


def padded(block, sides, width):
    for axis, dim in sides:
        count = lax.axis_size(axis)
        forward = [(i, i + 1) for i in range(count - 1)]
        backward = [(target, source) for source, target in forward]
        low = lax.ppermute(
            lax.slice_in_dim(block, block.shape[dim] - width, None, axis=dim), axis, forward
        )
        high = lax.ppermute(lax.slice_in_dim(block, 0, width, axis=dim), axis, backward)
        block = jnp.concatenate([low, block, high], axis=dim)
    return block


def layer_norm(hidden, gain, shift):
    center = hidden - jnp.mean(hidden, axis=-1, keepdims=True)
    inverse = lax.rsqrt(jnp.mean(center * center, axis=-1, keepdims=True) + EPSILON)
    normal = center * inverse
    return (normal * gain + shift, normal, inverse)


def norm_back(upstream, normal, inverse, gain):
    scaled = upstream * gain
    hidden_grad = inverse * (
        scaled
        - jnp.mean(scaled, axis=-1, keepdims=True)
        - normal * jnp.mean(scaled * normal, axis=-1, keepdims=True)
    )
    return (hidden_grad, jnp.sum(upstream * normal, axis=0), jnp.sum(upstream, axis=0))


def request_tables(random_rows, cycle_size, blocks_here):
    block_count = random_rows.shape[0]
    drawn = random_rows.reshape(cycle_size, 3 * blocks_here)
    global_pair = jnp.broadcast_to(jnp.array([0, block_count - 1], jnp.int32), (cycle_size, 2))
    wanted = jnp.concatenate([drawn, global_pair], axis=1)
    source = wanted // blocks_here
    within = wanted % blocks_here
    positions = jnp.arange(wanted.shape[1])
    earlier = positions[None, :] < positions[:, None]
    same_source = source[:, :, None] == source[:, None, :]
    ranking = jnp.sum(same_source & earlier[None], axis=2)
    return (source, within, ranking)


def send_slots(source, within, ranking, own_index, capacity):
    slot_ids = jnp.arange(capacity, dtype=jnp.int32)
    selected = (source[:, None, :] == own_index) & (ranking[:, None, :] == slot_ids[None, :, None])
    filled = jnp.any(selected, axis=2)
    picked = jnp.sum(jnp.where(selected, within[:, None, :], 0), axis=2)
    return (filled, picked)


def pack_blocks(paired, filled, picked, blocks_here, block_rows):
    features = paired.shape[-1]
    shaped = paired.reshape(2, blocks_here, block_rows, features)
    chosen = shaped[:, picked]
    return jnp.where(filled[None, :, :, None, None], chosen, jnp.zeros_like(chosen))


def assemble(extended, remote, blocks_here, block_rows):
    features = extended.shape[-1]
    padded_blocks = extended.reshape(2, blocks_here + 2, block_rows, features)
    window = jnp.stack(
        [
            padded_blocks[:, 0:blocks_here],
            padded_blocks[:, 1 : blocks_here + 1],
            padded_blocks[:, 2 : blocks_here + 2],
        ],
        axis=2,
    )
    global_part = jnp.broadcast_to(
        remote[:, None, 3 * blocks_here :], (2, blocks_here, 2, block_rows, features)
    )
    random_part = remote[:, : 3 * blocks_here].reshape(2, blocks_here, 3, block_rows, features)
    return jnp.concatenate([window, global_part, random_part], axis=2)


def masked_scores(query_heads, key_heads, usable, score_scale):
    scores = (
        jnp.einsum("gihd,gjthd->ghijt", query_heads, key_heads, preferred_element_type=jnp.float32)
        * score_scale
    )
    return jnp.where(usable[:, None, None, :, None], scores, NEG_FILL)


def gelu_slope(inner):
    cumulative = 0.5 * (1.0 + jax.scipy.special.erf(inner * (1.0 / math.sqrt(2.0))))
    density = jnp.exp(-0.5 * inner * inner) * (1.0 / math.sqrt(2.0 * math.pi))
    return cumulative + inner * density


def outer_product(left, right):
    return jnp.einsum("ta,tb->ab", left, right, preferred_element_type=jnp.float32)


def back_product(upstream, weight):
    return jnp.einsum("tb,ab->ta", upstream, weight, preferred_element_type=jnp.float32)


def column_sum(upstream):
    return jnp.sum(upstream.astype(jnp.float32), axis=0)


def shards(
    tokens,
    cotangent,
    random_blocks,
    query_weight,
    query_bias,
    key_weight,
    value_weight,
    value_bias,
    output_weight,
    output_bias,
    first_gain,
    first_shift,
    inner_weight,
    inner_bias,
    outer_weight,
    outer_bias,
    second_gain,
    second_shift,
):
    (
        full_query,
        full_query_bias,
        full_key,
        full_value,
        full_value_bias,
        full_output,
        full_output_bias,
        full_first_gain,
        full_first_shift,
        full_inner,
        full_inner_bias,
        full_outer,
        full_outer_bias,
        full_second_gain,
        full_second_shift,
    ) = (
        lax.all_gather(query_weight, "wsh", axis=0, tiled=True),
        lax.all_gather(query_bias, "wsh", axis=0, tiled=True),
        lax.all_gather(key_weight, "wsh", axis=0, tiled=True),
        lax.all_gather(value_weight, "wsh", axis=0, tiled=True),
        lax.all_gather(value_bias, "wsh", axis=0, tiled=True),
        lax.all_gather(output_weight, "wsh", axis=0, tiled=True),
        lax.all_gather(output_bias, "wsh", axis=0, tiled=True),
        lax.all_gather(first_gain, "wsh", axis=0, tiled=True),
        lax.all_gather(first_shift, "wsh", axis=0, tiled=True),
        lax.all_gather(inner_weight, "wsh", axis=0, tiled=True),
        lax.all_gather(inner_bias, "wsh", axis=0, tiled=True),
        lax.all_gather(outer_weight, "wsh", axis=0, tiled=True),
        lax.all_gather(outer_bias, "wsh", axis=0, tiled=True),
        lax.all_gather(second_gain, "wsh", axis=0, tiled=True),
        lax.all_gather(second_shift, "wsh", axis=0, tiled=True),
    )
    token_rows = tokens[0]
    length, features = token_rows.shape
    block_rows = BLK
    blocks_here = length // block_rows
    head_count = features // HD
    cycle_size = lax.axis_size("ctx")
    own_index = lax.axis_index("ctx")
    capacity = (3 * blocks_here + cycle_size - 3) // (cycle_size - 2)
    score_scale = HD ** (-0.5)
    first_gain_f = full_first_gain.astype(jnp.float32)
    second_gain_f = full_second_gain.astype(jnp.float32)
    queries_bf = (
        jnp.dot(token_rows, full_query, preferred_element_type=jnp.float32) + full_query_bias
    ).astype(jnp.bfloat16)
    keys_bf = jnp.dot(token_rows, full_key, preferred_element_type=jnp.float32).astype(jnp.bfloat16)
    values_bf = (
        jnp.dot(token_rows, full_value, preferred_element_type=jnp.float32) + full_value_bias
    ).astype(jnp.bfloat16)
    paired = jnp.stack([keys_bf, values_bf])
    extended = padded(paired, (("ctx", 1),), block_rows)
    source, within, ranking = request_tables(random_blocks[0], cycle_size, blocks_here)
    filled, picked = send_slots(source, within, ranking, own_index, capacity)
    own_source = lax.dynamic_index_in_dim(source, own_index, 0, keepdims=False)
    own_rank = lax.dynamic_index_in_dim(ranking, own_index, 0, keepdims=False)
    arrived = lax.all_to_all(
        pack_blocks(paired, filled, picked, blocks_here, block_rows),
        "ctx",
        split_axis=1,
        concat_axis=1,
        tiled=True,
    )
    listed = assemble(extended, arrived[:, own_source, own_rank], blocks_here, block_rows)
    block_index = own_index * blocks_here + jnp.arange(blocks_here)
    block_count = blocks_here * cycle_size
    always = jnp.ones((blocks_here,), bool)
    usable = jnp.stack(
        [
            block_index > 0,
            always,
            block_index < block_count - 1,
            always,
            always,
            always,
            always,
            always,
        ],
        axis=1,
    )
    query_heads = queries_bf.reshape(blocks_here, block_rows, head_count, HD)
    key_heads = listed[0].reshape(blocks_here, 8, block_rows, head_count, HD)
    value_heads = listed[1].reshape(blocks_here, 8, block_rows, head_count, HD)
    scores = masked_scores(query_heads, key_heads, usable, score_scale)
    row_top = jnp.max(scores, axis=(3, 4), keepdims=True)
    row_total = jnp.sum(jnp.exp(scores - row_top), axis=(3, 4), keepdims=True)
    log_total = row_top + jnp.log(row_total)
    probs_bf = jnp.exp(scores - log_total).astype(jnp.bfloat16)
    attended = jnp.einsum(
        "ghijt,gjthd->gihd", probs_bf, value_heads, preferred_element_type=jnp.float32
    ).reshape(length, features)
    mixed_bf = attended.astype(jnp.bfloat16)
    attention = (
        jnp.dot(mixed_bf, full_output, preferred_element_type=jnp.float32) + full_output_bias
    )
    stream = token_rows.astype(jnp.float32) + attention
    normed, first_normal, first_inverse = layer_norm(
        stream, first_gain_f, full_first_shift.astype(jnp.float32)
    )
    normed_bf = normed.astype(jnp.bfloat16)
    inner = jnp.dot(normed_bf, full_inner, preferred_element_type=jnp.float32) + full_inner_bias
    activated_bf = jax.nn.gelu(inner, approximate=False).astype(jnp.bfloat16)
    outer = jnp.dot(activated_bf, full_outer, preferred_element_type=jnp.float32) + full_outer_bias
    final, second_normal, second_inverse = layer_norm(
        normed + outer, second_gain_f, full_second_shift.astype(jnp.float32)
    )
    square_sums = lax.psum(
        (jnp.sum(stream * stream), jnp.sum(attention * attention)), ("ctx", "wsh")
    )
    element_count = cycle_size * lax.axis_size("wsh") * length * features
    stream_rms = jnp.sqrt(jnp.stack(square_sums) / element_count)
    output_grad = cotangent[0].astype(jnp.float32)
    second_stream_grad, second_gain_grad, second_shift_grad = norm_back(
        output_grad, second_normal, second_inverse, second_gain_f
    )
    outer_grad_bf = second_stream_grad.astype(jnp.bfloat16)
    outer_bias_grad = column_sum(outer_grad_bf)
    outer_weight_grad = outer_product(activated_bf, outer_grad_bf)
    inner_grad_bf = (back_product(outer_grad_bf, full_outer) * gelu_slope(inner)).astype(
        jnp.bfloat16
    )
    inner_bias_grad = column_sum(inner_grad_bf)
    inner_weight_grad = outer_product(normed_bf, inner_grad_bf)
    normed_grad = second_stream_grad + back_product(inner_grad_bf, full_inner)
    stream_grad, first_gain_grad, first_shift_grad = norm_back(
        normed_grad, first_normal, first_inverse, first_gain_f
    )
    attention_grad_bf = stream_grad.astype(jnp.bfloat16)
    output_bias_grad = column_sum(attention_grad_bf)
    output_weight_grad = outer_product(mixed_bf, attention_grad_bf)
    mixed_grad_bf = back_product(attention_grad_bf, full_output).astype(jnp.bfloat16)
    again = lax.all_to_all(
        pack_blocks(paired, filled, picked, blocks_here, block_rows),
        "ctx",
        split_axis=1,
        concat_axis=1,
        tiled=True,
    )
    relisted = assemble(extended, again[:, own_source, own_rank], blocks_here, block_rows)
    back_keys = relisted[0].reshape(blocks_here, 8, block_rows, head_count, HD)
    back_values = relisted[1].reshape(blocks_here, 8, block_rows, head_count, HD)
    rescored = masked_scores(query_heads, back_keys, usable, score_scale)
    probs = jnp.exp(rescored - log_total)
    probs_back_bf = probs.astype(jnp.bfloat16)
    mixed_heads = mixed_grad_bf.reshape(blocks_here, block_rows, head_count, HD)
    prob_grad = jnp.einsum(
        "gihd,gjthd->ghijt", mixed_heads, back_values, preferred_element_type=jnp.float32
    )
    row_delta = jnp.sum(probs * prob_grad, axis=(3, 4), keepdims=True)
    score_grad_bf = (probs * (prob_grad - row_delta)).astype(jnp.bfloat16)
    query_grad = (
        jnp.einsum(
            "ghijt,gjthd->gihd", score_grad_bf, back_keys, preferred_element_type=jnp.float32
        )
        * score_scale
    )
    query_grad_bf = query_grad.reshape(length, features).astype(jnp.bfloat16)
    listed_key_grad = (
        jnp.einsum(
            "ghijt,gihd->gjthd", score_grad_bf, query_heads, preferred_element_type=jnp.float32
        )
        * score_scale
    )
    listed_value_grad = jnp.einsum(
        "ghijt,gihd->gjthd", probs_back_bf, mixed_heads, preferred_element_type=jnp.float32
    )
    listed_grad = jnp.stack([listed_key_grad, listed_value_grad]).reshape(
        2, blocks_here, 8, block_rows, features
    )
    extended_grad = jnp.pad(listed_grad[:, :, 0], ((0, 0), (0, 2), (0, 0), (0, 0)))
    extended_grad = extended_grad + jnp.pad(listed_grad[:, :, 1], ((0, 0), (1, 1), (0, 0), (0, 0)))
    extended_grad = extended_grad + jnp.pad(listed_grad[:, :, 2], ((0, 0), (2, 0), (0, 0), (0, 0)))
    rim_pair = jnp.concatenate([extended_grad[:, 0], extended_grad[:, blocks_here + 1]], axis=1)
    rim_arrived = padded(rim_pair.astype(jnp.bfloat16), (("ctx", 1),), block_rows).astype(
        rim_pair.dtype
    )
    pair_grad = extended_grad[:, 1 : blocks_here + 1].reshape(2, length, features)
    pair_grad = pair_grad.at[:, :block_rows].add(rim_arrived[:, :block_rows])
    pair_grad = pair_grad.at[:, length - block_rows :].add(rim_arrived[:, 3 * block_rows :])
    random_grad = listed_grad[:, :, 5:8].reshape(2, 3 * blocks_here, block_rows, features)
    global_grad = jnp.sum(listed_grad[:, :, 3:5], axis=1)
    request_grad = jnp.concatenate([random_grad, global_grad], axis=1)
    outgoing_grad = (
        jnp.zeros((2, cycle_size, capacity, block_rows, features), jnp.float32)
        .at[:, own_source, own_rank]
        .set(request_grad)
    )
    incoming_grad = lax.all_to_all(
        outgoing_grad.astype(jnp.bfloat16), "ctx", split_axis=1, concat_axis=1, tiled=True
    ).astype(outgoing_grad.dtype)
    target = jnp.where(filled, picked, blocks_here).reshape(cycle_size * capacity)
    far_grad = (
        jnp.zeros((2, blocks_here, block_rows, features), jnp.float32)
        .at[:, target]
        .add(incoming_grad.reshape(2, cycle_size * capacity, block_rows, features), mode="drop")
    )
    pair_grad = pair_grad + far_grad.reshape(2, length, features)
    key_grad_bf = pair_grad[0].astype(jnp.bfloat16)
    value_grad_bf = pair_grad[1].astype(jnp.bfloat16)
    query_bias_grad = column_sum(query_grad_bf)
    value_bias_grad = column_sum(value_grad_bf)
    query_weight_grad = outer_product(token_rows, query_grad_bf)
    key_weight_grad = outer_product(token_rows, key_grad_bf)
    value_weight_grad = outer_product(token_rows, value_grad_bf)
    tokens_grad = (
        stream_grad
        + back_product(query_grad_bf, full_query)
        + back_product(key_grad_bf, full_key)
        + back_product(value_grad_bf, full_value)
    )
    parts = (
        lax.psum_scatter(
            query_weight_grad.astype(jnp.bfloat16), "wsh", scatter_dimension=0, tiled=True
        ).astype(jnp.float32),
        lax.psum_scatter(
            query_bias_grad.astype(jnp.bfloat16), "wsh", scatter_dimension=0, tiled=True
        ).astype(jnp.float32),
        lax.psum_scatter(
            key_weight_grad.astype(jnp.bfloat16), "wsh", scatter_dimension=0, tiled=True
        ).astype(jnp.float32),
        lax.psum_scatter(
            value_weight_grad.astype(jnp.bfloat16), "wsh", scatter_dimension=0, tiled=True
        ).astype(jnp.float32),
        lax.psum_scatter(
            value_bias_grad.astype(jnp.bfloat16), "wsh", scatter_dimension=0, tiled=True
        ).astype(jnp.float32),
        lax.psum_scatter(
            output_weight_grad.astype(jnp.bfloat16), "wsh", scatter_dimension=0, tiled=True
        ).astype(jnp.float32),
        lax.psum_scatter(
            output_bias_grad.astype(jnp.bfloat16), "wsh", scatter_dimension=0, tiled=True
        ).astype(jnp.float32),
        lax.psum_scatter(
            first_gain_grad.astype(jnp.bfloat16), "wsh", scatter_dimension=0, tiled=True
        ).astype(jnp.float32),
        lax.psum_scatter(
            first_shift_grad.astype(jnp.bfloat16), "wsh", scatter_dimension=0, tiled=True
        ).astype(jnp.float32),
        lax.psum_scatter(
            inner_weight_grad.astype(jnp.bfloat16), "wsh", scatter_dimension=0, tiled=True
        ).astype(jnp.float32),
        lax.psum_scatter(
            inner_bias_grad.astype(jnp.bfloat16), "wsh", scatter_dimension=0, tiled=True
        ).astype(jnp.float32),
        lax.psum_scatter(
            outer_weight_grad.astype(jnp.bfloat16), "wsh", scatter_dimension=0, tiled=True
        ).astype(jnp.float32),
        lax.psum_scatter(
            outer_bias_grad.astype(jnp.bfloat16), "wsh", scatter_dimension=0, tiled=True
        ).astype(jnp.float32),
        lax.psum_scatter(
            second_gain_grad.astype(jnp.bfloat16), "wsh", scatter_dimension=0, tiled=True
        ).astype(jnp.float32),
        lax.psum_scatter(
            second_shift_grad.astype(jnp.bfloat16), "wsh", scatter_dimension=0, tiled=True
        ).astype(jnp.float32),
    )
    reduced = lax.psum(
        (
            parts[0],
            parts[1],
            parts[2],
            parts[3],
            parts[4],
            parts[5],
            parts[6],
            parts[7],
            parts[8],
            parts[9],
            parts[10],
            parts[11],
            parts[12],
            parts[13],
            parts[14],
        ),
        "ctx",
    )
    return (
        final.astype(jnp.bfloat16)[None],
        tokens_grad.astype(jnp.bfloat16)[None],
        reduced[0],
        reduced[1],
        reduced[2],
        reduced[3],
        reduced[4],
        reduced[5],
        reduced[6],
        reduced[7],
        reduced[8],
        reduced[9],
        reduced[10],
        reduced[11],
        reduced[12],
        reduced[13],
        reduced[14],
        stream_rms,
    )


def solution(mesh):
    in_specs = (
        P("wsh", "ctx", None),
        P("wsh", "ctx", None),
        P("wsh", None, None),
        P("wsh", None),
        P("wsh"),
        P("wsh", None),
        P("wsh", None),
        P("wsh"),
        P("wsh", None),
        P("wsh"),
        P("wsh"),
        P("wsh"),
        P("wsh", None),
        P("wsh"),
        P("wsh", None),
        P("wsh"),
        P("wsh"),
        P("wsh"),
    )
    out_specs = (
        P("wsh", "ctx", None),
        P("wsh", "ctx", None),
        P("wsh", None),
        P("wsh"),
        P("wsh", None),
        P("wsh", None),
        P("wsh"),
        P("wsh", None),
        P("wsh"),
        P("wsh"),
        P("wsh"),
        P("wsh", None),
        P("wsh"),
        P("wsh", None),
        P("wsh"),
        P("wsh"),
        P("wsh"),
        P(),
    )
    return jax.shard_map(shards, mesh=mesh, in_specs=in_specs, out_specs=out_specs, check_vma=False)
```

profile of v0, /device:TPU:0, one launch (start us, length us, event | category | flops | bytes accessed | tf_op | source)
XLA Modules:
  0.0 1991.5 jit_solution(5699499822424285563)
XLA Ops:
  110.8 43.3 %collective-permute-done.1 = bf16[2,64,768]{2,1,0:T(8,128)(2,1)S(1)} collective-permute-done((bf16[2,64,768]{2,1,0:T(8,128)(2,1)}, bf16[2,64,768]{2,1,0:T(8,128)(2,1)S(1)}, u32[]{:S(2)}, u32[]{:S(2)}) %collective-permute-start.1) | collective-permute-done | bytes 196640 | tf_op jit(solution)/shard_map/ppermute | solution.py:24
  154.1 31.8 %collective-permute-done = bf16[2,64,768]{2,1,0:T(8,128)(2,1)S(1)} collective-permute-done((bf16[2,64,768]{2,1,0:T(8,128)(2,1)}, bf16[2,64,768]{2,1,0:T(8,128)(2,1)S(1)}, u32[]{:S(2)}, u32[]{:S(2)}) %collective-permute-start) | collective-permute-done | bytes 196640 | tf_op jit(solution)/shard_map/ppermute | solution.py:21
  194.0 158.2 %all-to-all-done = bf16[2,8,8,64,768]{4,3,2,0,1:T(8,128)(2,1)} async-done(((bf16[2,8,8,64,768]{4,3,2,0,1:T(8,128)(2,1)}), bf16[2,8,8,64,768]{4,3,2,0,1:T(8,128)(2,1)}, u32[]{:S(2)}, u32[]{:S(2)}) %all-to-all-start) | async-done | bytes 12582944 | tf_op jit(solution)/shard_map/all_to_all | solution.py:196
  414.5 38.3 %reshape_squeeze.4 = bf16[16,8,64,12,64]{4,3,2,1,0:T(8,128)(2,1)} reshape(bf16[1,16,8,64,768]{4,3,2,1,0:T(8,128)(2,1)} %get-tuple-element.226) | data formatting | bytes 25165824 | tf_op jit(solution)/shard_map/reshape;squeeze | solution.py:222
  472.6 38.3 %reshape_squeeze.10 = bf16[16,8,64,12,64]{4,3,2,1,0:T(8,128)(2,1)} reshape(bf16[1,16,8,64,768]{4,3,2,1,0:T(8,128)(2,1)} %get-tuple-element.225) | data formatting | bytes 25165824 | tf_op jit(solution)/shard_map/reshape;squeeze | solution.py:221
  510.9 19.9 copy.294
  530.8 25.9 %fusion = (f32[16,12,64]{2,1,0:T(8,128)S(1)}, f32[16,12,64,512]{2,3,1,0}) fusion(pred[16,8]{1,0:T(8,128)(4,1)S(1)} %stack.63, bf16[16,12,64,512]{2,3,1,0:T(8,128)(2,1)} %bitcast.239, bf16[16,64,12,64]{1,0,3,2:T(8,128)(2,1)S(1)} %reshape.555), kind=kOutput, calls=%fused_computation.10 | convolution fusion | flops 824168448 | bytes 39370880
  556.7 22.2 %exponential_reduce_fusion = f32[16,12,64]{2,1,0:T(8,128)S(1)} fusion(f32[16,12,64,512]{2,3,1,0} %get-tuple-element.235, f32[16,12,64]{2,1,0:T(8,128)S(1)} %get-tuple-element.234, pred[16,8]{1,0:T(8,128)(4,1)S(1)} %stack.63), kind=kLoop, calls=%fused_computation.8 | loop fusion | flops 25153536 | bytes 25264256 | tf_op jit(solution)/shard_map/reduce_sum | solution.py:225
  578.9 28.3 %fusion.26 = bf16[16,64,12,64]{1,3,2,0:T(8,128)(2,1)} fusion(bf16[16,8,64,12,64]{4,2,1,3,0:T(8,128)(2,1)} %copy.303, f32[16,12,64,512]{2,3,1,0} %get-tuple-element.235, f32[16,12,64]{2,1,0:T(8,128)S(1)} %log_add_fusion, pred[16,8]{1,0:T(8,128)(4,1)S(1)} %stack.63), kind=kOutput, calls=%fused_computation.65 | convolution fusion | flops 831258624 | bytes 39370880 | tf_op jit(solution)/shard_map/ghijt,gjthd->gihd/dot_general | solution.py:228
  620.1 38.4 %fusion.4 = (bf16[1024,3072]{1,0:T(8,128)(2,1)}, f32[1024,3072]{1,0:T(8,128)}) fusion(f32[3072]{0:T(1024)S(1)} %bitcast.259, bf16[768,3072]{1,0:T(8,128)(2,1)} %all-gather.16.cloned.1.call-done, f32[1024,768]{0,1:T(8,128)S(1)} %get-tuple-element.219, f32[768]{0:T(1024)S(1)} %copy-done.44, f32[768]{0:T(1024)S(1)} %copy-done.35, ...), kind=kOutput, calls=%fused_computation.20 | convolution fusion | flops 5043388416 | bytes 26765312 | tf_op jit(solution)/shard_map/dot_general | solution.py:240
  703.1 41.3 %multiply_reduce_fusion = (f32[16,12,64]{2,1,0:T(8,128)S(1)}, f32[16,12,64,512]{2,3,1,0}) fusion(f32[16,12,64,512]{2,3,1,0} %get-tuple-element.235, f32[16,12,64]{2,1,0:T(8,128)S(1)} %log_add_fusion, pred[16,8]{1,0:T(8,128)(4,1)S(1)} %stack.63, bf16[16,12,64,512]{2,3,1,0:T(8,128)(2,1)} %bitcast.240, bf16[16,64,12,64]{1,0,3,2:T(8,128)(2,1)S(1)} %reshape.556), kind=kOutput, calls=%fused_computation.6 | convolution fusion | flops 836751360 | bytes 64585856
  744.4 40.4 %multiply_convert_fusion = bf16[16,12,64,8,64]{2,4,3,1,0:T(8,128)(2,1)} fusion(f32[16,12,64,512]{2,3,1,0} %get-tuple-element.235, f32[16,12,64]{2,1,0:T(8,128)S(1)} %get-tuple-element.241, f32[16,12,64]{2,1,0:T(8,128)S(1)} %log_add_fusion, pred[16,8]{1,0:T(8,128)(4,1)S(1)} %stack.63, f32[16,12,64,512]{2,3,1,0} %get-tuple-element.242), kind=kLoop, calls=%fused_computation.5 | loop fusion | flops 37748736 | bytes 63012992 | tf_op jit(solution)/shard_map/convert_element_type | solution.py:289
  784.9 27.1 %multiply_bitcast_fusion = f32[16,8,64,12,64]{4,2,1,3,0:T(8,128)} fusion(bf16[16,12,64,8,64]{2,4,3,1,0:T(8,128)(2,1)} %multiply_convert_fusion, bf16[16,64,12,64,1]{1,0,3,2,4:T(8,128)(2,1)} %bitcast.251), kind=kOutput, calls=%fused_computation.4 | convolution fusion | flops 811597824 | bytes 39321600 | tf_op jit(solution)/shard_map/ghijt,gihd->gjthd/dot_general | solution.py:298
  812.0 51.7 %copy.311 = f32[16,8,64,12,64]{4,3,2,1,0:T(8,128)} copy(f32[16,8,64,12,64]{4,2,1,3,0:T(8,128)} %multiply_bitcast_fusion) | data formatting | bytes 50331648 | tf_op jit(solution)/shard_map/mul | solution.py:298
  863.6 49.9 %stack.64 = f32[1,16,8,64,768]{4,3,2,1,0:T(8,128)} reshape(f32[16,8,64,12,64]{4,3,2,1,0:T(8,128)} %copy.311) | data formatting | bytes 50331648 | tf_op jit(solution)/shard_map/stack | solution.py:306
  931.0 42.1 %convolution_bitcast_fusion = f32[16,8,64,12,64]{2,4,1,3,0:T(8,128)} fusion(bf16[16,64,12,64,1]{1,0,3,2,4:T(8,128)(2,1)S(1)} %bitcast.250, f32[16,12,64,512]{2,3,1,0} %get-tuple-element.235, f32[16,12,64]{2,1,0:T(8,128)S(1)} %log_add_fusion, pred[16,8]{1,0:T(8,128)(4,1)S(1)} %stack.63), kind=kOutput, calls=%fused_computation.17 | convolution fusion | flops 830472192 | bytes 51953792 | tf_op jit(solution)/shard_map/ghijt,gihd->gjthd/dot_general | solution.py:303
  973.1 59.5 %copy.314 = f32[16,8,64,12,64]{4,3,2,1,0:T(8,128)} copy(f32[16,8,64,12,64]{2,4,1,3,0:T(8,128)} %convolution_bitcast_fusion) | data formatting | bytes 50331648 | tf_op jit(solution)/shard_map/ghijt,gihd->gjthd/transpose | solution.py:303
  1032.7 50.1 %stack.65 = f32[1,16,8,64,768]{4,3,2,1,0:T(8,128)} reshape(f32[16,8,64,12,64]{4,3,2,1,0:T(8,128)} %copy.314) | data formatting | bytes 50331648 | tf_op jit(solution)/shard_map/stack | solution.py:306
  1132.5 40.9 %scatter_fusion = f32[2,8,8,64,768]{4,3,2,1,0:T(8,128)} fusion(f32[2,8,8,64,768]{4,3,2,1,0:T(8,128)} %broadcast_in_dim.58, s32[50]{0:T(128)S(1)} %copy-done.16, f32[50,2,64,768]{3,2,1,0:T(8,128)} %copy_bitcast_fusion), kind=kCustom, calls=%fused_computation.2 | custom fusion | bytes 58982800 | tf_op jit(solution)/shard_map/scatter | solution.py:325
  1284.8 25.4 %collective-permute-done.2 = bf16[2,64,768]{2,1,0:T(8,128)(2,1)S(1)} collective-permute-done((bf16[2,64,768]{2,1,0:T(8,128)(2,1)S(1)}, bf16[2,64,768]{2,1,0:T(8,128)(2,1)S(1)}, u32[]{:S(2)}, u32[]{:S(2)}) %collective-permute-start.2) | collective-permute-done | bytes 196640 | tf_op jit(solution)/shard_map/ppermute | solution.py:21
  1313.9 164.3 %all-to-all-done.1 = bf16[2,8,8,64,768]{4,3,2,0,1:T(8,128)(2,1)} async-done(((bf16[2,8,8,64,768]{4,3,2,0,1:T(8,128)(2,1)}), bf16[2,8,8,64,768]{4,3,2,0,1:T(8,128)(2,1)}, u32[]{:S(2)}, u32[]{:S(2)}) %all-to-all-start.1) | async-done | bytes 12582944 | tf_op jit(solution)/shard_map/all_to_all | solution.py:327
  1500.7 47.7 %scatter_fusion.1 = f32[2,16,64,768]{3,2,1,0:T(8,128)} fusion(f32[2,16,64,768]{3,2,1,0:T(8,128)} %broadcast_in_dim.57, s32[64]{0:T(128)S(1)} %fusion.91, f32[64,2,64,768]{3,2,1,0:T(8,128)} %copy.322), kind=kCustom, calls=%fused_computation.3 | custom fusion | flops 6291456 | bytes 75497728 | tf_op jit(solution)/shard_map/scatter-add | solution.py:334
  1564.4 57.4 %all-reduce.20 = (f32[1]{0:T(128)}, f32[1]{0:T(128)}) all-reduce(f32[1]{0:T(128)} %bitcast.59, f32[1]{0:T(128)} %bitcast.58), channel_id=1, replica_groups=mesh['ctx'=8,'wsh'=4] {'ctx','wsh'}, use_global_device_ids=true, to_apply=%region_59.60 | all-reduce | flops 2 | bytes 16 | tf_op jit(solution)/shard_map/psum | solution.py:246
  1678.1 300.9 %all-reduce.25 = (f32[192,768]{0,1:T(8,128)}, f32[192]{0:T(256)}, f32[192,768]{0,1:T(8,128)}, f32[192,768]{0,1:T(8,128)S(1)}, f32[192]{0:T(256)}, /*index=5*/f32...) all-reduce(bf16[192,768]{0,1:T(8,128)(2,1)S(1)} %copy.350, ...), channel_id=1, replica_groups=mesh['ctx'=8,'wsh'=4] {'ctx'}, use_global_device_ids=true, to_apply=%region_18.19 | all-reduce | flops 1771776 | bytes 10635264 | tf_op jit(solution)/shard_map/psum | solution.py:397
  (315 shorter events, 530.8 us)
Async XLA Ops:
  7.2 26.0 %all-gather.8.cloned.1.call-start = ((), (), s32[]{:S(2)}) async-start(), calls=%async_computation.8 | async-start | bytes 1474560 | tf_op jit(solution)/shard_map/all_gather | solution.py:158
  7.9 41.1 %all-gather.10.cloned.1.call-start = ((), (), s32[]{:S(2)}) async-start(), calls=%async_computation.9 | async-start | bytes 1474560 | tf_op jit(solution)/shard_map/all_gather | solution.py:159
  72.2 280.1 %all-to-all-start = ((bf16[2,8,8,64,768]{4,3,2,0,1:T(8,128)(2,1)}), bf16[2,8,8,64,768]{4,3,2,0,1:T(8,128)(2,1)}, u32[]{:S(2)}, u32[]{:S(2)}) async-start(bf16[2,8,8,64,768]{4,3,2,0,1:T(8,128)(2,1)} %copy.286), calls=%async_computation | async-start | bytes 25165824 | tf_op jit(solution)/shard_map/all_to_all | solution.py:196
  77.7 24.1 %all-gather.12.cloned.1.call-start = ((), (), s32[]{:S(2)}) async-start(), calls=%async_computation.10 | async-start | bytes 1474560 | tf_op jit(solution)/shard_map/all_gather | solution.py:156
  78.5 536.3 %all-gather.14.cloned.1.call-start = ((), (), s32[]{:S(2)}) async-start(), calls=%async_computation.11 | async-start | bytes 1474560 | tf_op jit(solution)/shard_map/all_gather | solution.py:161
  79.1 541.0 %all-gather.16.cloned.1.call-start = ((), (), s32[]{:S(2)}) async-start(), calls=%async_computation.12 | async-start | bytes 5898240 | tf_op jit(solution)/shard_map/all_gather | solution.py:165
  79.7 578.9 %all-gather.18.cloned.1.call-start = ((), (), s32[]{:S(2)}) async-start(), calls=%async_computation.13 | async-start | bytes 5898240 | tf_op jit(solution)/shard_map/all_gather | solution.py:167
  95.7 58.3 %collective-permute-start.1 = (bf16[2,64,768]{2,1,0:T(8,128)(2,1)}, bf16[2,64,768]{2,1,0:T(8,128)(2,1)S(1)}, u32[]{:S(2)}, u32[]{:S(2)}) collective-permute-start(bf16[2,64,768]{2,1,0:T(8,128)(2,1)} %get-tuple-element.231), channel_id=1, source_target_pairs={{4,0},{8,4},{12,8},{16,12},{20,16},{24,20},{28,24},{5,1},{9,5},{13... | collective-permute-start | bytes 589832 | tf_op jit(solution)/shard_map/ppermute | solution.py:24
  97.0 88.9 %collective-permute-start = (bf16[2,64,768]{2,1,0:T(8,128)(2,1)}, bf16[2,64,768]{2,1,0:T(8,128)(2,1)S(1)}, u32[]{:S(2)}, u32[]{:S(2)}) collective-permute-start(bf16[2,64,768]{2,1,0:T(8,128)(2,1)} %get-tuple-element.230), channel_id=1, source_target_pairs={{0,4},{4,8},{8,12},{12,16},{16,20},{20,24},{24,28},{1,5},{5,9},{9,... | collective-permute-start | bytes 589832 | tf_op jit(solution)/shard_map/ppermute | solution.py:21
  110.8 420.0 %copy-start.2 = (bf16[16,64,12,64]{1,0,3,2:T(8,128)(2,1)}, bf16[16,64,12,64]{1,0,3,2:T(8,128)(2,1)S(1)}, u32[]{:S(2)}) copy-start(bf16[16,64,12,64]{1,0,3,2:T(8,128)(2,1)S(1)} %reshape.555) | copy-start | bytes 4718596
  619.7 72.9 %copy-start.8 = (f32[1024,768]{0,1:T(8,128)}, f32[1024,768]{0,1:T(8,128)S(1)}, u32[]{:S(2)}) copy-start(f32[1024,768]{0,1:T(8,128)S(1)} %get-tuple-element.219) | copy-start | bytes 9437188
  1188.4 289.8 %all-to-all-start.1 = ((bf16[2,8,8,64,768]{4,3,2,0,1:T(8,128)(2,1)}), bf16[2,8,8,64,768]{4,3,2,0,1:T(8,128)(2,1)}, u32[]{:S(2)}, u32[]{:S(2)}) async-start(bf16[2,8,8,64,768]{4,3,2,0,1:T(8,128)(2,1)} %copy.320), calls=%async_computation.1 | async-start | bytes 25165824 | tf_op jit(solution)/shard_map/all_to_all | solution.py:327
  1202.6 421.8 %reduce-scatter.19.cloned.1.call-start = ((), (), s32[]{:S(2)}) async-start(), calls=%async_computation.17 | async-start | bytes 1474560
  1234.3 391.2 %reduce-scatter.13.cloned.1.call-start = ((), (), s32[]{:S(2)}) async-start(), calls=%async_computation.14 | async-start | bytes 1474560 | tf_op jit(solution)/shard_map/reduce_scatter | solution.py:366
  1239.3 386.2 %reduce-scatter.15.cloned.1.call-start = ((), (), s32[]{:S(2)}) async-start(), calls=%async_computation.15 | async-start | bytes 5898240 | tf_op jit(solution)/shard_map/reduce_scatter | solution.py:378
  1249.9 375.7 %reduce-scatter.17.cloned.1.call-start = ((), (), s32[]{:S(2)}) async-start(), calls=%async_computation.16 | async-start | bytes 5898240 | tf_op jit(solution)/shard_map/reduce_scatter | solution.py:384
  1261.0 406.3 %reduce-scatter.21.cloned.1.call-start = ((), (), s32[]{:S(2)}) async-start(), calls=%async_computation.18 | async-start | bytes 1474560
  1275.6 9.1 collective-permute-start.3
  1276.9 33.2 %collective-permute-start.2 = (bf16[2,64,768]{2,1,0:T(8,128)(2,1)S(1)}, bf16[2,64,768]{2,1,0:T(8,128)(2,1)S(1)}, u32[]{:S(2)}, u32[]{:S(2)}) collective-permute-start(bf16[2,64,768]{2,1,0:T(8,128)(2,1)S(1)} %get-tuple-element.227), channel_id=1, source_target_pairs={{0,4},{4,8},{8,12},{12,16},{16,20},{20,24},{24,28},{1,5},{5,9},{9,... | collective-permute-start | bytes 589832 | tf_op jit(solution)/shard_map/ppermute | solution.py:21
  1557.9 82.9 %copy-start.1 = (f32[1024,768]{0,1:T(8,128)S(1)}, f32[1024,768]{0,1:T(8,128)}, u32[]{:S(2)}) copy-start(f32[1024,768]{0,1:T(8,128)} %copy-done) | copy-start | bytes 9437188
  1558.0 82.9 %copy-start.26 = (f32[1024]{0:T(1024)S(1)}, f32[1024]{0:T(1024)}, u32[]{:S(2)}) copy-start(f32[1024]{0:T(1024)} %copy-done.25) | copy-start | bytes 12292
  1558.0 82.9 %copy-start.28 = (f32[768]{0:T(1024)S(1)}, f32[768]{0:T(1024)}, u32[]{:S(2)}) copy-start(f32[768]{0:T(1024)} %convert_element_type.238) | copy-start | bytes 9220
  1558.0 82.9 %copy-start.30 = (f32[1024]{0:T(1024)S(1)}, f32[1024]{0:T(1024)}, u32[]{:S(2)}) copy-start(f32[1024]{0:T(1024)} %copy-done.29) | copy-start | bytes 12292
  1560.5 116.4 %reduce-scatter.23.cloned.1.call-start = ((), (), s32[]{:S(2)}) async-start(), calls=%async_computation.19 | async-start | bytes 1474560
  (51 other events, 677.2 us)
Sparse Core Ops, SparseCore 0:
  9.6 20.3 all-gather.7
  31.5 17.4 all-gather.9
  80.1 17.9 all-gather.11
  99.5 17.4 all-gather.13
  118.4 37.4 all-gather.15
  157.3 37.4 all-gather.17
  1234.4 26.2 reduce-scatter.18
  1263.4 25.7 reduce-scatter.12
  1291.7 47.8 reduce-scatter.14
  1342.1 47.8 reduce-scatter.16
  1560.6 41.7 reduce-scatter.20
  1652.0 24.8 reduce-scatter.22
where the time goes:
time: 2010 us; the launch traced here: 1990 us
  local copies, waits for them, and re-layouts  613 us (30%)
  waiting for transfers between devices  447 us (22%)
  blocking collectives  389 us (19%)
  matrix products  308 us (15%)
  other arithmetic  185 us (9%)
  starting transfers between devices  32.1 us (2%)
    psum x1, blocking collectives, shards(): lax.psum((parts[0], parts[1], parts[2], parts[3], parts[4], parts[5], par...  301 us
    all_to_all x1, waiting for transfers between devices, shards(): lax.all_to_all(outgoing_grad.astype(jnp.bfloat16), 'ctx', split_axis=1, c...  164 us
    all_to_all x1, waiting for transfers between devices, shards(): lax.all_to_all(pack_blocks(paired, filled, picked, blocks_here, block_row...  158 us
    another operation x3, local copies, waits for them, and re-layouts, shards(): jnp.stack([listed_key_grad, listed_value_grad])  117 us
    unnamed x151, local copies, waits for them, and re-layouts  70.3 us
    unnamed x2, matrix products  67.2 us
    transpose x1, local copies, waits for them, and re-layouts, shards(): jnp.einsum('ghijt,gihd->gjthd', probs_back_bf, mixed_heads, preferred_ele...  59.5 us
    another operation x2, local copies, waits for them, and re-layouts, shards(): key_heads = listed[0].reshape(blocks_here, 8, block_rows, head_count, HD)  58.1 us
  transfers between devices with their start and end apart: 18, of which 7 were waited for; matrix products, arithmetic and copies ran while one was open for 27% of the time, Pallas kernels for 0%

commit v1 on v0

v1 whole, which is shorter than its diff:
```python
import functools
import math

import jax
import jax.numpy as jnp
from jax import lax
from jax.experimental import pallas as pl
from jax.experimental.pallas import tpu as pltpu
from jax.sharding import PartitionSpec as P

HD = 64
BLK = 64
PACKED = 4
LANES = PACKED * HD
LISTED = 8
EXTRA = 4

EPSILON = 1e-06
NEG_FILL = -1e30
MESH = pl.DeviceIdType.MESH
MIB = 1 << 20


def request_tables(random_rows, cycle_size, blocks_here):
    wanted = random_rows.reshape(cycle_size, 3 * blocks_here)
    source = wanted // blocks_here
    within = wanted % blocks_here
    positions = jnp.arange(wanted.shape[1])
    earlier = positions[None, :] < positions[:, None]
    same_source = source[:, :, None] == source[:, None, :]
    ranking = jnp.sum(same_source & earlier[None], axis=2, dtype=jnp.int32)
    return (source, within, ranking)


def send_slots(source, within, ranking, own_index, capacity):
    slot_ids = jnp.arange(capacity, dtype=jnp.int32)
    selected = (source[:, None, :] == own_index) & (ranking[:, None, :] == slot_ids[None, :, None])
    filled = jnp.any(selected, axis=2)
    picked = jnp.sum(jnp.where(selected, within[:, None, :], 0), axis=2, dtype=jnp.int32)
    return (filled.astype(jnp.int32), picked)


def key_slots(own_source, own_rank, blocks_here, capacity):
    block = jnp.arange(blocks_here, dtype=jnp.int32)
    left = jnp.where(block == 0, blocks_here, block - 1)
    right = jnp.where(block == blocks_here - 1, blocks_here + 1, block + 1)
    drawn = (blocks_here + EXTRA + (own_source - 1) * capacity + own_rank).reshape(blocks_here, 3)
    fixed = jnp.stack(
        [
            left,
            block,
            right,
            jnp.full_like(block, blocks_here + 2),
            jnp.full_like(block, blocks_here + 3),
        ],
        axis=1,
    )
    return jnp.concatenate([fixed, drawn], axis=1).astype(jnp.int32)


def pack_kernel(picked_ref, rows_ref, out_ref, sems):
    slots = out_ref.shape[0]

    def copy(i):
        return pltpu.make_async_copy(rows_ref.at[picked_ref[i]], out_ref.at[i], sems.at[i])

    @pl.loop(0, slots)
    def _(i):
        copy(i).start()

    @pl.loop(0, slots)
    def _(i):
        copy(i).wait()


def pack_blocks(rows, picked):
    slots = picked.shape[0]
    return pl.pallas_call(
        pack_kernel,
        out_shape=jax.ShapeDtypeStruct((slots,) + rows.shape[1:], rows.dtype),
        grid_spec=pltpu.PrefetchScalarGridSpec(
            num_scalar_prefetch=1,
            grid=(1,),
            in_specs=[pl.BlockSpec(rows.shape, lambda i, t: (0, 0, 0))],
            out_specs=pl.BlockSpec(memory_space=pl.ANY),
            scratch_shapes=[pltpu.SemaphoreType.DMA((slots,))],
        ),
        name="pack_blocks",
    )(picked, rows)


def spread_kernel(count, capacity, *refs):
    weights = (len(refs) - 2 - 1 - 9) // 2
    pack, rows = refs[:2]
    shards = refs[2 : 2 + weights]
    ext = refs[2 + weights]
    fulls = refs[3 + weights : 3 + 2 * weights]
    rand_s, rand_r, halo_s, halo_r, glob_s, glob_r, wgt_s, wgt_r, loc = refs[3 + 2 * weights :]
    blocks = rows.shape[0]
    base = blocks + EXTRA
    me = lax.axis_index("ctx")
    w = lax.axis_index("wsh")
    sib = w + 1 - 2 * (w % 2)
    far = (w + 2) % 4
    far_sib = (sib + 2) % 4
    last = count - 1
    is_source = jnp.logical_and(me >= 1, me <= last - 1)

    barrier = pltpu.get_barrier_semaphore()

    @pl.loop(1, count)
    def _(delta):
        pl.semaphore_signal(
            barrier, inc=1, device_id={"ctx": (me + delta) % count}, device_id_type=MESH
        )

    pl.semaphore_signal(barrier, inc=1, device_id={"wsh": sib}, device_id_type=MESH)
    pl.semaphore_signal(barrier, inc=1, device_id={"wsh": far}, device_id_type=MESH)
    pl.semaphore_wait(barrier, count + 1)

    def weight_copy(i, step):
        if step == 2:
            src, dst, target = fulls[i].at[far], fulls[i].at[far], sib
        else:
            src, dst, target = shards[i], fulls[i].at[w], (far, sib)[step]
        return pltpu.make_async_remote_copy(
            src_ref=src,
            dst_ref=dst,
            send_sem=wgt_s.at[i, step],
            recv_sem=wgt_r.at[i, step],
            device_id={"wsh": target},
            device_id_type=MESH,
        )

    def random_copy(dst):
        return pltpu.make_async_remote_copy(
            src_ref=pack.at[dst],
            dst_ref=ext.at[pl.ds(base + (me - 1) * capacity, capacity)],
            send_sem=rand_s.at[dst],
            recv_sem=rand_r.at[me],
            device_id={"ctx": dst},
            device_id_type=MESH,
        )

    def random_landed(source):
        return pltpu.make_async_remote_copy(
            src_ref=pack.at[source],
            dst_ref=ext.at[pl.ds(base + (source - 1) * capacity, capacity)],
            send_sem=rand_s.at[source],
            recv_sem=rand_r.at[source],
            device_id={"ctx": source},
            device_id_type=MESH,
        )

    def halo_copy(side):
        return pltpu.make_async_remote_copy(
            src_ref=rows.at[blocks - 1 if side == 0 else 0],
            dst_ref=ext.at[blocks + side],
            send_sem=halo_s.at[side],
            recv_sem=halo_r.at[side],
            device_id={"ctx": me + 1 if side == 0 else me - 1},
            device_id_type=MESH,
        )

    def global_copy(which, dst):
        return pltpu.make_async_remote_copy(
            src_ref=rows.at[0 if which == 0 else blocks - 1],
            dst_ref=ext.at[blocks + 2 + which],
            send_sem=glob_s.at[dst],
            recv_sem=glob_r.at[which],
            device_id={"ctx": dst},
            device_id_type=MESH,
        )

    for i in range(weights):
        weight_copy(i, 0).start()

    @pl.when(me < last)
    def _():
        halo_copy(0).start()

    @pl.when(me > 0)
    def _():
        halo_copy(1).start()

    @pl.when(is_source)
    def _():
        @pl.loop(1, count)
        def _(delta):
            random_copy((me + delta) % count).start()

    for which, owner in ((0, 0), (1, last)):

        @pl.when(me == owner)
        def _():
            @pl.loop(1, count)
            def _(delta):
                global_copy(which, (me + delta) % count).start()

    for i in range(weights):
        weight_copy(i, 1).start()

    def own_rows():
        return pltpu.make_async_copy(rows, ext.at[pl.ds(0, blocks)], loc.at[0])

    def own_weight(i):
        return pltpu.make_async_copy(shards[i], fulls[i].at[w], loc.at[5 + i])

    def own_random():
        return pltpu.make_async_copy(
            pack.at[me], ext.at[pl.ds(base + (me - 1) * capacity, capacity)], loc.at[1]
        )

    def own_rim(side):
        return pltpu.make_async_copy(rows.at[0], ext.at[blocks + side], loc.at[2])

    def own_global(which):
        return pltpu.make_async_copy(
            rows.at[0 if which == 0 else blocks - 1], ext.at[blocks + 2 + which], loc.at[3]
        )

    own_rows().start()
    for i in range(weights):
        own_weight(i).start()

    @pl.when(is_source)
    def _():
        own_random().start()

    for which, owner in ((0, 0), (1, last)):

        @pl.when(me == owner)
        def _():
            own_rim(which).start()
            own_global(which).start()

    for i in range(weights):
        weight_copy(i, 0).wait_recv()
        weight_copy(i, 2).start()

    own_rows().wait()
    for i in range(weights):
        own_weight(i).wait()

    @pl.when(is_source)
    def _():
        own_random().wait()

        @pl.loop(1, count)
        def _(delta):
            random_copy((me + delta) % count).wait_send()

    for which, owner in ((0, 0), (1, last)):

        @pl.when(me == owner)
        def _():
            own_rim(which).wait()
            own_global(which).wait()

            @pl.loop(1, count)
            def _(delta):
                global_copy(which, (me + delta) % count).wait_send()

        @pl.when(me != owner)
        def _():
            global_copy(which, owner).wait_recv()

    @pl.when(me < last)
    def _():
        halo_copy(0).wait_send()
        halo_copy(1).wait_recv()

    @pl.when(me > 0)
    def _():
        halo_copy(1).wait_send()
        halo_copy(0).wait_recv()

    @pl.loop(1, last)
    def _(source):
        @pl.when(source != me)
        def _():
            random_landed(source).wait_recv()

    for i in range(weights):
        for step in range(3):
            weight_copy(i, step).wait_send()
        weight_copy(i, 1).wait_recv()
        weight_copy(i, 2).wait_recv()


def spread(pack, rows, shards, count, capacity):
    blocks = rows.shape[0]
    weights = len(shards)
    slots = blocks + EXTRA + (count - 2) * capacity
    outs = pl.pallas_call(
        functools.partial(spread_kernel, count, capacity),
        out_shape=[jax.ShapeDtypeStruct((slots,) + rows.shape[1:], rows.dtype)]
        + [jax.ShapeDtypeStruct((4,) + shard.shape, shard.dtype) for shard in shards],
        in_specs=[pl.BlockSpec(memory_space=pl.ANY)] * (2 + weights),
        out_specs=[pl.BlockSpec(memory_space=pl.ANY)] * (1 + weights),
        scratch_shapes=[
            pltpu.SemaphoreType.DMA((count,)),
            pltpu.SemaphoreType.DMA((count,)),
            pltpu.SemaphoreType.DMA((2,)),
            pltpu.SemaphoreType.DMA((2,)),
            pltpu.SemaphoreType.DMA((count,)),
            pltpu.SemaphoreType.DMA((2,)),
            pltpu.SemaphoreType.DMA((weights, 3)),
            pltpu.SemaphoreType.DMA((weights, 3)),
            pltpu.SemaphoreType.DMA((5 + weights,)),
        ],
        compiler_params=pltpu.CompilerParams(collective_id=0, has_side_effects=True),
        name="spread_rows",
    )(pack, rows, *shards)
    return outs[0], outs[1:]


def return_kernel(
    count, capacity, far_grad, back, rim, glob, rand_s, rand_r, halo_s, halo_r, glob_s, glob_r, loc
):
    me = lax.axis_index("ctx")
    last = count - 1
    is_source = jnp.logical_and(me >= 1, me <= last - 1)
    barrier = pltpu.get_barrier_semaphore()

    @pl.loop(1, count)
    def _(delta):
        pl.semaphore_signal(
            barrier, inc=1, device_id={"ctx": (me + delta) % count}, device_id_type=MESH
        )

    pl.semaphore_wait(barrier, count - 1)

    def random_copy(owner, sender):
        return pltpu.make_async_remote_copy(
            src_ref=far_grad.at[pl.ds(EXTRA + (owner - 1) * capacity, capacity)],
            dst_ref=back.at[sender],
            send_sem=rand_s.at[owner],
            recv_sem=rand_r.at[sender],
            device_id={"ctx": owner},
            device_id_type=MESH,
        )

    def landed(sender):
        return pltpu.make_async_remote_copy(
            src_ref=far_grad.at[pl.ds(EXTRA, capacity)],
            dst_ref=back.at[sender],
            send_sem=rand_s.at[sender],
            recv_sem=rand_r.at[sender],
            device_id={"ctx": sender},
            device_id_type=MESH,
        )

    def halo_copy(side):
        return pltpu.make_async_remote_copy(
            src_ref=far_grad.at[side],
            dst_ref=rim.at[1 - side],
            send_sem=halo_s.at[side],
            recv_sem=halo_r.at[side],
            device_id={"ctx": me - 1 if side == 0 else me + 1},
            device_id_type=MESH,
        )

    def global_copy(which, sender):
        return pltpu.make_async_remote_copy(
            src_ref=far_grad.at[2 + which],
            dst_ref=glob.at[sender],
            send_sem=glob_s.at[which],
            recv_sem=glob_r.at[sender],
            device_id={"ctx": 0 if which == 0 else last},
            device_id_type=MESH,
        )

    @pl.when(me > 0)
    def _():
        halo_copy(0).start()
        global_copy(0, me).start()

    @pl.when(me < last)
    def _():
        halo_copy(1).start()
        global_copy(1, me).start()

    @pl.loop(1, count)
    def _(delta):
        owner = (me + delta) % count

        @pl.when(jnp.logical_and(owner >= 1, owner <= last - 1))
        def _():
            random_copy(owner, me).start()

    def own_random():
        return pltpu.make_async_copy(
            far_grad.at[pl.ds(EXTRA + (me - 1) * capacity, capacity)], back.at[me], loc.at[0]
        )

    def own_global(which):
        return pltpu.make_async_copy(far_grad.at[2 + which], glob.at[me], loc.at[1])

    @pl.when(is_source)
    def _():
        own_random().start()
        own_random().wait()

        @pl.loop(0, count)
        def _(sender):
            @pl.when(sender != me)
            def _():
                landed(sender).wait_recv()

    for which, owner in ((0, 0), (1, last)):

        @pl.when(me == owner)
        def _():
            own_global(which).start()
            own_global(which).wait()

            @pl.loop(0, count)
            def _(sender):
                @pl.when(sender != me)
                def _():
                    global_copy(which, sender).wait_recv()

    @pl.when(me > 0)
    def _():
        halo_copy(0).wait_send()
        halo_copy(1).wait_recv()
        global_copy(0, me).wait_send()

    @pl.when(me < last)
    def _():
        halo_copy(1).wait_send()
        halo_copy(0).wait_recv()
        global_copy(1, me).wait_send()

    @pl.loop(1, count)
    def _(delta):
        owner = (me + delta) % count

        @pl.when(jnp.logical_and(owner >= 1, owner <= last - 1))
        def _():
            random_copy(owner, me).wait_send()


def return_grads(far_grad, count, capacity):
    tail = far_grad.shape[1:]
    kind = far_grad.dtype
    return pl.pallas_call(
        functools.partial(return_kernel, count, capacity),
        out_shape=[
            jax.ShapeDtypeStruct((count, capacity) + tail, kind),
            jax.ShapeDtypeStruct((2,) + tail, kind),
            jax.ShapeDtypeStruct((count,) + tail, kind),
        ],
        in_specs=[pl.BlockSpec(memory_space=pl.ANY)],
        out_specs=[pl.BlockSpec(memory_space=pl.ANY)] * 3,
        scratch_shapes=[
            pltpu.SemaphoreType.DMA((count,)),
            pltpu.SemaphoreType.DMA((count,)),
            pltpu.SemaphoreType.DMA((2,)),
            pltpu.SemaphoreType.DMA((2,)),
            pltpu.SemaphoreType.DMA((2,)),
            pltpu.SemaphoreType.DMA((count,)),
            pltpu.SemaphoreType.DMA((2,)),
        ],
        compiler_params=pltpu.CompilerParams(collective_id=1, has_side_effects=True),
        name="return_grads",
    )(far_grad)


def unpack_kernel(
    capacity, picked_ref, filled_ref, edge_ref, base_ref, back_ref, rim_ref, glob_ref, out_ref, acc
):
    step = pl.program_id(0)
    blocks = base_ref.shape[0]

    @pl.when(step == 0)
    def _():
        acc[...] = base_ref[...]

        @pl.when(edge_ref[0] == 0)
        def _():
            acc[0] += rim_ref[0].astype(jnp.float32)

        @pl.when(edge_ref[1] == 0)
        def _():
            acc[blocks - 1] += rim_ref[1].astype(jnp.float32)

    for k in range(capacity):
        slot = step * capacity + k

        @pl.when(filled_ref[slot] == 1)
        def _():
            acc[picked_ref[slot]] += back_ref[0, k].astype(jnp.float32)

    for which, block in ((0, 0), (1, blocks - 1)):

        @pl.when(edge_ref[which] == 1)
        def _():
            acc[block] += glob_ref[0].astype(jnp.float32)

    @pl.when(step == pl.num_programs(0) - 1)
    def _():
        out_ref[...] = acc[...].astype(out_ref.dtype)


def unpack_grads(base, back, rim, glob, picked, filled, edge):
    count, capacity = back.shape[:2]
    blocks, block_rows, features = base.shape
    return pl.pallas_call(
        functools.partial(unpack_kernel, capacity),
        out_shape=jax.ShapeDtypeStruct(base.shape, jnp.bfloat16),
        grid_spec=pltpu.PrefetchScalarGridSpec(
            num_scalar_prefetch=3,
            grid=(count,),
            in_specs=[
                pl.BlockSpec(base.shape, lambda i, *t: (0, 0, 0)),
                pl.BlockSpec((1,) + back.shape[1:], lambda i, *t: (i, 0, 0, 0)),
                pl.BlockSpec(rim.shape, lambda i, *t: (0, 0, 0)),
                pl.BlockSpec((1, block_rows, features), lambda i, *t: (i, 0, 0)),
            ],
            out_specs=pl.BlockSpec(base.shape, lambda i, *t: (0, 0, 0)),
            scratch_shapes=[pltpu.VMEM(base.shape, jnp.float32)],
        ),
        compiler_params=pltpu.CompilerParams(vmem_limit_bytes=32 * MIB),
        name="unpack_grads",
    )(picked, filled, edge, base, back, rim, glob)


def head_mask():
    rows = lax.broadcasted_iota(jnp.int32, (LANES, LANES), 0) // HD
    columns = lax.broadcasted_iota(jnp.int32, (LANES, LANES), 1) // HD
    return rows == columns


def spread_heads(block, mask):
    tiled = jnp.concatenate([block] * PACKED, axis=0)
    return jnp.where(mask, tiled, jnp.zeros_like(tiled))


def fold_heads(square, mask):
    kept = jnp.where(mask, square, 0.0)
    total = kept[:BLK]
    for i in range(1, PACKED):
        total = total + kept[i * BLK : (i + 1) * BLK]
    return total


def listed_rows(ref, index_ref, b):
    return jnp.concatenate([ref[index_ref[b * LISTED + j]] for j in range(LISTED)], axis=0)


def nt(left, right):
    return lax.dot_general(
        left, right, (((1,), (1,)), ((), ())), preferred_element_type=jnp.float32
    )


def nn(left, right):
    return jnp.dot(left, right, preferred_element_type=jnp.float32)


def tn(left, right):
    return lax.dot_general(
        left, right, (((0,), (0,)), ((), ())), preferred_element_type=jnp.float32
    )


def mask_edges(scores, edge_ref, b, blocks):
    low = jnp.logical_and(b == 0, edge_ref[0] == 1)
    high = jnp.logical_and(b == blocks - 1, edge_ref[1] == 1)
    first = jnp.where(low, NEG_FILL, scores[:BLK])
    third = jnp.where(high, NEG_FILL, scores[2 * BLK : 3 * BLK])
    return jnp.concatenate([first, scores[BLK : 2 * BLK], third, scores[3 * BLK :]], axis=0)


def forward_kernel(index_ref, edge_ref, q_ref, k_ref, v_ref, o_ref, log_ref):
    blocks = q_ref.shape[0]
    mask = head_mask()

    @pl.loop(0, blocks)
    def _(b):
        query = spread_heads(q_ref[b] * HD**-0.5, mask)
        scores = mask_edges(nt(listed_rows(k_ref, index_ref, b), query), edge_ref, b, blocks)
        top = jnp.max(scores, axis=0, keepdims=True)
        raised = jnp.exp(scores - top)
        total = jnp.sum(raised, axis=0, keepdims=True)
        probs = (raised * (1.0 / total)).astype(jnp.bfloat16)
        log_ref[b] = top + jnp.log(total)
        mixed = tn(probs, listed_rows(v_ref, index_ref, b))
        o_ref[b] = fold_heads(mixed, mask).astype(o_ref.dtype)


def attend(queries, keys, values, index, edge):
    blocks, block_rows, features = queries.shape
    slots = keys.shape[0]
    groups = features // LANES
    column = lambda g, *t: (0, 0, g)
    return pl.pallas_call(
        forward_kernel,
        out_shape=[
            jax.ShapeDtypeStruct(queries.shape, jnp.bfloat16),
            jax.ShapeDtypeStruct((blocks, 1, features), jnp.float32),
        ],
        grid_spec=pltpu.PrefetchScalarGridSpec(
            num_scalar_prefetch=2,
            grid=(groups,),
            in_specs=[
                pl.BlockSpec((blocks, block_rows, LANES), column),
                pl.BlockSpec((slots, block_rows, LANES), column),
                pl.BlockSpec((slots, block_rows, LANES), column),
            ],
            out_specs=[
                pl.BlockSpec((blocks, block_rows, LANES), column),
                pl.BlockSpec((blocks, 1, LANES), column),
            ],
        ),
        compiler_params=pltpu.CompilerParams(vmem_limit_bytes=40 * MIB),
        name="attend",
    )(index, edge, queries, keys, values)


def backward_kernel(
    index_ref,
    edge_ref,
    q_ref,
    g_ref,
    k_ref,
    v_ref,
    log_ref,
    dq_ref,
    dk_ref,
    dv_ref,
    key_sum,
    value_sum,
):
    blocks = q_ref.shape[0]
    near = blocks + EXTRA
    mask = head_mask()
    key_sum[...] = jnp.zeros_like(key_sum)
    value_sum[...] = jnp.zeros_like(value_sum)
    dk_ref[...] = jnp.zeros_like(dk_ref)
    dv_ref[...] = jnp.zeros_like(dv_ref)

    @pl.loop(0, blocks)
    def _(b):
        query = spread_heads(q_ref[b] * HD**-0.5, mask)
        upstream = spread_heads(g_ref[b], mask)
        key_rows = listed_rows(k_ref, index_ref, b)
        scores = mask_edges(nt(key_rows, query), edge_ref, b, blocks)
        probs = jnp.exp(scores - log_ref[b])
        prob_grad = nt(listed_rows(v_ref, index_ref, b), upstream)
        delta = jnp.sum(probs * prob_grad, axis=0, keepdims=True)
        score_grad = (probs * (prob_grad - delta)).astype(jnp.bfloat16)
        value_grad = nn(probs.astype(jnp.bfloat16), upstream)
        key_grad = nn(score_grad, query)
        query_grad = fold_heads(tn(score_grad, key_rows), mask) * HD**-0.5
        dq_ref[b] = query_grad.astype(dq_ref.dtype)
        for j in range(LISTED):
            slot = index_ref[b * LISTED + j]
            piece = slice(j * BLK, (j + 1) * BLK)
            if j < 5:
                key_sum[slot] += key_grad[piece]
                value_sum[slot] += value_grad[piece]
            else:
                dk_ref[slot] = key_grad[piece].astype(dk_ref.dtype)
                dv_ref[slot] = value_grad[piece].astype(dv_ref.dtype)

    dk_ref[:near] = key_sum[...].astype(dk_ref.dtype)
    dv_ref[:near] = value_sum[...].astype(dv_ref.dtype)


def attend_back(queries, upstream, keys, values, log_total, index, edge):
    blocks, block_rows, features = queries.shape
    slots = keys.shape[0]
    groups = features // LANES
    column = lambda g, *t: (0, 0, g)
    few = pl.BlockSpec((blocks, block_rows, LANES), column)
    many = pl.BlockSpec((slots, block_rows, LANES), column)
    return pl.pallas_call(
        backward_kernel,
        out_shape=[
            jax.ShapeDtypeStruct(queries.shape, jnp.bfloat16),
            jax.ShapeDtypeStruct(keys.shape, jnp.bfloat16),
            jax.ShapeDtypeStruct(keys.shape, jnp.bfloat16),
        ],
        grid_spec=pltpu.PrefetchScalarGridSpec(
            num_scalar_prefetch=2,
            grid=(groups,),
            in_specs=[few, few, many, many, pl.BlockSpec((blocks, 1, LANES), column)],
            out_specs=[few, many, many],
            scratch_shapes=[
                pltpu.VMEM((blocks + EXTRA, block_rows, LANES), jnp.float32),
                pltpu.VMEM((blocks + EXTRA, block_rows, LANES), jnp.float32),
            ],
        ),
        compiler_params=pltpu.CompilerParams(vmem_limit_bytes=48 * MIB),
        name="attend_back",
    )(index, edge, queries, upstream, keys, values, log_total)


def layer_norm(hidden, gain, shift):
    center = hidden - jnp.mean(hidden, axis=-1, keepdims=True)
    inverse = lax.rsqrt(jnp.mean(center * center, axis=-1, keepdims=True) + EPSILON)
    normal = center * inverse
    return (normal * gain + shift, normal, inverse)


def norm_back(upstream, normal, inverse, gain):
    scaled = upstream * gain
    hidden_grad = inverse * (
        scaled
        - jnp.mean(scaled, axis=-1, keepdims=True)
        - normal * jnp.mean(scaled * normal, axis=-1, keepdims=True)
    )
    return (hidden_grad, jnp.sum(upstream * normal, axis=0), jnp.sum(upstream, axis=0))


def gelu_slope(inner):
    cumulative = 0.5 * (1.0 + jax.scipy.special.erf(inner * (1.0 / math.sqrt(2.0))))
    density = jnp.exp(-0.5 * inner * inner) * (1.0 / math.sqrt(2.0 * math.pi))
    return cumulative + inner * density


def outer_product(left, right):
    return jnp.einsum("ta,tb->ab", left, right, preferred_element_type=jnp.float32)


def back_product(upstream, weight):
    return jnp.einsum("tb,ab->ta", upstream, weight, preferred_element_type=jnp.float32)


def column_sum(upstream):
    return jnp.sum(upstream.astype(jnp.float32), axis=0)


def shards(
    tokens,
    cotangent,
    random_blocks,
    query_weight,
    query_bias,
    key_weight,
    value_weight,
    value_bias,
    output_weight,
    output_bias,
    first_gain,
    first_shift,
    inner_weight,
    inner_bias,
    outer_weight,
    outer_bias,
    second_gain,
    second_shift,
):
    token_rows = tokens[0]
    length, features = token_rows.shape
    blocks_here = length // BLK
    count = lax.axis_size("ctx")
    groups = lax.axis_size("wsh")
    own_index = lax.axis_index("ctx")
    own_group = lax.axis_index("wsh")
    capacity = (3 * blocks_here + count - 3) // (count - 2)
    part = features // groups
    inner_parts = inner_bias.shape[0] // part

    small = jnp.concatenate(
        [
            vector.reshape(-1, part)
            for vector in (
                query_bias,
                value_bias,
                output_bias,
                first_gain,
                first_shift,
                outer_bias,
                second_gain,
                second_shift,
                inner_bias,
            )
        ],
        axis=0,
    )
    small = jnp.pad(small, ((0, (-small.shape[0]) % 16), (0, (-part) % 128)))

    source, within, ranking = request_tables(random_blocks[0], count, blocks_here)
    filled, picked = send_slots(source, within, ranking, own_index, capacity)
    filled, picked = filled.reshape(-1), picked.reshape(-1)
    own_source = lax.dynamic_index_in_dim(source, own_index, 0, keepdims=False)
    own_rank = lax.dynamic_index_in_dim(ranking, own_index, 0, keepdims=False)
    index = key_slots(own_source, own_rank, blocks_here, capacity).reshape(-1)
    edge = jnp.stack([own_index == 0, own_index == count - 1]).astype(jnp.int32)

    row_blocks = token_rows.reshape(blocks_here, BLK, features)
    pack = pack_blocks(row_blocks, picked).reshape(count, capacity, BLK, features)
    ext_rows, fulls = spread(
        pack,
        row_blocks,
        (
            query_weight,
            key_weight,
            value_weight,
            output_weight,
            inner_weight,
            outer_weight,
            small,
        ),
        count,
        capacity,
    )
    full_query, full_key, full_value, full_output, full_inner, full_outer = (
        full.reshape(-1, full.shape[-1]) for full in fulls[:6]
    )
    vectors = [fulls[6][:, i, :part].reshape(-1) for i in range(8)]
    (
        full_query_bias,
        full_value_bias,
        full_output_bias,
        full_first_gain,
        full_first_shift,
        full_outer_bias,
        full_second_gain,
        full_second_shift,
    ) = vectors
    full_inner_bias = fulls[6][:, 8 : 8 + inner_parts, :part].reshape(-1)
    first_gain_f = full_first_gain.astype(jnp.float32)
    second_gain_f = full_second_gain.astype(jnp.float32)

    slots = ext_rows.shape[0]
    ext_flat = ext_rows.reshape(slots * BLK, features)
    queries_bf = (
        jnp.dot(token_rows, full_query, preferred_element_type=jnp.float32) + full_query_bias
    ).astype(jnp.bfloat16)
    keys_bf = jnp.dot(ext_flat, full_key, preferred_element_type=jnp.float32).astype(jnp.bfloat16)
    values_bf = (
        jnp.dot(ext_flat, full_value, preferred_element_type=jnp.float32) + full_value_bias
    ).astype(jnp.bfloat16)
    query_blocks = queries_bf.reshape(blocks_here, BLK, features)
    key_blocks = keys_bf.reshape(slots, BLK, features)
    value_blocks = values_bf.reshape(slots, BLK, features)
    mixed_blocks, log_total = attend(query_blocks, key_blocks, value_blocks, index, edge)
    mixed_bf = mixed_blocks.reshape(length, features)

    attention = (
        jnp.dot(mixed_bf, full_output, preferred_element_type=jnp.float32) + full_output_bias
    )
    stream = token_rows.astype(jnp.float32) + attention
    normed, first_normal, first_inverse = layer_norm(
        stream, first_gain_f, full_first_shift.astype(jnp.float32)
    )
    normed_bf = normed.astype(jnp.bfloat16)
    inner = jnp.dot(normed_bf, full_inner, preferred_element_type=jnp.float32) + full_inner_bias
    activated_bf = jax.nn.gelu(inner, approximate=False).astype(jnp.bfloat16)
    outer = jnp.dot(activated_bf, full_outer, preferred_element_type=jnp.float32) + full_outer_bias
    final, second_normal, second_inverse = layer_norm(
        normed + outer, second_gain_f, full_second_shift.astype(jnp.float32)
    )
    square_sums = jnp.stack([jnp.sum(stream * stream), jnp.sum(attention * attention)])

    output_grad = cotangent[0].astype(jnp.float32)
    second_stream_grad, second_gain_grad, second_shift_grad = norm_back(
        output_grad, second_normal, second_inverse, second_gain_f
    )
    outer_grad_bf = second_stream_grad.astype(jnp.bfloat16)
    outer_bias_grad = column_sum(outer_grad_bf)
    outer_weight_grad = outer_product(activated_bf, outer_grad_bf)
    inner_grad_bf = (back_product(outer_grad_bf, full_outer) * gelu_slope(inner)).astype(
        jnp.bfloat16
    )
    inner_bias_grad = column_sum(inner_grad_bf)
    inner_weight_grad = outer_product(normed_bf, inner_grad_bf)
    normed_grad = second_stream_grad + back_product(inner_grad_bf, full_inner)
    stream_grad, first_gain_grad, first_shift_grad = norm_back(
        normed_grad, first_normal, first_inverse, first_gain_f
    )
    attention_grad_bf = stream_grad.astype(jnp.bfloat16)
    output_bias_grad = column_sum(attention_grad_bf)
    output_weight_grad = outer_product(mixed_bf, attention_grad_bf)
    mixed_grad_bf = back_product(attention_grad_bf, full_output).astype(jnp.bfloat16)

    dq_blocks, dk_blocks, dv_blocks = attend_back(
        query_blocks,
        mixed_grad_bf.reshape(blocks_here, BLK, features),
        key_blocks,
        value_blocks,
        log_total,
        index,
        edge,
    )
    dq = dq_blocks.reshape(length, features)
    dk = dk_blocks.reshape(slots * BLK, features)
    dv = dv_blocks.reshape(slots * BLK, features)
    far_grad = (
        (back_product(dk[length:], full_key) + back_product(dv[length:], full_value))
        .astype(jnp.bfloat16)
        .reshape(slots - blocks_here, BLK, features)
    )
    back, rim, glob = return_grads(far_grad, count, capacity)
    near_grad = (
        stream_grad
        + back_product(dq, full_query)
        + back_product(dk[:length], full_key)
        + back_product(dv[:length], full_value)
    ).reshape(blocks_here, BLK, features)
    tokens_grad = unpack_grads(near_grad, back, rim, glob, picked, filled, edge)

    query_bias_grad = column_sum(dq)
    value_bias_grad = column_sum(dv)
    query_weight_grad = outer_product(token_rows, dq)
    key_weight_grad = outer_product(ext_flat, dk)
    value_weight_grad = outer_product(ext_flat, dv)

    def shared(grad):
        scattered = lax.psum_scatter(
            grad.astype(jnp.bfloat16), "wsh", scatter_dimension=0, tiled=True
        )
        return lax.psum(scattered, "ctx").astype(jnp.float32)

    vector_grads = (
        query_bias_grad,
        value_bias_grad,
        output_bias_grad,
        first_gain_grad,
        first_shift_grad,
        outer_bias_grad,
        second_gain_grad,
        second_shift_grad,
    )
    small_grads = jnp.concatenate(vector_grads + (inner_bias_grad, square_sums))
    small_sums = lax.psum(small_grads, ("ctx", "wsh"))
    element_count = count * groups * length * features
    stream_rms = jnp.sqrt(small_sums[-2:] / element_count)
    (
        query_bias_grad,
        value_bias_grad,
        output_bias_grad,
        first_gain_grad,
        first_shift_grad,
        outer_bias_grad,
        second_gain_grad,
        second_shift_grad,
    ) = (
        lax.dynamic_slice_in_dim(small_sums, i * features + own_group * part, part)
        for i in range(8)
    )
    inner_bias_grad = lax.dynamic_slice_in_dim(
        small_sums, 8 * features + own_group * inner_parts * part, inner_parts * part
    )
    return (
        final.astype(jnp.bfloat16)[None],
        tokens_grad.reshape(1, length, features),
        shared(query_weight_grad),
        query_bias_grad,
        shared(key_weight_grad),
        shared(value_weight_grad),
        value_bias_grad,
        shared(output_weight_grad),
        output_bias_grad,
        first_gain_grad,
        first_shift_grad,
        shared(inner_weight_grad),
        inner_bias_grad,
        shared(outer_weight_grad),
        outer_bias_grad,
        second_gain_grad,
        second_shift_grad,
        stream_rms,
    )


def solution(mesh):
    in_specs = (
        P("wsh", "ctx", None),
        P("wsh", "ctx", None),
        P("wsh", None, None),
        P("wsh", None),
        P("wsh"),
        P("wsh", None),
        P("wsh", None),
        P("wsh"),
        P("wsh", None),
        P("wsh"),
        P("wsh"),
        P("wsh"),
        P("wsh", None),
        P("wsh"),
        P("wsh", None),
        P("wsh"),
        P("wsh"),
        P("wsh"),
    )
    out_specs = (
        P("wsh", "ctx", None),
        P("wsh", "ctx", None),
        P("wsh", None),
        P("wsh"),
        P("wsh", None),
        P("wsh", None),
        P("wsh"),
        P("wsh", None),
        P("wsh"),
        P("wsh"),
        P("wsh"),
        P("wsh", None),
        P("wsh"),
        P("wsh", None),
        P("wsh"),
        P("wsh"),
        P("wsh"),
        P(),
    )
    return jax.shard_map(shards, mesh=mesh, in_specs=in_specs, out_specs=out_specs, check_vma=False)
```

time: 2010 us -> 887 us (0.44)
  local copies, waits for them, and re-layouts: 613 us -> 41.3 us
  Pallas kernels: 0 us -> 392 us
  blocking collectives: 389 us -> 68.9 us
  waiting for transfers between devices: 447 us -> 168 us
  other arithmetic: 185 us -> 24.5 us
  matrix products: 308 us -> 168 us
  starting transfers between devices: 32.1 us -> 0.29 us
    pallas_call x0 -> x6, Pallas kernels: none -> 392 us  [the longest x1 169 us: spread(): pl.pallas_call(functools.partial(spread_kernel, count, capacity), out_sha...]
    all_to_all x2 -> x0, waiting for transfers between devices: 323 us -> none  [the longest x1 164 us: shards(): lax.all_to_all(outgoing_grad.astype(jnp.bfloat16), 'ctx', split_axis=1, c...]
    psum x2 -> x1, blocking collectives: 358 us -> 68.9 us  [shards(): small_sums = lax.psum(small_grads, ('ctx', 'wsh'))]
    another operation x10 -> x3, local copies, waits for them, and re-layouts: 234 us -> 0.1 us  [the longest x1 0.09 us: request_tables(): wanted = random_rows.reshape(cycle_size, 3 * blocks_here)]
    reduce_scatter x3 -> x5, waiting for transfers between devices: 0.06 us -> 153 us  [shared(): lax.psum_scatter(grad.astype(jnp.bfloat16), 'wsh', scatter_dimension=0, t...]
    dot_general x6 -> x2, matrix products: 123 us -> 20.5 us  [the longest x1 12.5 us: shards(): jnp.dot(ext_flat, full_value, preferred_element_type=jnp.float32)]
    ppermute x4 -> x0, waiting for transfers between devices: 100 us -> none  [the longest x2 57.2 us: padded(): lax.ppermute(lax.slice_in_dim(block, block.shape[dim] - width, None, axis...]
    unnamed x2 -> x0, matrix products: 67.2 us -> none
  transfers between devices with their start and end apart: 18 -> 7, of which waited for: 7 -> 5; matrix products, arithmetic and copies ran while one was open for 27% -> 11% of each run, Pallas kernels for 0% -> 15%
where the time goes in v1:
time: 887 us; the launch traced here: 879 us
  Pallas kernels  392 us (44%)
  matrix products  168 us (19%)
  waiting for transfers between devices  168 us (19%)
  blocking collectives  68.9 us (8%)
  local copies, waits for them, and re-layouts  41.3 us (5%)
  other arithmetic  24.5 us (3%)
  between operations  15.1 us (2%)
    pallas_call x1, Pallas kernels, spread(): pl.pallas_call(functools.partial(spread_kernel, count, capacity), out_sha...  169 us
    reduce_scatter x5, waiting for transfers between devices, shared(): lax.psum_scatter(grad.astype(jnp.bfloat16), 'wsh', scatter_dimension=0, t...  153 us
    pallas_call x1, Pallas kernels, return_grads(): pl.pallas_call(functools.partial(return_kernel, count, capacity), out_sha...  133 us
    psum x1, blocking collectives, shards(): small_sums = lax.psum(small_grads, ('ctx', 'wsh'))  68.9 us
    dot_general x6, matrix products, outer_product(): jnp.einsum('ta,tb->ab', left, right, preferred_element_type=jnp.float32)  48 us
    dot_general x8, matrix products, back_product(): jnp.einsum('tb,ab->ta', upstream, weight, preferred_element_type=jnp.floa...  45.7 us
    pallas_call x1, Pallas kernels, attend_back(): pl.pallas_call(backward_kernel, out_shape=[jax.ShapeDtypeStruct(queries.s...  44.3 us
    pallas_call x1, Pallas kernels, attend(): pl.pallas_call(forward_kernel, out_shape=[jax.ShapeDtypeStruct(queries.sh...  37.8 us
  transfers between devices with their start and end apart: 7, of which 5 were waited for; matrix products, arithmetic and copies ran while one was open for 11% of the time, Pallas kernels for 15%

profile of v1, /device:TPU:0, one launch (start us, length us, event | category | flops | bytes accessed | tf_op | source)
XLA Modules:
  0.0 878.5 jit_solution(8631327343454402817)
XLA Ops:
  21.4 169.0 %spread_rows.1 = (bf16[68,64,768]{2,1,0:T(8,128)(2,1)}, bf16[4,192,768]{2,1,0:T(8,128)(2,1)}, bf16[4,192,768]{2,1,0:T(8,128)(2,1)}, bf16[4,192,768]{2,1,0:T(8,12...) custom-call(bf16[8,8,64,768]{3,2,1,0:T(8,128)(2,1)} %bitcast.117, ...), custom_call_target="tpu_custom_call" | custom-call | tf_op jit(solution)/shard_map/spread_rows/pallas_call | solution.py:295
  198.5 8.0 convolution_convert_fusion
  206.4 12.5 %add_convert_fusion = bf16[4352,768]{1,0:T(8,128)(2,1)} fusion(bf16[4352,768]{1,0:T(8,128)(2,1)} %bitcast.130, bf16[768,768]{1,0:T(8,128)(2,1)S(1)} %bitcast.126, f32[768]{0:T(1024)S(1)} %reshape.407), kind=kOutput, calls=%fused_computation.3 | convolution fusion | flops 5140512768 | bytes 14552064 | tf_op jit(solution)/shard_map/dot_general | solution.py:837
  219.1 37.8 %attend.1 = (bf16[16,64,768]{2,1,0:T(8,128)(2,1)S(1)}, f32[16,1,768]{2,1,0:T(1,128)S(1)}) custom-call(s32[128]{0:T(128)S(1)} %reshape.378.index_ref, s32[2]{0:T(128)S(1)} %add_convert_fusion.4.edge_ref, bf16[16,64,768]{2,1,0:T(8,128)(2,1)S(1)} %bitcast.105, bf16[68,64,768]{2,1,0:T(8,128)(2,1)S(1)} %bitcast.103, bf16[68,64,768]{2,1,0:T(8,128)(2,1)} %bitcast.115), custom_call_target="tpu_custom_call" | custom-call | tf_op jit(solution)/shard_map/attend/pallas_call | solution.py:599
  261.8 37.4 %fusion.2 = (bf16[1024,3072]{1,0:T(8,128)(2,1)S(1)}, f32[1024,3072]{1,0:T(8,128)}) fusion(f32[3072]{0:T(1024)S(1)} %reshape.411, bf16[768,3072]{1,0:T(8,128)(2,1)} %bitcast.131, f32[1024,768]{1,0:T(8,128)} %copy-done.9, f32[768]{0:T(1024)S(1)} %reshape.410, f32[768]{0:T(1024)S(1)} %reshape.409, f32[1024]{0:T(1024)S(1)} %add_rsqrt_fusion.1, ...), kind=kOutput, calls=%fused_computation.6 | convolution fusion | flops 5043388416 | bytes 26765312 | tf_op jit(solution)/shard_map/dot_general | solution.py:853
  299.2 9.9 %fusion.56 = (f32[1024]{0:T(1024)S(1)}, f32[1024,768]{1,0:T(8,128)S(1)}) fusion(f32[768]{0:T(1024)S(1)} %reshape.412, bf16[1024,3072]{1,0:T(8,128)(2,1)S(1)} %get-tuple-element.162, bf16[3072,768]{1,0:T(8,128)(2,1)} %bitcast.135, f32[768]{0:T(1024)S(1)} %reshape.410, f32[768]{0:T(1024)S(1)} %reshape.409, f32[1024]{0:T(1024)S(1)} %add_rsqrt_fusion.1, ...), kind=kOutput, calls=%fused_computation.125 | convolution fusion | flops 4837342208 | bytes 17323008 | tf_op jit(solution)/shard_map/dot_general | solution.py:855
  319.0 13.2 %convert_reduce_fusion.1 = (f32[3072]{0:T(1024)S(1)}, bf16[1024,3072]{1,0:T(8,128)(2,1)S(1)}) fusion(f32[1024,3072]{1,0:T(8,128)} %get-tuple-element.163, f32[3072]{0:T(1024)S(1)} %reshape.411, bf16[3072,768]{1,0:T(8,128)(2,1)} %bitcast.136, f32[1024,768]{1,0:T(8,128)S(1)} %get-tuple-element.145), kind=kOutput, calls=%fused_computation.13 | convolution fusion | flops 4873516032 | bytes 26763264 | tf_op jit(solution)/shard_map/tb,ab->ta/dot_general | solution.py:730
  332.2 6.4 multiply_reduce_fusion.2
  341.4 44.3 %attend_back.1 = (bf16[16,64,768]{2,1,0:T(8,128)(2,1)S(1)}, bf16[68,64,768]{2,1,0:T(8,128)(2,1)}, bf16[68,64,768]{2,1,0:T(8,128)(2,1)}) custom-call(s32[128]{0:T(128)S(1)} %reshape.378.index_ref, s32[2]{0:T(128)S(1)} %add_convert_fusion.4.edge_ref, bf16[16,64,768]{2,1,0:T(8,128)(2,1)S(1)} %bitcast.106, bf16[16,64,768]{2,1,0:T(8,128)(2,1)S(1)} %bitcast.110, ...), custom_call_target="tpu_custom_call" | custom-call | tf_op jit(solution)/shard_map/attend_back/pallas_call | solution.py:680
  395.2 10.6 %bitcast_convert_fusion = bf16[768,768]{1,0:T(8,128)(2,1)} fusion(bf16[68,64,768]{2,1,0:T(8,128)(2,1)} %get-tuple-element.36, bf16[68,64,768]{2,1,0:T(8,128)(2,1)} %get-tuple-element.46), kind=kOutput, calls=%fused_computation.64 | convolution fusion | flops 5134417920 | bytes 14548992 | tf_op jit(solution)/shard_map/ta,tb->ab/dot_general | solution.py:726
  405.9 10.4 %bitcast_convert_fusion.1 = bf16[768,768]{1,0:T(8,128)(2,1)} fusion(bf16[68,64,768]{2,1,0:T(8,128)(2,1)} %get-tuple-element.36, bf16[68,64,768]{2,1,0:T(8,128)(2,1)} %get-tuple-element.45), kind=kOutput, calls=%fused_computation.65 | convolution fusion | flops 5134417920 | bytes 14548992 | tf_op jit(solution)/shard_map/ta,tb->ab/dot_general | solution.py:726
  416.3 10.4 %convolution_convert_fusion.2 = bf16[768,3072]{1,0:T(8,128)(2,1)} fusion(bf16[1024,3072]{1,0:T(8,128)(2,1)} %copy-done.36, f32[1024,768]{1,0:T(8,128)} %copy-done.9, f32[768]{0:T(1024)S(1)} %reshape.410, f32[768]{0:T(1024)S(1)} %reshape.409, f32[1024]{0:T(1024)S(1)} %add_rsqrt_fusion.1, f32[1024]{0:T(1024)S(1)} %broadcast_multiply_fusion.5), kind=kOutput, calls=%fused_computation.32 | convolution fusion | flops 4838129664 | bytes 14170112 | tf_op jit(solution)/shard_map/ta,tb->ab/dot_general | solution.py:726
  426.9 9.7 %convolution_convert_fusion.1 = bf16[3072,768]{1,0:T(8,128)(2,1)} fusion(bf16[1024,3072]{1,0:T(8,128)(2,1)} %copy-done.37, f32[1024,768]{1,0:T(8,128)} %copy-done.17), kind=kOutput, calls=%fused_computation.31 | convolution fusion | flops 4834983936 | bytes 14155776 | tf_op jit(solution)/shard_map/ta,tb->ab/dot_general | solution.py:726
  436.6 5.3 slice.67
  441.9 5.4 slice.69
  453.0 9.4 %fusion.59 = f32[3328,768]{1,0:T(8,128)} fusion(bf16[3328,768]{1,0:T(8,128)(2,1)} %bitcast.122, bf16[768,768]{1,0:T(8,128)(2,1)S(1)} %bitcast.138), kind=kOutput, calls=%fused_computation.128 | convolution fusion | flops 3925868544 | bytes 16515072 | tf_op jit(solution)/shard_map/tb,ab->ta/dot_general | solution.py:730
  464.4 24.1 %reduce-scatter.11.cloned.1.call-done = bf16[192,768]{1,0:T(8,128)(2,1)} async-done(((bf16[768,768]{1,0:T(8,128)(2,1)}), bf16[192,768]{1,0:T(8,128)(2,1)}) %reduce-scatter.11.cloned.1.call-update) | async-done | bytes 294928 | tf_op jit(solution)/shard_map/reduce_scatter | solution.py:915
  488.5 28.3 %reduce-scatter.9.cloned.1.call-done = bf16[192,768]{1,0:T(8,128)(2,1)} async-done(((bf16[768,768]{1,0:T(8,128)(2,1)}), bf16[192,768]{1,0:T(8,128)(2,1)}) %reduce-scatter.9.cloned.1.call-update) | async-done | bytes 294928 | tf_op jit(solution)/shard_map/reduce_scatter | solution.py:915
  516.8 50.2 %reduce-scatter.15.cloned.1.call-done = bf16[192,3072]{1,0:T(8,128)(2,1)} async-done(((bf16[768,3072]{1,0:T(8,128)(2,1)}), bf16[192,3072]{1,0:T(8,128)(2,1)}) %reduce-scatter.15.cloned.1.call-update) | async-done | bytes 1179664 | tf_op jit(solution)/shard_map/reduce_scatter | solution.py:915
  567.1 50.4 %reduce-scatter.17.cloned.1.call-done = bf16[768,768]{1,0:T(8,128)(2,1)} async-done(((bf16[3072,768]{1,0:T(8,128)(2,1)}), bf16[768,768]{1,0:T(8,128)(2,1)}) %reduce-scatter.17.cloned.1.call-update) | async-done | bytes 1179664 | tf_op jit(solution)/shard_map/reduce_scatter | solution.py:915
  617.5 10.7 %add_convert_fusion.1 = bf16[3328,768]{1,0:T(8,128)(2,1)} fusion(f32[3328,768]{1,0:T(8,128)} %fusion.59, bf16[3328,768]{1,0:T(8,128)(2,1)} %bitcast.121, bf16[768,768]{1,0:T(8,128)(2,1)S(1)} %bitcast.127), kind=kOutput, calls=%fused_computation.29 | convolution fusion | flops 3930980352 | bytes 21626880 | tf_op jit(solution)/shard_map/tb,ab->ta/dot_general | solution.py:730
  628.3 132.6 %return_grads.1 = (bf16[8,8,64,768]{3,2,1,0:T(8,128)(2,1)}, bf16[2,64,768]{2,1,0:T(8,128)(2,1)}, bf16[8,64,768]{2,1,0:T(8,128)(2,1)}) custom-call(bf16[52,64,768]{2,1,0:T(8,128)(2,1)} %bitcast.123), custom_call_target="tpu_custom_call" | custom-call | tf_op jit(solution)/shard_map/return_grads/pallas_call | solution.py:448
  767.3 68.9 %psum.50 = f32[9218]{0:T(1024)S(1)} all-reduce(f32[9218]{0:T(1024)S(1)} %concatenate.11), channel_id=1, replica_groups=mesh['ctx'=8,'wsh'=4] {'ctx','wsh'}, use_global_device_ids=true, to_apply=%region_24.25 | all-reduce | flops 9218 | bytes 73744 | tf_op jit(solution)/shard_map/psum | solution.py:931
  847.8 15.2 %all-reduce.4.cloned.1.call-done = (bf16[192,768]{0,1:T(8,128)(2,1)}, bf16[192,768]{1,0:T(8,128)(2,1)}, bf16[192,768]{1,0:T(8,128)(2,1)}, bf16[192,768]{1,0:T(8,...) async-done(((bf16[192,768]{0,1:T(8,128)(2,1)}, bf16[192,768]{1,0:T(8,128)(2,1)}, bf16[192,768]{1,0:T(8,128)(2,1)}, bf16[192,768]{1,0:T(8,128)(2,1)}, ...) | async-done | bytes 3538960 | tf_op jit(solution)/shard_map/psum | solution.py:918
  (185 shorter events, 83.0 us)
Async XLA Ops:
  7.2 455.2 %reduce-scatter.19.cloned.1.call-start = ((), (), s32[]{:S(2)}) async-start(), calls=%async_computation.11 | async-start | bytes 1474560
  8.2 12.5 %copy-start.29 = (pred[8,48]{1,0:T(8,128)(4,1)}, pred[8,48]{1,0:T(8,128)(4,1)S(1)}, u32[]{:S(2)}) copy-start(pred[8,48]{1,0:T(8,128)(4,1)S(1)} %get-tuple-element.150) | copy-start | bytes 1156
  8.5 189.5 %copy-start.27 = (s32[8,48]{1,0:T(8,128)}, s32[8,48]{1,0:T(8,128)S(1)}, u32[]{:S(2)}) copy-start(s32[8,48]{1,0:T(8,128)S(1)} %convert_reduce_fusion.6) | copy-start | bytes 4612
  21.3 171.1 %copy-start.15 = (bf16[1,1024,768]{2,1,0:T(8,128)(2,1)S(1)}, bf16[1,1024,768]{2,1,0:T(8,128)(2,1)}, u32[]{:S(2)}) copy-start(bf16[1,1024,768]{2,1,0:T(8,128)(2,1)} %param.18) | copy-start | bytes 4718596
  206.4 12.6 %copy-start = (bf16[4352,768]{1,0:T(8,128)(2,1)}, bf16[4352,768]{1,0:T(8,128)(2,1)S(1)}, u32[]{:S(2)}) copy-start(bf16[4352,768]{1,0:T(8,128)(2,1)S(1)} %convolution_convert_fusion) | copy-start | bytes 20054020
  219.1 37.8 %copy-start.34 = (bf16[4,192,768]{2,1,0:T(8,128)(2,1)S(1)}, bf16[4,192,768]{2,1,0:T(8,128)(2,1)}, u32[]{:S(2)}) copy-start(bf16[4,192,768]{2,1,0:T(8,128)(2,1)} %get-tuple-element.40) | copy-start | bytes 3538948
  261.8 37.4 %copy-start.10 = (f32[1024,768]{1,0:T(8,128)S(1)}, f32[1024,768]{1,0:T(8,128)}, u32[]{:S(2)}) copy-start(f32[1024,768]{1,0:T(8,128)} %copy-done.9) | copy-start | bytes 9437188
  299.1 10.0 %copy-start.37 = (bf16[1024,3072]{1,0:T(8,128)(2,1)}, bf16[1024,3072]{1,0:T(8,128)(2,1)S(1)}, u32[]{:S(2)}) copy-start(bf16[1024,3072]{1,0:T(8,128)(2,1)S(1)} %get-tuple-element.162) | copy-start | bytes 18874372
  315.1 17.0 %slice-start.2 = ((s8[4718592]{0:T(1024)(128)(4,1)}), s8[4194304]{0:T(1024)(128)(4,1)S(1)}, s32[]{:S(2)}) async-start(s8[4718592]{0:T(1024)(128)(4,1)} %bitcast.132), calls=%async_computation.15 | async-start | bytes 8388608
  319.0 13.2 %copy-start.17 = (f32[1024,768]{1,0:T(8,128)}, f32[1024,768]{1,0:T(8,128)S(1)}, u32[]{:S(2)}) copy-start(f32[1024,768]{1,0:T(8,128)S(1)} %get-tuple-element.145) | copy-start | bytes 9437188
  319.0 13.2 %copy-start.11 = (f32[1024,768]{1,0:T(8,128)S(1)}, f32[1024,768]{1,0:T(8,128)}, u32[]{:S(2)}) copy-start(f32[1024,768]{1,0:T(8,128)} %copy-done.9) | copy-start | bytes 9437188
  319.0 13.2 %slice-start.3 = ((s8[4718592]{0:T(1024)(128)(4,1)}), s8[524288]{0:T(1024)(128)(4,1)S(1)}, s32[]{:S(2)}) async-start(s8[4718592]{0:T(1024)(128)(4,1)} %bitcast.132), calls=%async_computation.16 | async-start | bytes 1048576
  341.4 44.3 %copy-start.16 = (bf16[1,1024,768]{2,1,0:T(8,128)(2,1)S(1)}, bf16[1,1024,768]{2,1,0:T(8,128)(2,1)}, u32[]{:S(2)}) copy-start(bf16[1,1024,768]{2,1,0:T(8,128)(2,1)} %param.18) | copy-start | bytes 4718596
  390.7 73.7 %reduce-scatter.13.cloned.1.call-start = ((), (), s32[]{:S(2)}) async-start(), calls=%async_computation.8 | async-start | bytes 1474560 | tf_op jit(solution)/shard_map/reduce_scatter | solution.py:915
  395.2 93.3 %reduce-scatter.11.cloned.1.call-start = ((), (), s32[]{:S(2)}) async-start(), calls=%async_computation.7 | async-start | bytes 1474560 | tf_op jit(solution)/shard_map/reduce_scatter | solution.py:915
  405.8 111.0 %reduce-scatter.9.cloned.1.call-start = ((), (), s32[]{:S(2)}) async-start(), calls=%async_computation.6 | async-start | bytes 1474560 | tf_op jit(solution)/shard_map/reduce_scatter | solution.py:915
  416.3 150.8 %reduce-scatter.15.cloned.1.call-start = ((), (), s32[]{:S(2)}) async-start(), calls=%async_computation.9 | async-start | bytes 5898240 | tf_op jit(solution)/shard_map/reduce_scatter | solution.py:915
  426.8 190.7 %reduce-scatter.17.cloned.1.call-start = ((), (), s32[]{:S(2)}) async-start(), calls=%async_computation.10 | async-start | bytes 5898240 | tf_op jit(solution)/shard_map/reduce_scatter | solution.py:915
  436.6 426.5 %all-reduce.4.cloned.1.call-start = ((), (), s32[]{:S(2)}) async-start(), calls=%async_computation.12 | async-start | bytes 7274496 | tf_op jit(solution)/shard_map/psum | solution.py:918
  462.4 155.1 %copy-start.21 = (bf16[4,192,768]{2,1,0:T(8,128)(2,1)S(1)}, bf16[4,192,768]{2,1,0:T(8,128)(2,1)}, u32[]{:S(2)}) copy-start(bf16[4,192,768]{2,1,0:T(8,128)(2,1)} %get-tuple-element.38) | copy-start | bytes 3538948
  628.3 132.6 %copy-start.28 = (s32[8,48]{1,0:T(8,128)S(1)}, s32[8,48]{1,0:T(8,128)}, u32[]{:S(2)}) copy-start(s32[8,48]{1,0:T(8,128)} %copy-done.27) | copy-start | bytes 4612
  628.3 132.6 %copy-start.30 = (pred[8,48]{1,0:T(8,128)(4,1)S(1)}, pred[8,48]{1,0:T(8,128)(4,1)}, u32[]{:S(2)}) copy-start(pred[8,48]{1,0:T(8,128)(4,1)} %copy-done.29) | copy-start | bytes 1156
  628.3 133.3 %copy-start.8 = (bf16[1,1024,768]{2,1,0:T(8,128)(2,1)S(1)}, bf16[1,1024,768]{2,1,0:T(8,128)(2,1)}, u32[]{:S(2)}) copy-start(bf16[1,1024,768]{2,1,0:T(8,128)(2,1)} %param.19) | copy-start | bytes 4718596
  761.8 75.1 %copy-start.33 = (bf16[4,192,768]{2,1,0:T(8,128)(2,1)S(1)}, bf16[4,192,768]{2,1,0:T(8,128)(2,1)}, u32[]{:S(2)}) copy-start(bf16[4,192,768]{2,1,0:T(8,128)(2,1)} %get-tuple-element.34) | copy-start | bytes 3538948
  (25 other events, 76.2 us)
Sparse Core Ops, SparseCore 0:
  390.8 40.8 reduce-scatter.18
  434.4 25.7 reduce-scatter.12
  462.7 25.7 reduce-scatter.10
  491.1 25.7 reduce-scatter.8
  519.2 47.8 reduce-scatter.14
  569.6 47.8 reduce-scatter.16
  622.4 240.5 all-reduce.3

commit v2 on v1

--- a/solution.py
+++ b/solution.py
@@ -19,6 +19,12 @@
 NEG_FILL = -1e30
 MESH = pl.DeviceIdType.MESH
 MIB = 1 << 20
+
+
+def lasting(microseconds):
+    return pl.CostEstimate(
+        flops=int(microseconds * 1e9), bytes_accessed=int(microseconds * 1e6), transcendentals=0
+    )
 
 
 def request_tables(random_rows, cycle_size, blocks_here):
@@ -89,34 +95,55 @@
     )(picked, rows)
 
 
+def greet(count, groups):
+    barrier = pltpu.get_barrier_semaphore()
+    me = lax.axis_index("ctx")
+    w = lax.axis_index("wsh")
+
+    @pl.loop(1, count)
+    def _(delta):
+        pl.semaphore_signal(
+            barrier, inc=1, device_id={"ctx": (me + delta) % count}, device_id_type=MESH
+        )
+
+    for delta in range(1, groups):
+        pl.semaphore_signal(
+            barrier, inc=1, device_id={"wsh": (w + delta) % groups}, device_id_type=MESH
+        )
+    pl.semaphore_wait(barrier, count + groups - 2)
+
+
+def relays(count):
+    return ((3, 2, (4, 6)), (4, 5, (3, 1))) if count == 8 else ()
+
+
 def spread_kernel(count, capacity, *refs):
-    weights = (len(refs) - 2 - 1 - 9) // 2
+    weights = (len(refs) - 2 - 2 - 14) // 3
     pack, rows = refs[:2]
     shards = refs[2 : 2 + weights]
-    ext = refs[2 + weights]
-    fulls = refs[3 + weights : 3 + 2 * weights]
-    rand_s, rand_r, halo_s, halo_r, glob_s, glob_r, wgt_s, wgt_r, loc = refs[3 + 2 * weights :]
+    ext, passing = refs[2 + weights : 4 + weights]
+    fulls = refs[4 + weights : 4 + 2 * weights]
+    rest = refs[4 + 2 * weights :]
+    held = rest[:weights]
+    rand_s, rand_r, halo_s, halo_r, glob_s, glob_r, wgt_s, wgt_r = rest[weights : weights + 8]
+    pass_s, pass_r, loc_in, loc_out, own_pack, own_row = rest[weights + 8 :]
     blocks = rows.shape[0]
     base = blocks + EXTRA
     me = lax.axis_index("ctx")
     w = lax.axis_index("wsh")
     sib = w + 1 - 2 * (w % 2)
     far = (w + 2) % 4
-    far_sib = (sib + 2) % 4
     last = count - 1
     is_source = jnp.logical_and(me >= 1, me <= last - 1)
-
-    barrier = pltpu.get_barrier_semaphore()
-
-    @pl.loop(1, count)
-    def _(delta):
-        pl.semaphore_signal(
-            barrier, inc=1, device_id={"ctx": (me + delta) % count}, device_id_type=MESH
-        )
-
-    pl.semaphore_signal(barrier, inc=1, device_id={"wsh": sib}, device_id_type=MESH)
-    pl.semaphore_signal(barrier, inc=1, device_id={"wsh": far}, device_id_type=MESH)
-    pl.semaphore_wait(barrier, count + 1)
+    routes = relays(count)
+    greet(count, 4)
+
+    def relayed(dst):
+        found = me < 0
+        for source, _, targets in routes:
+            for target in targets:
+                found = jnp.logical_or(found, jnp.logical_and(me == source, dst == target))
+        return found
 
     def weight_copy(i, step):
         if step == 2:
@@ -132,23 +159,43 @@
             device_id_type=MESH,
         )
 
-    def random_copy(dst):
+    def random_copy(dst, k):
         return pltpu.make_async_remote_copy(
-            src_ref=pack.at[dst],
-            dst_ref=ext.at[pl.ds(base + (me - 1) * capacity, capacity)],
-            send_sem=rand_s.at[dst],
-            recv_sem=rand_r.at[me],
+            src_ref=pack.at[dst, k],
+            dst_ref=ext.at[base + (me - 1) * capacity + k],
+            send_sem=rand_s.at[dst, k],
+            recv_sem=rand_r.at[me, k],
             device_id={"ctx": dst},
             device_id_type=MESH,
         )
 
-    def random_landed(source):
+    def random_landed(source, k):
         return pltpu.make_async_remote_copy(
-            src_ref=pack.at[source],
-            dst_ref=ext.at[pl.ds(base + (source - 1) * capacity, capacity)],
-            send_sem=rand_s.at[source],
-            recv_sem=rand_r.at[source],
+            src_ref=pack.at[source, k],
+            dst_ref=ext.at[base + (source - 1) * capacity + k],
+            send_sem=rand_s.at[source, k],
+            recv_sem=rand_r.at[source, k],
             device_id={"ctx": source},
+            device_id_type=MESH,
+        )
+
+    def to_relay(via, r, dst, k):
+        return pltpu.make_async_remote_copy(
+            src_ref=pack.at[dst, k],
+            dst_ref=passing.at[r, k],
+            send_sem=rand_s.at[dst, k],
+            recv_sem=pass_r.at[r, k],
+            device_id={"ctx": via},
+            device_id_type=MESH,
+        )
+
+    def from_relay(source, r, dst, k):
+        return pltpu.make_async_remote_copy(
+            src_ref=passing.at[r, k],
+            dst_ref=ext.at[base + (source - 1) * capacity + k],
+            send_sem=pass_s.at[r, k],
+            recv_sem=rand_r.at[source, k],
+            device_id={"ctx": dst},
             device_id_type=MESH,
         )
 
@@ -172,8 +219,39 @@
             device_id_type=MESH,
         )
 
+    def held_in(i):
+        return pltpu.make_async_copy(shards[i], held[i], loc_in.at[2 + i])
+
+    def held_out(i):
+        return pltpu.make_async_copy(held[i], fulls[i].at[w], loc_out.at[2 + i])
+
+    def rows_in():
+        return pltpu.make_async_copy(rows, own_row, loc_in.at[0])
+
+    def rows_out():
+        return pltpu.make_async_copy(own_row, ext.at[pl.ds(0, blocks)], loc_out.at[0])
+
+    def pack_in():
+        return pltpu.make_async_copy(pack.at[me], own_pack, loc_in.at[1])
+
+    def pack_out():
+        return pltpu.make_async_copy(
+            own_pack, ext.at[pl.ds(base + (me - 1) * capacity, capacity)], loc_out.at[1]
+        )
+
+    def rim_out(side):
+        return pltpu.make_async_copy(own_row.at[0], ext.at[blocks + side], loc_out.at[2 + weights])
+
+    def global_out(which):
+        return pltpu.make_async_copy(
+            own_row.at[0 if which == 0 else blocks - 1],
+            ext.at[blocks + 2 + which],
+            loc_out.at[3 + weights],
+        )
+
     for i in range(weights):
         weight_copy(i, 0).start()
+        weight_copy(i, 1).start()
 
     @pl.when(me < last)
     def _():
@@ -182,12 +260,6 @@
     @pl.when(me > 0)
     def _():
         halo_copy(1).start()
-
-    @pl.when(is_source)
-    def _():
-        @pl.loop(1, count)
-        def _(delta):
-            random_copy((me + delta) % count).start()
 
     for which, owner in ((0, 0), (1, last)):
 
@@ -197,65 +269,89 @@
             def _(delta):
                 global_copy(which, (me + delta) % count).start()
 
+    for k in range(capacity):
+        for source, via, targets in routes:
+
+            @pl.when(me == source)
+            def _():
+                for r, target in enumerate(targets):
+                    to_relay(via, r, target, k).start()
+
+        @pl.when(is_source)
+        def _():
+            @pl.loop(1, count)
+            def _(delta):
+                dst = (me + delta) % count
+
+                @pl.when(jnp.logical_not(relayed(dst)))
+                def _():
+                    random_copy(dst, k).start()
+
+    rows_in().start()
     for i in range(weights):
-        weight_copy(i, 1).start()
-
-    def own_rows():
-        return pltpu.make_async_copy(rows, ext.at[pl.ds(0, blocks)], loc.at[0])
-
-    def own_weight(i):
-        return pltpu.make_async_copy(shards[i], fulls[i].at[w], loc.at[5 + i])
-
-    def own_random():
-        return pltpu.make_async_copy(
-            pack.at[me], ext.at[pl.ds(base + (me - 1) * capacity, capacity)], loc.at[1]
-        )
-
-    def own_rim(side):
-        return pltpu.make_async_copy(rows.at[0], ext.at[blocks + side], loc.at[2])
-
-    def own_global(which):
-        return pltpu.make_async_copy(
-            rows.at[0 if which == 0 else blocks - 1], ext.at[blocks + 2 + which], loc.at[3]
-        )
-
-    own_rows().start()
-    for i in range(weights):
-        own_weight(i).start()
+        held_in(i).start()
 
     @pl.when(is_source)
     def _():
-        own_random().start()
-
+        pack_in().start()
+        pack_in().wait()
+        pack_out().start()
+
+    rows_in().wait()
+    rows_out().start()
     for which, owner in ((0, 0), (1, last)):
 
         @pl.when(me == owner)
         def _():
-            own_rim(which).start()
-            own_global(which).start()
+            rim_out(which).start()
+            global_out(which).start()
 
     for i in range(weights):
-        weight_copy(i, 0).wait_recv()
-        weight_copy(i, 2).start()
-
-    own_rows().wait()
+        held_in(i).wait()
+        held_out(i).start()
+
+    for step in range(max(capacity, weights)):
+        if step < capacity:
+            for source, via, targets in routes:
+
+                @pl.when(me == via)
+                def _():
+                    for r, target in enumerate(targets):
+                        to_relay(via, r, target, step).wait_recv()
+                        from_relay(source, r, target, step).start()
+
+        if step < weights:
+            weight_copy(step, 0).wait_recv()
+            weight_copy(step, 2).start()
+
+    rows_out().wait()
     for i in range(weights):
-        own_weight(i).wait()
+        held_out(i).wait()
 
     @pl.when(is_source)
     def _():
-        own_random().wait()
-
-        @pl.loop(1, count)
-        def _(delta):
-            random_copy((me + delta) % count).wait_send()
+        pack_out().wait()
+
+        for k in range(capacity):
+
+            @pl.loop(1, count)
+            def _(delta):
+                random_copy((me + delta) % count, k).wait_send()
+
+    for source, via, targets in routes:
+
+        @pl.when(me == via)
+        def _():
+            for r, target in enumerate(targets):
+                for k in range(capacity):
+                    from_relay(source, r, target, k).wait_send()
 
     for which, owner in ((0, 0), (1, last)):
 
         @pl.when(me == owner)
         def _():
-            own_rim(which).wait()
-            own_global(which).wait()
+            rim_out(which).wait()
+            global_out(which).wait()
 
             @pl.loop(1, count)
             def _(delta):
@@ -275,11 +371,13 @@
         halo_copy(1).wait_send()
         halo_copy(0).wait_recv()
 
-    @pl.loop(1, last)
-    def _(source):
-        @pl.when(source != me)
-        def _():
-            random_landed(source).wait_recv()
+    for k in range(capacity):
+
+        @pl.loop(1, last)
+        def _(source):
+            @pl.when(source != me)
+            def _():
+                random_landed(source, k).wait_recv()
 
     for i in range(weights):
         for step in range(3):
@@ -290,66 +388,339 @@
 
 def spread(pack, rows, shards, count, capacity):
     blocks = rows.shape[0]
+    tail = rows.shape[1:]
     weights = len(shards)
     slots = blocks + EXTRA + (count - 2) * capacity
     outs = pl.pallas_call(
         functools.partial(spread_kernel, count, capacity),
-        out_shape=[jax.ShapeDtypeStruct((slots,) + rows.shape[1:], rows.dtype)]
+        out_shape=[
+            jax.ShapeDtypeStruct((slots,) + tail, rows.dtype),
+            jax.ShapeDtypeStruct((2, capacity) + tail, rows.dtype),
+        ]
         + [jax.ShapeDtypeStruct((4,) + shard.shape, shard.dtype) for shard in shards],
         in_specs=[pl.BlockSpec(memory_space=pl.ANY)] * (2 + weights),
-        out_specs=[pl.BlockSpec(memory_space=pl.ANY)] * (1 + weights),
-        scratch_shapes=[
-            pltpu.SemaphoreType.DMA((count,)),
-            pltpu.SemaphoreType.DMA((count,)),
+        out_specs=[pl.BlockSpec(memory_space=pl.ANY)] * (2 + weights),
+        scratch_shapes=[pltpu.VMEM(shard.shape, shard.dtype) for shard in shards]
+        + [
+            pltpu.SemaphoreType.DMA((count, capacity)),
+            pltpu.SemaphoreType.DMA((count, capacity)),
             pltpu.SemaphoreType.DMA((2,)),
             pltpu.SemaphoreType.DMA((2,)),
             pltpu.SemaphoreType.DMA((count,)),
             pltpu.SemaphoreType.DMA((2,)),
             pltpu.SemaphoreType.DMA((weights, 3)),
             pltpu.SemaphoreType.DMA((weights, 3)),
-            pltpu.SemaphoreType.DMA((5 + weights,)),
+            pltpu.SemaphoreType.DMA((2, capacity)),
+            pltpu.SemaphoreType.DMA((2, capacity)),
+            pltpu.SemaphoreType.DMA((4 + weights,)),
+            pltpu.SemaphoreType.DMA((4 + weights,)),
+            pltpu.VMEM((capacity,) + tail, rows.dtype),
+            pltpu.VMEM(rows.shape, rows.dtype),
         ],
-        compiler_params=pltpu.CompilerParams(collective_id=0, has_side_effects=True),
+        compiler_params=pltpu.CompilerParams(
+            collective_id=0, has_side_effects=True, vmem_limit_bytes=16 * MIB
+        ),
+        cost_estimate=lasting(110),
         name="spread_rows",
     )(pack, rows, *shards)
-    return outs[0], outs[1:]
-
-
-def return_kernel(
-    count, capacity, far_grad, back, rim, glob, rand_s, rand_r, halo_s, halo_r, glob_s, glob_r, loc
-):
+    return outs[0], outs[2:]
+
+
+class Reducer:
+    def __init__(self, count, grads, out, scratch):
+        self.grads = grads
+        self.out = out
+        (
+            self.own,
+            self.from_sib,
+            self.from_far,
+            self.from_pair,
+            self.chain_in,
+            self.load_sem,
+            self.sib_s,
+            self.sib_r,
+            self.far_s,
+            self.far_r,
+            self.pair_s,
+            self.pair_r,
+            self.chain_s,
+            self.chain_r,
+            self.wide_s,
+            self.wide_r,
+            self.back_s,
+            self.back_r,
+        ) = scratch
+        self.units = out.shape[0]
+        self.top = count // 2 - 1
+        me = lax.axis_index("ctx")
+        w = lax.axis_index("wsh")
+        self.w = w
+        self.me = me
+        self.sib = w + 1 - 2 * (w % 2)
+        self.far = (w + 2) % 4
+        self.sib_far = (self.sib + 2) % 4
+        self.side = me % 2
+        self.level = me // 2
+        self.pair = me + 1 - 2 * self.side
+
+    def unit(self, u, quarter):
+        singles = len(self.grads) - 2
+        inner, outer = self.grads[-2:]
+        part, features = self.out.shape[1] * self.out.shape[2], self.out.shape[3]
+        if u < singles:
+            return self.grads[u].at[quarter]
+        u -= singles
+        across = inner.shape[2] // features
+        if u < across:
+            return inner.at[quarter, :, pl.ds(u * features, features)]
+        return outer.at[quarter, pl.ds((u - across) * part, part)]
+
+    def load(self, u, slot):
+        return pltpu.make_async_copy(
+            self.unit(u, (self.w, self.far)[slot]), self.own.at[u, slot], self.load_sem.at[u, slot]
+        )
+
+    def remote(self, src, dst, send, recv, **device):
+        return pltpu.make_async_remote_copy(
+            src_ref=src,
+            dst_ref=dst,
+            send_sem=send,
+            recv_sem=recv,
+            device_id=device,
+            device_id_type=MESH,
+        )
+
+    def to_sib(self, u, slot):
+        return self.remote(
+            self.unit(u, (self.sib, self.sib_far)[slot]),
+            self.from_sib.at[u, slot],
+            self.sib_s.at[u, slot],
+            self.sib_r.at[u, slot],
+            wsh=self.sib,
+        )
+
+    def to_far(self, u):
+        return self.remote(
+            self.own.at[u, 1],
+            self.from_far.at[u],
+            self.far_s.at[u],
+            self.far_r.at[u],
+            wsh=self.far,
+        )
+
+    def half(self, u, side):
+        rows = self.out.shape[2]
+        return self.own.at[u, 0, pl.ds(pl.multiple_of(side * rows, rows), rows)]
+
+    def to_pair(self, u):
+        return self.remote(
+            self.half(u, 1 - self.side),
+            self.from_pair.at[u],
+            self.pair_s.at[u],
+            self.pair_r.at[u],
+            ctx=self.pair,
+        )
+
+    def toward(self, u):
+        return 2 if u % 2 == 0 else -2
+
+    def place(self, u, hop):
+        return hop if u % 2 == 0 else self.top - hop
+
+    def along(self, u):
+        return self.remote(
+            self.from_pair.at[u],
+            self.chain_in.at[u],
+            self.chain_s.at[u],
+            self.chain_r.at[u],
+            ctx=self.me + self.toward(u),
+        )
+
+    def widen(self, u):
+        place = self.out.at[u, self.side]
+        return self.remote(
+            place, place, self.wide_s.at[u], self.wide_r.at[u], ctx=self.me - self.toward(u)
+        )
+
+    def give_back(self, u, side):
+        place = self.out.at[u, side]
+        return self.remote(place, place, self.back_s.at[u], self.back_r.at[u], ctx=self.pair)
+
+
+    def begin(self, u):
+        for slot in (1, 0):
+            self.to_sib(u, slot).start()
+            self.load(u, slot).start()
+
+    def join_sib(self, u):
+        for slot in (1, 0):
+            self.load(u, slot).wait()
+            self.to_sib(u, slot).wait_recv()
+            self.own[u, slot] = add_bf16(self.own[u, slot], self.from_sib[u, slot])
+            if slot == 1:
+                self.to_far(u).start()
+
+    def join_far(self, u):
+        self.to_far(u).wait_recv()
+        self.own[u, 0] = add_bf16(self.own[u, 0], self.from_far[u])
+        self.to_pair(u).start()
+
+    def join_pair(self, u):
+        self.to_pair(u).wait_recv()
+        self.from_pair[u] = add_bf16(self.half(u, self.side)[...], self.from_pair[u])
+
+    def gather(self, u, hop):
+        @pl.when(self.level == self.place(u, hop))
+        def _():
+            if hop > 0:
+                self.along(u).wait_recv()
+                total = add_bf16(self.from_pair[u], self.chain_in[u])
+                if hop < self.top:
+                    self.from_pair[u] = total
+                else:
+                    self.out[u, self.side] = total
+            if hop < self.top:
+                self.along(u).start()
+            else:
+                self.widen(u).start()
+                self.give_back(u, self.side).start()
+
+    def spread_out(self, u, hop):
+        @pl.when(self.level == self.place(u, hop))
+        def _():
+            self.widen(u).wait_recv()
+            if hop > 0:
+                self.widen(u).start()
+            self.give_back(u, self.side).start()
+
+    def steps(self):
+        return self.units + 2 * self.top + 3
+
+    def step(self, t):
+        lag = 0
+
+        def unit(lag):
+            u = t - lag
+            return u if 0 <= u < self.units else None
+
+        for stage in (self.join_sib, self.join_far, self.join_pair):
+            if unit(lag) is not None:
+                stage(unit(lag))
+            lag += 1
+        lag -= 1
+        for hop in range(self.top + 1):
+            if unit(lag) is not None:
+                self.gather(unit(lag), hop)
+            lag += 1
+        for hop in range(self.top - 1, -1, -1):
+            if unit(lag) is not None:
+                self.spread_out(unit(lag), hop)
+            lag += 1
+
+    def finish(self):
+        for u in range(self.units):
+            self.give_back(u, 1 - self.side).wait_recv()
+            self.give_back(u, self.side).wait_send()
+
+            @pl.when(self.level != self.place(u, self.top))
+            def _():
+                self.along(u).wait_send()
+
+            @pl.when(self.level != self.place(u, 0))
+            def _():
+                self.widen(u).wait_send()
+
+            for slot in range(2):
+                self.to_sib(u, slot).wait_send()
+            self.to_far(u).wait_send()
+            self.to_pair(u).wait_send()
+
+
+def add_bf16(left, right):
+    return (left.astype(jnp.float32) + right.astype(jnp.float32)).astype(jnp.bfloat16)
+
+
+def unit_count(grads):
+    inner, outer = grads[-2:]
+    features = outer.shape[2]
+    return len(grads) - 2 + inner.shape[2] // features + outer.shape[1] // (features // 4)
+
+
+def reducer_shapes(grads):
+    units = unit_count(grads)
+    features = grads[-1].shape[2]
+    part = features // 4
+    dma = pltpu.SemaphoreType.DMA
+    kind = jnp.bfloat16
+    out = jax.ShapeDtypeStruct((units, 2, part // 2, features), kind)
+    scratch = [
+        pltpu.VMEM((units, 2, part, features), kind),
+        pltpu.VMEM((units, 2, part, features), kind),
+        pltpu.VMEM((units, part, features), kind),
+        pltpu.VMEM((units, part // 2, features), kind),
+        pltpu.VMEM((units, part // 2, features), kind),
+        dma((units, 2)),
+        dma((units, 2)),
+        dma((units, 2)),
+        dma((units,)),
+        dma((units,)),
+        dma((units,)),
+        dma((units,)),
+        dma((units,)),
+        dma((units,)),
+        dma((units,)),
+        dma((units,)),
+        dma((units,)),
+        dma((units,)),
+    ]
+    return out, scratch
+
+
+def return_kernel(count, capacity, weights, far_grad, small, *refs):
+    grads = refs[:weights]
+    back, rim, glob, small_out = refs[weights : weights + 4]
+    refs = refs[weights + 4 :]
+    reducer = None
+    if weights:
+        reducer = Reducer(count, grads, refs[0], refs[1 + 15 :])
+        refs = refs[1:]
+    rand_s, rand_r, halo_s, halo_r, glob_s, glob_r, loc, own_far, own_glob = refs[:9]
+    group_part, ring_part, group_s, group_r, ring_s, ring_r = refs[9:15]
     me = lax.axis_index("ctx")
+    w = lax.axis_index("wsh")
     last = count - 1
+    groups = small.shape[0]
     is_source = jnp.logical_and(me >= 1, me <= last - 1)
-    barrier = pltpu.get_barrier_semaphore()
-
-    @pl.loop(1, count)
-    def _(delta):
-        pl.semaphore_signal(
-            barrier, inc=1, device_id={"ctx": (me + delta) % count}, device_id_type=MESH
-        )
-
-    pl.semaphore_wait(barrier, count - 1)
-
-    def random_copy(owner, sender):
+    greet(count, groups)
+
+    def random_copy(owner, sender, k):
         return pltpu.make_async_remote_copy(
-            src_ref=far_grad.at[pl.ds(EXTRA + (owner - 1) * capacity, capacity)],
-            dst_ref=back.at[sender],
-            send_sem=rand_s.at[owner],
-            recv_sem=rand_r.at[sender],
+            src_ref=far_grad.at[EXTRA + (owner - 1) * capacity + k],
+            dst_ref=back.at[sender, k],
+            send_sem=rand_s.at[owner, k],
+            recv_sem=rand_r.at[sender, k],
             device_id={"ctx": owner},
             device_id_type=MESH,
         )
 
-    def landed(sender):
+    def landed(sender, k):
         return pltpu.make_async_remote_copy(
-            src_ref=far_grad.at[pl.ds(EXTRA, capacity)],
-            dst_ref=back.at[sender],
-            send_sem=rand_s.at[sender],
-            recv_sem=rand_r.at[sender],
+            src_ref=far_grad.at[EXTRA + k],
+            dst_ref=back.at[sender, k],
+            send_sem=rand_s.at[sender, k],
+            recv_sem=rand_r.at[sender, k],
             device_id={"ctx": sender},
             device_id_type=MESH,
         )
+
+    def send_random(k):
+        @pl.loop(1, count)
+        def _(delta):
+            owner = (me + delta) % count
+
+            @pl.when(jnp.logical_and(owner >= 1, owner <= last - 1))
+            def _():
+                random_copy(owner, me, k).start()
 
     def halo_copy(side):
         return pltpu.make_async_remote_copy(
@@ -371,6 +742,29 @@
             device_id_type=MESH,
         )
 
+    def group_copy(target, sender):
+        return pltpu.make_async_remote_copy(
+            src_ref=small.at[target],
+            dst_ref=group_part.at[sender],
+            send_sem=group_s.at[target],
+            recv_sem=group_r.at[sender],
+            device_id={"wsh": target},
+            device_id_type=MESH,
+        )
+
+    def ring_copy(target, sender):
+        return pltpu.make_async_remote_copy(
+            src_ref=ring_part.at[me],
+            dst_ref=ring_part.at[sender],
+            send_sem=ring_s.at[target],
+            recv_sem=ring_r.at[sender],
+            device_id={"ctx": target},
+            device_id_type=MESH,
+        )
+
+    for delta in range(1, groups):
+        group_copy((w + delta) % groups, w).start()
+
     @pl.when(me > 0)
     def _():
         halo_copy(0).start()
@@ -381,40 +775,87 @@
         halo_copy(1).start()
         global_copy(1, me).start()
 
+    if reducer:
+        for u in range(reducer.units):
+            reducer.begin(u)
+    else:
+        for k in range(capacity):
+            send_random(k)
+
+    total = small[w]
+    for delta in range(1, groups):
+        sender = (w + delta) % groups
+        group_copy(w, sender).wait_recv()
+        total = total + group_part[sender]
+    ring_part[me] = total
+
     @pl.loop(1, count)
     def _(delta):
-        owner = (me + delta) % count
-
-        @pl.when(jnp.logical_and(owner >= 1, owner <= last - 1))
-        def _():
-            random_copy(owner, me).start()
-
-    def own_random():
+        ring_copy((me + delta) % count, me).start()
+
+    def own_random_in():
         return pltpu.make_async_copy(
-            far_grad.at[pl.ds(EXTRA + (me - 1) * capacity, capacity)], back.at[me], loc.at[0]
-        )
-
-    def own_global(which):
-        return pltpu.make_async_copy(far_grad.at[2 + which], glob.at[me], loc.at[1])
+            far_grad.at[pl.ds(EXTRA + (me - 1) * capacity, capacity)], own_far, loc.at[0]
+        )
+
+    def own_random_out():
+        return pltpu.make_async_copy(own_far, back.at[me], loc.at[1])
+
+    def own_global_in(which):
+        return pltpu.make_async_copy(far_grad.at[2 + which], own_glob, loc.at[2])
+
+    def own_global_out():
+        return pltpu.make_async_copy(own_glob, glob.at[me], loc.at[3])
 
     @pl.when(is_source)
     def _():
-        own_random().start()
-        own_random().wait()
-
+        own_random_in().start()
+        own_random_in().wait()
+        own_random_out().start()
+        own_random_out().wait()
+
+    for which, owner in ((0, 0), (1, last)):
+
+        @pl.when(me == owner)
+        def _():
+            own_global_in(which).start()
+            own_global_in(which).wait()
+            own_global_out().start()
+            own_global_out().wait()
+
+    @pl.loop(1, count)
+    def _(delta):
+        ring_copy(me, (me + delta) % count).wait_recv()
+
+    small_out[...] = jnp.sum(ring_part[...], axis=0)
+
+    if reducer:
+        for t in range(reducer.steps()):
+            if t < capacity:
+                send_random(t)
+            reducer.step(t)
+        reducer.finish()
+
+    @pl.loop(1, count)
+    def _(delta):
+        ring_copy((me + delta) % count, me).wait_send()
+
+    for delta in range(1, groups):
+        group_copy((w + delta) % groups, w).wait_send()
+
+    @pl.when(is_source)
+    def _():
         @pl.loop(0, count)
         def _(sender):
             @pl.when(sender != me)
             def _():
-                landed(sender).wait_recv()
+                for k in range(capacity):
+                    landed(sender, k).wait_recv()
 
     for which, owner in ((0, 0), (1, last)):
 
         @pl.when(me == owner)
         def _():
-            own_global(which).start()
-            own_global(which).wait()
-
             @pl.loop(0, count)
             def _(sender):
                 @pl.when(sender != me)
@@ -439,33 +880,53 @@
 
         @pl.when(jnp.logical_and(owner >= 1, owner <= last - 1))
         def _():
-            random_copy(owner, me).wait_send()
-
-
-def return_grads(far_grad, count, capacity):
+            for k in range(capacity):
+                random_copy(owner, me, k).wait_send()
+
+
+def return_grads(far_grad, small, grads, count, capacity):
     tail = far_grad.shape[1:]
     kind = far_grad.dtype
+    groups = small.shape[0]
+    hbm = pl.BlockSpec(memory_space=pl.ANY)
+    vmem = pl.BlockSpec(memory_space=pltpu.VMEM)
+    sums, sum_scratch = reducer_shapes(grads) if grads else (None, [])
+    dma = pltpu.SemaphoreType.DMA
     return pl.pallas_call(
-        functools.partial(return_kernel, count, capacity),
+        functools.partial(return_kernel, count, capacity, len(grads)),
         out_shape=[
             jax.ShapeDtypeStruct((count, capacity) + tail, kind),
             jax.ShapeDtypeStruct((2,) + tail, kind),
             jax.ShapeDtypeStruct((count,) + tail, kind),
-        ],
-        in_specs=[pl.BlockSpec(memory_space=pl.ANY)],
-        out_specs=[pl.BlockSpec(memory_space=pl.ANY)] * 3,
+            jax.ShapeDtypeStruct(small.shape[1:], jnp.float32),
+        ]
+        + ([sums] if grads else []),
+        in_specs=[hbm, vmem] + [hbm] * len(grads),
+        out_specs=[hbm, hbm, hbm, vmem] + ([vmem] if grads else []),
         scratch_shapes=[
-            pltpu.SemaphoreType.DMA((count,)),
-            pltpu.SemaphoreType.DMA((count,)),
-            pltpu.SemaphoreType.DMA((2,)),
-            pltpu.SemaphoreType.DMA((2,)),
-            pltpu.SemaphoreType.DMA((2,)),
-            pltpu.SemaphoreType.DMA((count,)),
-            pltpu.SemaphoreType.DMA((2,)),
-        ],
-        compiler_params=pltpu.CompilerParams(collective_id=1, has_side_effects=True),
+            dma((count, capacity)),
+            dma((count, capacity)),
+            dma((2,)),
+            dma((2,)),
+            dma((2,)),
+            dma((count,)),
+            dma((4,)),
+            pltpu.VMEM((capacity,) + tail, kind),
+            pltpu.VMEM(tail, kind),
+            pltpu.VMEM(small.shape, jnp.float32),
+            pltpu.VMEM((count,) + small.shape[1:], jnp.float32),
+            dma((groups,)),
+            dma((groups,)),
+            dma((count,)),
+            dma((count,)),
+        ]
+        + sum_scratch,
+        compiler_params=pltpu.CompilerParams(
+            collective_id=1, has_side_effects=True, vmem_limit_bytes=48 * MIB
+        ),
+        cost_estimate=lasting(150),
         name="return_grads",
-    )(far_grad)
+    )(far_grad, small, *grads)
 
 
 def unpack_kernel(
@@ -616,6 +1077,7 @@
             ],
         ),
         compiler_params=pltpu.CompilerParams(vmem_limit_bytes=40 * MIB),
+        cost_estimate=lasting(37),
         name="attend",
     )(index, edge, queries, keys, values)
 
@@ -695,6 +1157,7 @@
             ],
         ),
         compiler_params=pltpu.CompilerParams(vmem_limit_bytes=48 * MIB),
+        cost_estimate=lasting(44),
         name="attend_back",
     )(index, edge, queries, upstream, keys, values, log_total)
 
@@ -760,7 +1223,6 @@
     count = lax.axis_size("ctx")
     groups = lax.axis_size("wsh")
     own_index = lax.axis_index("ctx")
-    own_group = lax.axis_index("wsh")
     capacity = (3 * blocks_here + count - 3) // (count - 2)
     part = features // groups
     inner_parts = inner_bias.shape[0] // part
@@ -896,27 +1358,19 @@
         .astype(jnp.bfloat16)
         .reshape(slots - blocks_here, BLK, features)
     )
-    back, rim, glob = return_grads(far_grad, count, capacity)
-    near_grad = (
-        stream_grad
-        + back_product(dq, full_query)
-        + back_product(dk[:length], full_key)
-        + back_product(dv[:length], full_value)
-    ).reshape(blocks_here, BLK, features)
-    tokens_grad = unpack_grads(near_grad, back, rim, glob, picked, filled, edge)
-
     query_bias_grad = column_sum(dq)
     value_bias_grad = column_sum(dv)
-    query_weight_grad = outer_product(token_rows, dq)
-    key_weight_grad = outer_product(ext_flat, dk)
-    value_weight_grad = outer_product(ext_flat, dv)
-
-    def shared(grad):
-        scattered = lax.psum_scatter(
-            grad.astype(jnp.bfloat16), "wsh", scatter_dimension=0, tiled=True
-        )
-        return lax.psum(scattered, "ctx").astype(jnp.float32)
-
+    weight_grads = tuple(
+        grad.astype(jnp.bfloat16).reshape(groups, -1, grad.shape[-1])
+        for grad in (
+            outer_product(token_rows, dq),
+            outer_product(ext_flat, dk),
+            outer_product(ext_flat, dv),
+            output_weight_grad,
+            inner_weight_grad,
+            outer_weight_grad,
+        )
+    )
     vector_grads = (
         query_bias_grad,
         value_bias_grad,
@@ -927,10 +1381,51 @@
         second_gain_grad,
         second_shift_grad,
     )
-    small_grads = jnp.concatenate(vector_grads + (inner_bias_grad, square_sums))
-    small_sums = lax.psum(small_grads, ("ctx", "wsh"))
+    small_grads = jnp.concatenate(
+        [vector.reshape(groups, 1, part) for vector in vector_grads]
+        + [
+            inner_bias_grad.reshape(groups, inner_parts, part),
+            jnp.broadcast_to(
+                jnp.pad(square_sums, (0, part - 2)).reshape(1, 1, part), (groups, 1, part)
+            ),
+        ],
+        axis=1,
+    )
+    small_grads = jnp.pad(
+        small_grads, ((0, 0), (0, (-small_grads.shape[1]) % 8), (0, (-part) % 128))
+    )
+    chained = count == 8
+    back, rim, glob, small_sums, *chain_sums = return_grads(
+        far_grad, small_grads, weight_grads if chained else (), count, capacity
+    )
+    near_grad = (
+        stream_grad
+        + back_product(dq, full_query)
+        + back_product(dk[:length], full_key)
+        + back_product(dv[:length], full_value)
+    ).reshape(blocks_here, BLK, features)
+    tokens_grad = unpack_grads(near_grad, back, rim, glob, picked, filled, edge)
+
+    if chained:
+        units = chain_sums[0].reshape(-1, part, features).astype(jnp.float32)
+        across = full_inner.shape[1] // features
+        sums = [units[i] for i in range(4)] + [
+            jnp.concatenate([units[4 + i] for i in range(across)], axis=1),
+            units[4 + across :].reshape(-1, features),
+        ]
+    else:
+        sums = lax.psum(
+            tuple(
+                lax.psum_scatter(
+                    grad.reshape(-1, grad.shape[-1]), "wsh", scatter_dimension=0, tiled=True
+                )
+                for grad in weight_grads
+            ),
+            "ctx",
+        )
+        sums = [total.astype(jnp.float32) for total in sums]
     element_count = count * groups * length * features
-    stream_rms = jnp.sqrt(small_sums[-2:] / element_count)
+    stream_rms = jnp.sqrt(small_sums[8 + inner_parts, :2] / element_count)
     (
         query_bias_grad,
         value_bias_grad,
@@ -940,28 +1435,24 @@
         outer_bias_grad,
         second_gain_grad,
         second_shift_grad,
-    ) = (
-        lax.dynamic_slice_in_dim(small_sums, i * features + own_group * part, part)
-        for i in range(8)
-    )
-    inner_bias_grad = lax.dynamic_slice_in_dim(
-        small_sums, 8 * features + own_group * inner_parts * part, inner_parts * part
-    )
+    ) = (small_sums[i, :part] for i in range(8))
+    inner_bias_grad = small_sums[8 : 8 + inner_parts, :part].reshape(-1)
+    query_weight_sum, key_weight_sum, value_weight_sum, output_weight_sum = sums[:4]
     return (
         final.astype(jnp.bfloat16)[None],
         tokens_grad.reshape(1, length, features),
-        shared(query_weight_grad),
+        query_weight_sum,
         query_bias_grad,
-        shared(key_weight_grad),
-        shared(value_weight_grad),
+        key_weight_sum,
+        value_weight_sum,
         value_bias_grad,
-        shared(output_weight_grad),
+        output_weight_sum,
         output_bias_grad,
         first_gain_grad,
         first_shift_grad,
-        shared(inner_weight_grad),
+        sums[4],
         inner_bias_grad,
-        shared(outer_weight_grad),
+        sums[5],
         outer_bias_grad,
         second_gain_grad,
         second_shift_grad,

time: 887 us -> 635 us (0.72)
  waiting for transfers between devices: 168 us -> 0 us
  blocking collectives: 68.9 us -> 0 us
  between operations: 15.1 us -> 1.74 us
  matrix products: 168 us -> 156 us
  local copies, waits for them, and re-layouts: 41.3 us -> 53.3 us
    reduce_scatter x5 -> x0, waiting for transfers between devices: 153 us -> none  [shared(): lax.psum_scatter(grad.astype(jnp.bfloat16), 'wsh', scatter_dimension=0, t...]
    psum x1 -> x0, blocking collectives: 68.9 us -> none  [shards(): small_sums = lax.psum(small_grads, ('ctx', 'wsh'))]
    pallas_call x1, Pallas kernels: 133 us -> 195 us  [return_grads(): pl.pallas_call(functools.partial(return_kernel, count, capacity, len(grad...]
    pallas_call x1, Pallas kernels: 169 us -> 111 us  [spread(): pl.pallas_call(functools.partial(spread_kernel, count, capacity), out_sha...]
    psum x1 -> x0, waiting for transfers between devices: 15.2 us -> none  [shared(): return lax.psum(scattered, 'ctx').astype(jnp.float32)]
    unnamed x88 -> x115, local copies, waits for them, and re-layouts: 12.2 us -> 25.7 us
    dot_general x6, matrix products: 48 us -> 38.9 us  [outer_product(): jnp.einsum('ta,tb->ab', left, right, preferred_element_type=jnp.float32)]
  transfers between devices with their start and end apart: 7 -> 0, of which waited for: 5 -> 0; matrix products, arithmetic and copies ran while one was open for 11% -> 0% of each run, Pallas kernels for 15% -> 0%
where the time goes in v2:
time: 635 us; the launch traced here: 632 us
  Pallas kernels  400 us (63%)
  matrix products  156 us (25%)
  local copies, waits for them, and re-layouts  53.3 us (8%)
  other arithmetic  20.6 us (3%)
    pallas_call x1, Pallas kernels, return_grads(): pl.pallas_call(functools.partial(return_kernel, count, capacity, len(grad...  195 us
    pallas_call x1, Pallas kernels, spread(): pl.pallas_call(functools.partial(spread_kernel, count, capacity), out_sha...  111 us
    dot_general x8, matrix products, back_product(): jnp.einsum('tb,ab->ta', upstream, weight, preferred_element_type=jnp.floa...  52.5 us
    pallas_call x1, Pallas kernels, attend_back(): pl.pallas_call(backward_kernel, out_shape=[jax.ShapeDtypeStruct(queries.s...  44.6 us
    pallas_call x1, Pallas kernels, attend(): pl.pallas_call(forward_kernel, out_shape=[jax.ShapeDtypeStruct(queries.sh...  40 us
    dot_general x6, matrix products, outer_product(): jnp.einsum('ta,tb->ab', left, right, preferred_element_type=jnp.float32)  38.9 us
    dot_general x1, matrix products, shards(): jnp.dot(normed_bf, full_inner, preferred_element_type=jnp.float32)  34.6 us
    unnamed x115, local copies, waits for them, and re-layouts  25.7 us

profile of v2, /device:TPU:0, one launch (start us, length us, event | category | flops | bytes accessed | tf_op | source)
XLA Modules:
  0.0 632.0 jit_solution(4664843883697456922)
XLA Ops:
  11.9 5.6 pack_blocks.1
  23.6 111.4 %spread_rows.1 = (bf16[68,64,768]{2,1,0:T(8,128)(2,1)S(1)}, bf16[2,8,64,768]{3,2,1,0:T(8,128)(2,1)}, bf16[4,192,768]{2,1,0:T(8,128)(2,1)S(1)}, bf16[4,192,768]{2...) custom-call(bf16[8,8,64,768]{3,2,1,0:T(8,128)(2,1)S(1)} %bitcast.126, ...), custom_call_target="tpu_custom_call" | custom-call | flops 109999996928 | bytes 110000000 | tf_op jit(solution)/shard_map/spread_rows/pallas_call | solution.py:394
  148.8 3.9 fusion.33
  154.4 9.7 %add_convert_fusion = bf16[4352,768]{1,0:T(8,128)(2,1)} fusion(bf16[4352,768]{1,0:T(8,128)(2,1)} %bitcast.136, bf16[768,768]{1,0:T(8,128)(2,1)} %bitcast.133, f32[768]{0:T(1024)S(1)} %reshape.502), kind=kOutput, calls=%fused_computation.3 | convolution fusion | flops 5140512768 | bytes 14552064 | tf_op jit(solution)/shard_map/dot_general | solution.py:1299
  164.1 8.7 %convolution_convert_fusion = bf16[4352,768]{1,0:T(8,128)(2,1)S(1)} fusion(bf16[4352,768]{1,0:T(8,128)(2,1)} %bitcast.137, bf16[768,768]{1,0:T(8,128)(2,1)S(1)} %bitcast.155), kind=kOutput, calls=%fused_computation.30 | convolution fusion | flops 5137170432 | bytes 14548992 | tf_op jit(solution)/shard_map/dot_general | solution.py:1297
  172.8 40.0 %attend.1 = (bf16[16,64,768]{2,1,0:T(8,128)(2,1)S(1)}, f32[16,1,768]{2,1,0:T(1,128)S(1)}) custom-call(s32[128]{0:T(128)S(1)} %reshape.456.index_ref, s32[2]{0:T(128)S(1)} %add_convert_fusion.4.edge_ref, bf16[16,64,768]{2,1,0:T(8,128)(2,1)S(1)} %bitcast.127, bf16[68,64,768]{2,1,0:T(8,128)(2,1)S(1)} %bitcast.140, bf16[68,64,768]{2,1,0:T(8,128)(2,1)} %bitcast.194), custom_call_target="tpu_custom_call" | custom-call | flops 36999999488 | bytes 37000000 | tf_op jit(solution)/shard_map/attend/pallas_call | solution.py:1060
  215.9 34.6 %fusion.2 = (bf16[1024,3072]{1,0:T(8,128)(2,1)S(1)}, f32[1024,3072]{1,0:T(8,128)}) fusion(f32[3072]{0:T(1024)S(1)} %reshape.506, bf16[768,3072]{1,0:T(8,128)(2,1)S(1)} %bitcast.144, f32[1024,768]{1,0:T(8,128)S(1)} %get-tuple-element.75, f32[768]{0:T(1024)S(1)} %reshape.505, f32[768]{0:T(1024)S(1)} %reshape.504, f32[1024]{0:T(1024)S(1)} %add_rsqrt_fusion.1, ...), kind=kOutput, calls=%fused_computation.6 | convolution fusion | flops 5043388416 | bytes 26765312 | tf_op jit(solution)/shard_map/dot_general | solution.py:1315
  250.6 5.5 fusion.53
  260.2 3.8 convert_reduce_fusion.3
  264.1 11.9 %convert_reduce_fusion.1 = (f32[3072]{0:T(1024)S(1)}, bf16[1024,3072]{1,0:T(8,128)(2,1)S(1)}) fusion(f32[1024,3072]{1,0:T(8,128)} %get-tuple-element.97, f32[3072]{0:T(1024)S(1)} %reshape.506, bf16[3072,768]{1,0:T(8,128)(2,1)} %bitcast.148, f32[1024,768]{1,0:T(8,128)S(1)} %get-tuple-element.71), kind=kOutput, calls=%fused_computation.13 | convolution fusion | flops 4873516032 | bytes 26763264 | tf_op jit(solution)/shard_map/tb,ab->ta/dot_general | solution.py:1193
  276.0 12.5 %convolution_convert_fusion.1 = bf16[3072,768]{1,0:T(8,128)(2,1)} fusion(bf16[1024,3072]{1,0:T(8,128)(2,1)} %copy-done.42, f32[1024,768]{1,0:T(8,128)S(1)} %get-tuple-element.71), kind=kOutput, calls=%fused_computation.31 | convolution fusion | flops 4834983936 | bytes 14155776 | tf_op jit(solution)/shard_map/ta,tb->ab/dot_general | solution.py:1189
  288.5 8.5 %multiply_reduce_fusion.2 = (f32[768]{0:T(1024)S(1)}, f32[1024]{0:T(1024)S(1)}, f32[1024]{0:T(1024)S(1)}, f32[]{:T(128)}, f32[768]{0:T(1024)S(1)}, /*index=5*/f32[1024,768]{1,0:T(8,128)}) fusion(f32[1024,768]{1,0:T(8,128)S(1)} %copy-done.32, f32[1024]{0:T(1024)S(1)} %add_rsqrt_fusion.1, f32[1024]{0:T(1024)S(1)} %broadcast_multiply_fusion.5, ...), kind=kOutput, calls=%fused_computation.47 | convolution fusion | flops 4841271296 | bytes 20472836 | tf_op jit(solution)/shard_map/tb,ab->ta/dot_general | solution.py:1193
  298.6 3.5 convert_reduce_fusion.4
  304.2 7.8 %convolution_convert_fusion.2 = bf16[768,3072]{1,0:T(8,128)(2,1)} fusion(bf16[1024,3072]{1,0:T(8,128)(2,1)S(1)} %copy-done.41, f32[1024,768]{1,0:T(8,128)S(1)} %copy-done.33, f32[768]{0:T(1024)S(1)} %reshape.505, f32[768]{0:T(1024)S(1)} %reshape.504, f32[1024]{0:T(1024)S(1)} %add_rsqrt_fusion.1, f32[1024]{0:T(1024)S(1)} %broadcast_multiply_fusion.5), kind=kOutput, calls=%fused_computation.32 | convolution fusion | flops 4838129664 | bytes 14170112 | tf_op jit(solution)/shard_map/ta,tb->ab/dot_general | solution.py:1189
  314.7 3.3 convolution_convert_fusion.3
  318.1 44.6 %attend_back.1 = (bf16[16,64,768]{2,1,0:T(8,128)(2,1)S(1)}, bf16[68,64,768]{2,1,0:T(8,128)(2,1)}, bf16[68,64,768]{2,1,0:T(8,128)(2,1)}) custom-call(s32[128]{0:T(128)S(1)} %reshape.456.index_ref, s32[2]{0:T(128)S(1)} %add_convert_fusion.4.edge_ref, bf16[16,64,768]{2,1,0:T(8,128)(2,1)S(1)} %bitcast.128, bf16[16,64,768]{2,1,0:T(8,128)(2,1)S(1)} %bitcast.154, ...), custom_call_target="tpu_custom_call" | custom-call | flops 44000002048 | bytes 44000000 | tf_op jit(solution)/shard_map/attend_back/pallas_call | solution.py:1142
  363.1 4.2 convert_reduce_fusion
  372.1 8.7 %bitcast_convert_fusion.1 = bf16[768,768]{1,0:T(8,128)(2,1)S(1)} fusion(bf16[68,64,768]{2,1,0:T(8,128)(2,1)S(1)} %bitcast.139, bf16[68,64,768]{2,1,0:T(8,128)(2,1)} %get-tuple-element.47), kind=kOutput, calls=%fused_computation.66 | convolution fusion | flops 5134417920 | bytes 14548992 | tf_op jit(solution)/shard_map/ta,tb->ab/dot_general | solution.py:1189
  380.8 6.0 bitcast_convert_fusion
  388.4 5.5 slice.130
  401.2 4.6 add_add_fusion
  405.8 9.4 %fusion.56 = f32[3328,768]{1,0:T(8,128)} fusion(bf16[3328,768]{1,0:T(8,128)(2,1)} %bitcast.171, bf16[768,768]{1,0:T(8,128)(2,1)S(1)} %bitcast.157), kind=kOutput, calls=%fused_computation.129 | convolution fusion | flops 3925868544 | bytes 16515072 | tf_op jit(solution)/shard_map/tb,ab->ta/dot_general | solution.py:1193
  415.1 8.5 %add_convert_fusion.1 = bf16[3328,768]{1,0:T(8,128)(2,1)} fusion(f32[3328,768]{1,0:T(8,128)} %fusion.56, bf16[3328,768]{1,0:T(8,128)(2,1)S(1)} %bitcast.174, bf16[768,768]{1,0:T(8,128)(2,1)S(1)} %bitcast.135), kind=kOutput, calls=%fused_computation.29 | convolution fusion | flops 3930980352 | bytes 21626880 | tf_op jit(solution)/shard_map/tb,ab->ta/dot_general | solution.py:1193
  423.7 195.4 %return_grads.1 = (bf16[8,8,64,768]{3,2,1,0:T(8,128)(2,1)}, bf16[2,64,768]{2,1,0:T(8,128)(2,1)S(1)}, bf16[8,64,768]{2,1,0:T(8,128)(2,1)S(1)}, f32[16,256]{1,0:T(8,128)S(1)}, bf16[12,2,96,768]{3,2,1,0:T(8,128)(2,1)}) custom-call(bf16[52,64,768]{2,1,0:T(8,128)(2,1)} %bitcast.196, f32[4,16,256]{2,1,0:T(8,128)S(1)} %pad.14.small, ...), custom_call_target="tpu_custom_call" | custom-call | flops 149999992832 | bytes 150000000 | tf_op jit(solution)/shard_map/return_grads/pallas_call | solution.py:895
  (206 shorter events, 72.5 us)
Async XLA Ops:
  11.9 5.7 copy-start.2
  11.9 5.7 copy-start.7
  11.9 5.7 copy-start.9
  11.9 5.7 copy-start.10
  154.4 9.7 %copy-start.20 = (bf16[4,192,768]{2,1,0:T(8,128)(2,1)S(1)}, bf16[4,192,768]{2,1,0:T(8,128)(2,1)}, u32[]{:S(2)}) copy-start(bf16[4,192,768]{2,1,0:T(8,128)(2,1)} %copy-done.19) | copy-start | bytes 3538948
  172.8 40.1 %copy-start.14 = (bf16[4352,768]{1,0:T(8,128)(2,1)}, bf16[4352,768]{1,0:T(8,128)(2,1)S(1)}, u32[]{:S(2)}) copy-start(bf16[4352,768]{1,0:T(8,128)(2,1)S(1)} %convolution_convert_fusion) | copy-start | bytes 20054020
  172.8 40.1 %copy-start.25 = (bf16[4,192,768]{2,1,0:T(8,128)(2,1)S(1)}, bf16[4,192,768]{2,1,0:T(8,128)(2,1)}, u32[]{:S(2)}) copy-start(bf16[4,192,768]{2,1,0:T(8,128)(2,1)} %copy-done.24) | copy-start | bytes 3538948
  212.9 37.7 %slice-start.6 = ((s8[4718592]{0:T(1024)(128)(4,1)}), s8[4194304]{0:T(1024)(128)(4,1)S(1)}, s32[]{:S(2)}) async-start(s8[4718592]{0:T(1024)(128)(4,1)} %bitcast.149), calls=%async_computation.6 | async-start | bytes 8388608
  215.3 35.2 %copy-start.31 = (f32[1024,768]{1,0:T(8,128)}, f32[1024,768]{1,0:T(8,128)S(1)}, u32[]{:S(2)}) copy-start(f32[1024,768]{1,0:T(8,128)S(1)} %get-tuple-element.75) | copy-start | bytes 9437188
  215.9 34.7 %slice-start.7 = ((s8[4718592]{0:T(1024)(128)(4,1)}), s8[524288]{0:T(1024)(128)(4,1)S(1)}, s32[]{:S(2)}) async-start(s8[4718592]{0:T(1024)(128)(4,1)} %bitcast.149), calls=%async_computation.7 | async-start | bytes 1048576
  215.9 34.7 %copy-start.39 = (f32[768]{0:T(1024)S(1)}, f32[768]{0:T(1024)}, u32[]{:S(2)}) copy-start(f32[768]{0:T(1024)} %reshape.507) | copy-start | bytes 9220
  260.2 28.2 %slice-start.4 = ((s8[4718592]{0:T(1024)(128)(4,1)}), s8[4194304]{0:T(1024)(128)(4,1)S(1)}, s32[]{:S(2)}) async-start(s8[4718592]{0:T(1024)(128)(4,1)} %bitcast.145), calls=%async_computation.4 | async-start | bytes 8388608
  264.1 24.4 %slice-start.5 = ((s8[4718592]{0:T(1024)(128)(4,1)}), s8[524288]{0:T(1024)(128)(4,1)S(1)}, s32[]{:S(2)}) async-start(s8[4718592]{0:T(1024)(128)(4,1)} %bitcast.145), calls=%async_computation.5 | async-start | bytes 1048576
  275.9 12.5 %copy-start.40 = (bf16[1024,3072]{1,0:T(8,128)(2,1)}, bf16[1024,3072]{1,0:T(8,128)(2,1)S(1)}, u32[]{:S(2)}) copy-start(bf16[1024,3072]{1,0:T(8,128)(2,1)S(1)} %get-tuple-element.102) | copy-start | bytes 18874372
  276.0 12.5 %copy-start.32 = (f32[1024,768]{1,0:T(8,128)S(1)}, f32[1024,768]{1,0:T(8,128)}, u32[]{:S(2)}) copy-start(f32[1024,768]{1,0:T(8,128)} %copy-done.31) | copy-start | bytes 9437188
  304.2 7.8 %copy-start.34 = (f32[1024,768]{1,0:T(8,128)}, f32[1024,768]{1,0:T(8,128)S(1)}, u32[]{:S(2)}) copy-start(f32[1024,768]{1,0:T(8,128)S(1)} %get-tuple-element.73) | copy-start | bytes 9437188
  304.2 7.8 %copy-start.18 = (bf16[16,64,768]{2,1,0:T(8,128)(2,1)S(1)}, bf16[16,64,768]{2,1,0:T(8,128)(2,1)}, u32[]{:S(2)}) copy-start(bf16[16,64,768]{2,1,0:T(8,128)(2,1)} %copy-done.17) | copy-start | bytes 4718596
  369.0 11.8 %slice-start.8 = ((s8[6684672]{0:T(1024)(128)(4,1)}), s8[4194304]{0:T(1024)(128)(4,1)S(1)}, s32[]{:S(2)}) async-start(s8[6684672]{0:T(1024)(128)(4,1)} %bitcast.166), calls=%async_computation.8 | async-start | bytes 8388608
  372.1 8.7 %slice-start.9 = ((s8[6684672]{0:T(1024)(128)(4,1)}), s8[2490368]{0:T(1024)(128)(4,1)S(1)}, s32[]{:S(2)}) async-start(s8[6684672]{0:T(1024)(128)(4,1)} %bitcast.166), calls=%async_computation.9 | async-start | bytes 4980736
  388.4 8.8 %slice-start.10 = ((s8[6684672]{0:T(1024)(128)(4,1)}), s8[4194304]{0:T(1024)(128)(4,1)S(1)}, s32[]{:S(2)}) async-start(s8[6684672]{0:T(1024)(128)(4,1)} %bitcast.168), calls=%async_computation.10 | async-start | bytes 8388608
  401.2 14.0 %slice-start.12 = ((s8[5111808]{0:T(1024)(128)(4,1)}), s8[917504]{0:T(1024)(128)(4,1)S(1)}, s32[]{:S(2)}) async-start(s8[5111808]{0:T(1024)(128)(4,1)} %bitcast.172), calls=%async_computation.12 | async-start | bytes 1835008
  405.8 9.4 %slice-start.13 = ((s8[5111808]{0:T(1024)(128)(4,1)}), s8[4194304]{0:T(1024)(128)(4,1)S(1)}, s32[]{:S(2)}) async-start(s8[5111808]{0:T(1024)(128)(4,1)} %bitcast.172), calls=%async_computation.13 | async-start | bytes 8388608
  415.1 8.5 %copy-start.27 = (bf16[768,768]{1,0:T(8,128)(2,1)S(1)}, bf16[768,768]{1,0:T(8,128)(2,1)}, u32[]{:S(2)}) copy-start(bf16[768,768]{1,0:T(8,128)(2,1)} %convolution_convert_fusion.4) | copy-start | bytes 3538948
  423.7 195.4 %copy-start.6 = (s32[64]{0:T(128)S(1)}, s32[64]{0:T(128)}, u32[]{:S(2)}) copy-start(s32[64]{0:T(128)} %reshape.457.picked_ref) | copy-start | bytes 772
  (33 other events, 97.3 us)

commit v3 on v2

--- a/solution.py
+++ b/solution.py
@@ -19,6 +19,8 @@
 NEG_FILL = -1e30
 MESH = pl.DeviceIdType.MESH
 MIB = 1 << 20
+MID_ROWS = 256
+MID_CHUNK = 768
 
 
 def lasting(microseconds):
@@ -418,7 +420,7 @@
             pltpu.VMEM(rows.shape, rows.dtype),
         ],
         compiler_params=pltpu.CompilerParams(
-            collective_id=0, has_side_effects=True, vmem_limit_bytes=16 * MIB
+            collective_id=0, has_side_effects=True, vmem_limit_bytes=56 * MIB
         ),
         cost_estimate=lasting(110),
         name="spread_rows",
@@ -922,7 +924,7 @@
         ]
         + sum_scratch,
         compiler_params=pltpu.CompilerParams(
-            collective_id=1, has_side_effects=True, vmem_limit_bytes=48 * MIB
+            collective_id=1, has_side_effects=True, vmem_limit_bytes=56 * MIB
         ),
         cost_estimate=lasting(150),
         name="return_grads",
@@ -1171,18 +1173,153 @@
 
 def norm_back(upstream, normal, inverse, gain):
     scaled = upstream * gain
-    hidden_grad = inverse * (
+    return inverse * (
         scaled
         - jnp.mean(scaled, axis=-1, keepdims=True)
         - normal * jnp.mean(scaled * normal, axis=-1, keepdims=True)
     )
-    return (hidden_grad, jnp.sum(upstream * normal, axis=0), jnp.sum(upstream, axis=0))
-
-
-def gelu_slope(inner):
-    cumulative = 0.5 * (1.0 + jax.scipy.special.erf(inner * (1.0 / math.sqrt(2.0))))
-    density = jnp.exp(-0.5 * inner * inner) * (1.0 / math.sqrt(2.0 * math.pi))
-    return cumulative + inner * density
+
+
+def erf_f32(x):
+    return lax.erf(x)
+
+
+def mid_kernel(
+    chunk,
+    mixed_ref,
+    rows_ref,
+    cot_ref,
+    vec_ref,
+    inner_bias_ref,
+    wo_ref,
+    w1_ref,
+    w2_ref,
+    final_ref,
+    stream_grad_ref,
+    mixed_grad_ref,
+    normed_ref,
+    act_ref,
+    outer_grad_ref,
+    inner_grad_ref,
+    att_grad_ref,
+    sums_ref,
+    inner_sums_ref,
+    slope,
+):
+    @pl.when(pl.program_id(0) == 0)
+    def _():
+        sums_ref[...] = jnp.zeros_like(sums_ref)
+        inner_sums_ref[...] = jnp.zeros_like(inner_sums_ref)
+
+    def vector(i):
+        return vec_ref[i : i + 1]
+
+    def tally(i, value):
+        sums_ref[i : i + 1] += jnp.sum(value, axis=0, keepdims=True)
+
+    hidden = w1_ref.shape[1]
+    pieces = [slice(at, at + chunk) for at in range(0, hidden, chunk)]
+    attention = nn(mixed_ref[...], wo_ref[...]) + vector(2)
+    stream = rows_ref[...].astype(jnp.float32) + attention
+    tally(6, stream * stream)
+    tally(7, attention * attention)
+    first_gain = vector(3)
+    normed, first_normal, first_inverse = layer_norm(stream, first_gain, vector(4))
+    normed_bf = normed.astype(jnp.bfloat16)
+    normed_ref[...] = normed_bf
+    outer = jnp.zeros_like(normed)
+    for piece in pieces:
+        inner = nn(normed_bf, w1_ref[:, piece]) + inner_bias_ref[:, piece]
+        cumulative = 0.5 * (1.0 + erf_f32(inner * (1.0 / math.sqrt(2.0))))
+        density = jnp.exp(-0.5 * inner * inner) * (1.0 / math.sqrt(2.0 * math.pi))
+        slope[:, piece] = cumulative + inner * density
+        active = (inner * cumulative).astype(jnp.bfloat16)
+        act_ref[:, piece] = active
+        outer = outer + nn(active, w2_ref[piece])
+    second_gain = vector(6)
+    final, second_normal, second_inverse = layer_norm(
+        normed + (outer + vector(5)), second_gain, vector(7)
+    )
+    final_ref[...] = final.astype(final_ref.dtype)
+    upstream = cot_ref[...].astype(jnp.float32)
+    tally(4, upstream * second_normal)
+    tally(5, upstream)
+    second_grad = norm_back(upstream, second_normal, second_inverse, second_gain)
+    outer_grad = second_grad.astype(jnp.bfloat16)
+    outer_grad_ref[...] = outer_grad
+    tally(3, outer_grad.astype(jnp.float32))
+    normed_grad = second_grad
+    for piece in pieces:
+        inner_grad = (nt(outer_grad, w2_ref[piece]) * slope[:, piece]).astype(jnp.bfloat16)
+        inner_grad_ref[:, piece] = inner_grad
+        inner_sums_ref[:, piece] += jnp.sum(
+            inner_grad.astype(jnp.float32), axis=0, keepdims=True
+        )
+        normed_grad = normed_grad + nt(inner_grad, w1_ref[:, piece])
+    tally(1, normed_grad * first_normal)
+    tally(2, normed_grad)
+    stream_grad = norm_back(normed_grad, first_normal, first_inverse, first_gain)
+    stream_grad_ref[...] = stream_grad
+    att_grad = stream_grad.astype(jnp.bfloat16)
+    att_grad_ref[...] = att_grad
+    tally(0, att_grad.astype(jnp.float32))
+    mixed_grad_ref[...] = nt(att_grad, wo_ref[...]).astype(jnp.bfloat16)
+
+
+def middle(mixed, rows, cotangent, vectors, inner_bias, wo, w1, w2):
+    length, features = rows.shape
+    hidden = w1.shape[1]
+    block = min(MID_ROWS, length)
+    by_row = pl.BlockSpec((block, features), lambda i: (i, 0))
+    wide = pl.BlockSpec((block, hidden), lambda i: (i, 0))
+
+    def whole(array):
+        return pl.BlockSpec(array.shape, lambda i: (0, 0), pipeline_mode=pl.Buffered(1))
+
+    narrow_bf = jax.ShapeDtypeStruct((length, features), jnp.bfloat16)
+    wide_bf = jax.ShapeDtypeStruct((length, hidden), jnp.bfloat16)
+    return pl.pallas_call(
+        functools.partial(mid_kernel, MID_CHUNK),
+        grid=(length // block,),
+        out_shape=[
+            narrow_bf,
+            jax.ShapeDtypeStruct((length, features), jnp.float32),
+            narrow_bf,
+            narrow_bf,
+            wide_bf,
+            narrow_bf,
+            wide_bf,
+            narrow_bf,
+            jax.ShapeDtypeStruct((8, features), jnp.float32),
+            jax.ShapeDtypeStruct((1, hidden), jnp.float32),
+        ],
+        in_specs=[
+            by_row,
+            by_row,
+            by_row,
+            whole(vectors),
+            whole(inner_bias),
+            whole(wo),
+            whole(w1),
+            whole(w2),
+        ],
+        out_specs=[
+            by_row,
+            by_row,
+            by_row,
+            by_row,
+            wide,
+            by_row,
+            wide,
+            by_row,
+            pl.BlockSpec((8, features), lambda i: (0, 0)),
+            pl.BlockSpec((1, hidden), lambda i: (0, 0)),
+        ],
+        scratch_shapes=[pltpu.VMEM((block, hidden), jnp.float32)],
+        compiler_params=pltpu.CompilerParams(vmem_limit_bytes=56 * MIB),
+        cost_estimate=lasting(50),
+        name="middle",
+    )(mixed, rows, cotangent, vectors, inner_bias, wo, w1, w2)
 
 
 def outer_product(left, right):
@@ -1228,23 +1365,19 @@
     inner_parts = inner_bias.shape[0] // part
 
     small = jnp.concatenate(
-        [
-            vector.reshape(-1, part)
-            for vector in (
-                query_bias,
-                value_bias,
-                output_bias,
-                first_gain,
-                first_shift,
-                outer_bias,
-                second_gain,
-                second_shift,
-                inner_bias,
-            )
-        ],
-        axis=0,
-    )
-    small = jnp.pad(small, ((0, (-small.shape[0]) % 16), (0, (-part) % 128)))
+        (
+            query_bias,
+            value_bias,
+            output_bias,
+            first_gain,
+            first_shift,
+            outer_bias,
+            second_gain,
+            second_shift,
+            inner_bias,
+        )
+    )
+    small = jnp.pad(small, (0, (-small.shape[0]) % 2048)).reshape(-1, 128)
 
     source, within, ranking = request_tables(random_blocks[0], count, blocks_here)
     filled, picked = send_slots(source, within, ranking, own_index, capacity)
@@ -1274,29 +1407,19 @@
     full_query, full_key, full_value, full_output, full_inner, full_outer = (
         full.reshape(-1, full.shape[-1]) for full in fulls[:6]
     )
-    vectors = [fulls[6][:, i, :part].reshape(-1) for i in range(8)]
-    (
-        full_query_bias,
-        full_value_bias,
-        full_output_bias,
-        full_first_gain,
-        full_first_shift,
-        full_outer_bias,
-        full_second_gain,
-        full_second_shift,
-    ) = vectors
-    full_inner_bias = fulls[6][:, 8 : 8 + inner_parts, :part].reshape(-1)
-    first_gain_f = full_first_gain.astype(jnp.float32)
-    second_gain_f = full_second_gain.astype(jnp.float32)
+    gathered = fulls[6].reshape(groups, -1).astype(jnp.float32)
+    vectors = gathered[:, : 8 * part].reshape(groups, 8, part)
+    vectors = jnp.transpose(vectors, (1, 0, 2)).reshape(8, features)
+    full_inner_bias = gathered[:, 8 * part : (8 + inner_parts) * part].reshape(1, -1)
 
     slots = ext_rows.shape[0]
     ext_flat = ext_rows.reshape(slots * BLK, features)
     queries_bf = (
-        jnp.dot(token_rows, full_query, preferred_element_type=jnp.float32) + full_query_bias
+        jnp.dot(token_rows, full_query, preferred_element_type=jnp.float32) + vectors[0]
     ).astype(jnp.bfloat16)
     keys_bf = jnp.dot(ext_flat, full_key, preferred_element_type=jnp.float32).astype(jnp.bfloat16)
     values_bf = (
-        jnp.dot(ext_flat, full_value, preferred_element_type=jnp.float32) + full_value_bias
+        jnp.dot(ext_flat, full_value, preferred_element_type=jnp.float32) + vectors[1]
     ).astype(jnp.bfloat16)
     query_blocks = queries_bf.reshape(blocks_here, BLK, features)
     key_blocks = keys_bf.reshape(slots, BLK, features)
@@ -1304,42 +1427,31 @@
     mixed_blocks, log_total = attend(query_blocks, key_blocks, value_blocks, index, edge)
     mixed_bf = mixed_blocks.reshape(length, features)
 
-    attention = (
-        jnp.dot(mixed_bf, full_output, preferred_element_type=jnp.float32) + full_output_bias
-    )
-    stream = token_rows.astype(jnp.float32) + attention
-    normed, first_normal, first_inverse = layer_norm(
-        stream, first_gain_f, full_first_shift.astype(jnp.float32)
-    )
-    normed_bf = normed.astype(jnp.bfloat16)
-    inner = jnp.dot(normed_bf, full_inner, preferred_element_type=jnp.float32) + full_inner_bias
-    activated_bf = jax.nn.gelu(inner, approximate=False).astype(jnp.bfloat16)
-    outer = jnp.dot(activated_bf, full_outer, preferred_element_type=jnp.float32) + full_outer_bias
-    final, second_normal, second_inverse = layer_norm(
-        normed + outer, second_gain_f, full_second_shift.astype(jnp.float32)
-    )
-    square_sums = jnp.stack([jnp.sum(stream * stream), jnp.sum(attention * attention)])
-
-    output_grad = cotangent[0].astype(jnp.float32)
-    second_stream_grad, second_gain_grad, second_shift_grad = norm_back(
-        output_grad, second_normal, second_inverse, second_gain_f
-    )
-    outer_grad_bf = second_stream_grad.astype(jnp.bfloat16)
-    outer_bias_grad = column_sum(outer_grad_bf)
+    (
+        final,
+        stream_grad,
+        mixed_grad_bf,
+        normed_bf,
+        activated_bf,
+        outer_grad_bf,
+        inner_grad_bf,
+        attention_grad_bf,
+        middle_sums,
+        inner_bias_grad,
+    ) = middle(
+        mixed_bf,
+        token_rows,
+        cotangent[0],
+        vectors,
+        full_inner_bias,
+        full_output,
+        full_inner,
+        full_outer,
+    )
+    output_weight_grad = outer_product(mixed_bf, attention_grad_bf)
+    inner_weight_grad = outer_product(normed_bf, inner_grad_bf)
     outer_weight_grad = outer_product(activated_bf, outer_grad_bf)
-    inner_grad_bf = (back_product(outer_grad_bf, full_outer) * gelu_slope(inner)).astype(
-        jnp.bfloat16
-    )
-    inner_bias_grad = column_sum(inner_grad_bf)
-    inner_weight_grad = outer_product(normed_bf, inner_grad_bf)
-    normed_grad = second_stream_grad + back_product(inner_grad_bf, full_inner)
-    stream_grad, first_gain_grad, first_shift_grad = norm_back(
-        normed_grad, first_normal, first_inverse, first_gain_f
-    )
-    attention_grad_bf = stream_grad.astype(jnp.bfloat16)
-    output_bias_grad = column_sum(attention_grad_bf)
-    output_weight_grad = outer_product(mixed_bf, attention_grad_bf)
-    mixed_grad_bf = back_product(attention_grad_bf, full_output).astype(jnp.bfloat16)
+    square_sums = jnp.sum(middle_sums[6:8], axis=1)
 
     dq_blocks, dk_blocks, dv_blocks = attend_back(
         query_blocks,
@@ -1371,19 +1483,12 @@
             outer_weight_grad,
         )
     )
-    vector_grads = (
-        query_bias_grad,
-        value_bias_grad,
-        output_bias_grad,
-        first_gain_grad,
-        first_shift_grad,
-        outer_bias_grad,
-        second_gain_grad,
-        second_shift_grad,
+    vector_grads = jnp.concatenate(
+        [query_bias_grad[None], value_bias_grad[None], middle_sums[:6]], axis=0
     )
     small_grads = jnp.concatenate(
-        [vector.reshape(groups, 1, part) for vector in vector_grads]
-        + [
+        [
+            jnp.transpose(vector_grads.reshape(8, groups, part), (1, 0, 2)),
             inner_bias_grad.reshape(groups, inner_parts, part),
             jnp.broadcast_to(
                 jnp.pad(square_sums, (0, part - 2)).reshape(1, 1, part), (groups, 1, part)
@@ -1439,7 +1544,7 @@
     inner_bias_grad = small_sums[8 : 8 + inner_parts, :part].reshape(-1)
     query_weight_sum, key_weight_sum, value_weight_sum, output_weight_sum = sums[:4]
     return (
-        final.astype(jnp.bfloat16)[None],
+        final[None],
         tokens_grad.reshape(1, length, features),
         query_weight_sum,
         query_bias_grad,

time: 635 us -> 569 us (0.90)
  matrix products: 156 us -> 79.7 us
  Pallas kernels: 400 us -> 437 us
  local copies, waits for them, and re-layouts: 53.3 us -> 32 us
  other arithmetic: 20.6 us -> 9.88 us
    dot_general x3 -> x0, matrix products: 42.5 us -> none  [the longest x1 34.6 us: shards(): jnp.dot(normed_bf, full_inner, preferred_element_type=jnp.float32)]
    pallas_call x0 -> x1, Pallas kernels: none -> 38.1 us  [middle(): pl.pallas_call(functools.partial(mid_kernel, MID_CHUNK), grid=(length //...]
    dot_general x8 -> x5, matrix products: 52.5 us -> 22.7 us  [back_product(): jnp.einsum('tb,ab->ta', upstream, weight, preferred_element_type=jnp.floa...]
    unnamed x115 -> x100, local copies, waits for them, and re-layouts: 25.7 us -> 12.4 us
    reduce_sum x4 -> x2, other arithmetic: 11.8 us -> 4.54 us  [column_sum(): return jnp.sum(upstream.astype(jnp.float32), axis=0)]
where the time goes in v3:
time: 569 us; the launch traced here: 560 us
  Pallas kernels  437 us (77%)
  matrix products  79.7 us (14%)
  local copies, waits for them, and re-layouts  32 us (6%)
  other arithmetic  9.88 us (2%)
    pallas_call x1, Pallas kernels, return_grads(): pl.pallas_call(functools.partial(return_kernel, count, capacity, len(grad...  196 us
    pallas_call x1, Pallas kernels, spread(): pl.pallas_call(functools.partial(spread_kernel, count, capacity), out_sha...  112 us
    pallas_call x1, Pallas kernels, attend_back(): pl.pallas_call(backward_kernel, out_shape=[jax.ShapeDtypeStruct(queries.s...  44.6 us
    pallas_call x1, Pallas kernels, middle(): pl.pallas_call(functools.partial(mid_kernel, MID_CHUNK), grid=(length //...  38.1 us
    pallas_call x1, Pallas kernels, attend(): pl.pallas_call(forward_kernel, out_shape=[jax.ShapeDtypeStruct(queries.sh...  37.6 us
    dot_general x6, matrix products, outer_product(): jnp.einsum('ta,tb->ab', left, right, preferred_element_type=jnp.float32)  36.6 us
    dot_general x5, matrix products, back_product(): jnp.einsum('tb,ab->ta', upstream, weight, preferred_element_type=jnp.floa...  22.7 us
    unnamed x100, local copies, waits for them, and re-layouts  12.4 us

profile of v3, /device:TPU:0, one launch (start us, length us, event | category | flops | bytes accessed | tf_op | source)
XLA Modules:
  0.0 560.0 jit_solution(5236250417189185177)
XLA Ops:
  2.8 5.4 pack_blocks.1
  9.0 111.7 %spread_rows.1 = (bf16[68,64,768]{2,1,0:T(8,128)(2,1)}, bf16[2,8,64,768]{3,2,1,0:T(8,128)(2,1)}, bf16[4,192,768]{2,1,0:T(8,128)(2,1)}, bf16[4,192,768]{2,1,0:T(8...) custom-call(bf16[8,8,64,768]{3,2,1,0:T(8,128)(2,1)} %bitcast.122, ...), custom_call_target="tpu_custom_call" | custom-call | flops 109999996928 | bytes 110000000 | tf_op jit(solution)/shard_map/spread_rows/pallas_call | solution.py:396
  121.8 10.2 %add_convert_fusion = bf16[4352,768]{1,0:T(8,128)(2,1)} fusion(bf16[4352,768]{1,0:T(8,128)(2,1)} %bitcast.157, bf16[768,768]{1,0:T(8,128)(2,1)} %bitcast.135, f32[768]{0:T(1024)S(1)} %add.112), kind=kOutput, calls=%fused_computation.1 | convolution fusion | flops 5140512768 | bytes 14552064 | tf_op jit(solution)/shard_map/dot_general | solution.py:1422
  132.0 7.4 %convolution_convert_fusion = bf16[4352,768]{1,0:T(8,128)(2,1)} fusion(bf16[4352,768]{1,0:T(8,128)(2,1)S(1)} %bitcast.158, bf16[768,768]{1,0:T(8,128)(2,1)S(1)} %bitcast.169), kind=kOutput, calls=%fused_computation.3 | convolution fusion | flops 5137170432 | bytes 14548992 | tf_op jit(solution)/shard_map/dot_general | solution.py:1420
  139.5 2.8 fusion
  143.4 2.9 copy-done.8
  146.3 37.6 %attend.1 = (bf16[16,64,768]{2,1,0:T(8,128)(2,1)S(1)}, f32[16,1,768]{2,1,0:T(1,128)S(1)}) custom-call(s32[128]{0:T(128)S(1)} %reshape.325.index_ref, s32[2]{0:T(128)S(1)} %add_convert_fusion.3.edge_ref, bf16[16,64,768]{2,1,0:T(8,128)(2,1)S(1)} %bitcast.110, bf16[68,64,768]{2,1,0:T(8,128)(2,1)S(1)} %bitcast.113, bf16[68,64,768]{2,1,0:T(8,128)(2,1)} %bitcast.161), custom_call_target="tpu_custom_call" | custom-call | flops 36999999488 | bytes 37000000 | tf_op jit(solution)/shard_map/attend/pallas_call | solution.py:1062
  186.4 38.1 %middle.1 = (bf16[1024,768]{1,0:T(8,128)(2,1)}, f32[1024,768]{1,0:T(8,128)}, bf16[1024,768]{1,0:T(8,128)(2,1)}, bf16[1024,768]{1,0:T(8,128)(2,1)}, bf16[1024,307...) custom-call(bf16[1024,768]{1,0:T(8,128)(2,1)} %bitcast.114, ...), custom_call_target="tpu_custom_call" | custom-call | flops 49999998976 | bytes 50000000 | tf_op jit(solution)/shard_map/middle/pallas_call | solution.py:1281
  224.5 9.3 %convolution_convert_fusion.1 = bf16[3072,768]{1,0:T(8,128)(2,1)} fusion(bf16[1024,3072]{1,0:T(8,128)(2,1)} %get-tuple-element.67, bf16[1024,768]{1,0:T(8,128)(2,1)} %get-tuple-element.68), kind=kOutput, calls=%fused_computation.4 | convolution fusion | flops 4834197504 | bytes 12582912 | tf_op jit(solution)/shard_map/ta,tb->ab/dot_general | solution.py:1326
  233.8 6.8 %convolution_convert_fusion.2 = bf16[768,3072]{1,0:T(8,128)(2,1)} fusion(bf16[1024,768]{1,0:T(8,128)(2,1)S(1)} %copy-done.41, bf16[1024,3072]{1,0:T(8,128)(2,1)S(1)} %copy-done.39), kind=kOutput, calls=%fused_computation.5 | convolution fusion | flops 4834197504 | bytes 12582912 | tf_op jit(solution)/shard_map/ta,tb->ab/dot_general | solution.py:1326
  240.6 44.6 %attend_back.1 = (bf16[16,64,768]{2,1,0:T(8,128)(2,1)S(1)}, bf16[68,64,768]{2,1,0:T(8,128)(2,1)}, bf16[68,64,768]{2,1,0:T(8,128)(2,1)}) custom-call(s32[128]{0:T(128)S(1)} %reshape.325.index_ref, s32[2]{0:T(128)S(1)} %add_convert_fusion.3.edge_ref, bf16[16,64,768]{2,1,0:T(8,128)(2,1)S(1)} %bitcast.111, bf16[16,64,768]{2,1,0:T(8,128)(2,1)S(1)} %bitcast.116, ...), custom_call_target="tpu_custom_call" | custom-call | flops 44000002048 | bytes 44000000 | tf_op jit(solution)/shard_map/attend_back/pallas_call | solution.py:1144
  285.6 4.3 convert_reduce_fusion
  292.2 2.9 slice.118
  295.1 6.9 %fusion.14 = f32[3328,768]{1,0:T(8,128)} fusion(bf16[3328,768]{1,0:T(8,128)(2,1)S(1)} %bitcast.124, bf16[768,768]{1,0:T(8,128)(2,1)S(1)} %bitcast.170), kind=kOutput, calls=%fused_computation.57 | convolution fusion | flops 3925868544 | bytes 16515072 | tf_op jit(solution)/shard_map/tb,ab->ta/dot_general | solution.py:1330
  302.1 2.9 slice.120
  305.0 11.5 %add_convert_fusion.1 = bf16[3328,768]{1,0:T(8,128)(2,1)} fusion(f32[3328,768]{1,0:T(8,128)} %fusion.14, bf16[3328,768]{1,0:T(8,128)(2,1)} %bitcast.123, bf16[768,768]{1,0:T(8,128)(2,1)S(1)} %bitcast.136), kind=kOutput, calls=%fused_computation.2 | convolution fusion | flops 3930980352 | bytes 21626880 | tf_op jit(solution)/shard_map/tb,ab->ta/dot_general | solution.py:1330
  316.5 2.5 convolution_convert_fusion.3
  319.1 8.9 %bitcast_convert_fusion.1 = bf16[768,768]{1,0:T(8,128)(2,1)} fusion(bf16[68,64,768]{2,1,0:T(8,128)(2,1)} %get-tuple-element.48, bf16[68,64,768]{2,1,0:T(8,128)(2,1)S(1)} %bitcast.120), kind=kOutput, calls=%fused_computation.11 | convolution fusion | flops 5134417920 | bytes 14548992 | tf_op jit(solution)/shard_map/ta,tb->ab/dot_general | solution.py:1326
  328.0 6.6 %bitcast_convert_fusion = bf16[768,768]{1,0:T(8,128)(2,1)} fusion(bf16[68,64,768]{2,1,0:T(8,128)(2,1)S(1)} %bitcast.160, bf16[68,64,768]{2,1,0:T(8,128)(2,1)S(1)} %bitcast.118), kind=kOutput, calls=%fused_computation.10 | convolution fusion | flops 5134417920 | bytes 14548992 | tf_op jit(solution)/shard_map/ta,tb->ab/dot_general | solution.py:1326
  334.6 2.5 convolution_convert_fusion.4
  337.1 196.2 %return_grads.1 = (bf16[8,8,64,768]{3,2,1,0:T(8,128)(2,1)}, bf16[2,64,768]{2,1,0:T(8,128)(2,1)}, bf16[8,64,768]{2,1,0:T(8,128)(2,1)}, f32[16,256]{1,0:T(8,128)}, bf16[12,2,96,768]{3,2,1,0:T(8,128)(2,1)}) custom-call(bf16[52,64,768]{2,1,0:T(8,128)(2,1)} %bitcast.163, f32[4,16,256]{2,1,0:T(8,128)} %select_maximum_fusion.small, bf16[4,192,768]{2,1,0:T(8,128)(2,1)} %bitcast.178, ...), custom_call_target="tpu_custom_call" | custom-call | flops 149999992832 | bytes 150000000 | tf_op jit(solution)/shard_map/return_grads/pallas_call | solution.py:897
  533.3 3.3 fusion.9
  550.8 2.8 copy-done
  554.7 3.0 unpack_grads.1
  (155 shorter events, 27.1 us)
Async XLA Ops:
  1.6 6.7 %copy-start.23 = (pred[8,48]{1,0:T(8,128)(4,1)}, pred[8,48]{1,0:T(8,128)(4,1)S(1)}, u32[]{:S(2)}) copy-start(pred[8,48]{1,0:T(8,128)(4,1)S(1)} %get-tuple-element.74) | copy-start | bytes 1156
  1.9 141.1 %copy-start.18 = (s32[8,48]{1,0:T(8,128)}, s32[8,48]{1,0:T(8,128)S(1)}, u32[]{:S(2)}) copy-start(s32[8,48]{1,0:T(8,128)S(1)} %convert_reduce_fusion.2) | copy-start | bytes 4612
  2.7 5.5 copy-start.28
  2.8 5.5 copy-start.29
  2.8 5.5 copy-start.30
  2.8 5.5 copy-start.31
  2.8 5.5 copy-start.32
  121.8 10.2 %copy-start.34 = (bf16[68,64,768]{2,1,0:T(8,128)(2,1)S(1)}, bf16[68,64,768]{2,1,0:T(8,128)(2,1)}, u32[]{:S(2)}) copy-start(bf16[68,64,768]{2,1,0:T(8,128)(2,1)} %get-tuple-element.48) | copy-start | bytes 20054020
  121.8 10.2 %copy-start.35 = (bf16[4,192,768]{2,1,0:T(8,128)(2,1)S(1)}, bf16[4,192,768]{2,1,0:T(8,128)(2,1)}, u32[]{:S(2)}) copy-start(bf16[4,192,768]{2,1,0:T(8,128)(2,1)} %get-tuple-element.49) | copy-start | bytes 3538948
  132.0 7.5 %copy-start.14 = (bf16[1,1024,768]{2,1,0:T(8,128)(2,1)S(1)}, bf16[1,1024,768]{2,1,0:T(8,128)(2,1)}, u32[]{:S(2)}) copy-start(bf16[1,1024,768]{2,1,0:T(8,128)(2,1)} %param.18) | copy-start | bytes 4718596
  146.3 94.3 %copy-start.6 = (s32[2]{0:T(128)}, s32[2]{0:T(128)S(1)}, u32[]{:S(2)}) copy-start(s32[2]{0:T(128)S(1)} %add_convert_fusion.3.edge_ref) | copy-start | bytes 28
  224.5 9.3 %copy-start.39 = (bf16[1024,3072]{1,0:T(8,128)(2,1)S(1)}, bf16[1024,3072]{1,0:T(8,128)(2,1)}, u32[]{:S(2)}) copy-start(bf16[1024,3072]{1,0:T(8,128)(2,1)} %get-tuple-element.66) | copy-start | bytes 18874372
  224.5 9.3 %copy-start.41 = (bf16[1024,768]{1,0:T(8,128)(2,1)S(1)}, bf16[1024,768]{1,0:T(8,128)(2,1)}, u32[]{:S(2)}) copy-start(bf16[1024,768]{1,0:T(8,128)(2,1)} %get-tuple-element.65) | copy-start | bytes 4718596
  233.8 6.8 %copy-start.11 = (bf16[1024,768]{1,0:T(8,128)(2,1)S(1)}, bf16[1024,768]{1,0:T(8,128)(2,1)}, u32[]{:S(2)}) copy-start(bf16[1024,768]{1,0:T(8,128)(2,1)} %get-tuple-element.57) | copy-start | bytes 4718596
  285.3 49.4 %copy-start.1 = (bf16[16,64,768]{2,1,0:T(8,128)(2,1)}, bf16[16,64,768]{2,1,0:T(8,128)(2,1)S(1)}, u32[]{:S(2)}) copy-start(bf16[16,64,768]{2,1,0:T(8,128)(2,1)S(1)} %get-tuple-element.59) | copy-start | bytes 4718596
  292.2 9.9 %slice-start = ((s8[6684672]{0:T(1024)(128)(4,1)}), s8[4194304]{0:T(1024)(128)(4,1)S(1)}, s32[]{:S(2)}) async-start(s8[6684672]{0:T(1024)(128)(4,1)} %bitcast.117), calls=%async_computation | async-start | bytes 8388608
  295.1 6.9 %slice-start.1 = ((s8[6684672]{0:T(1024)(128)(4,1)}), s8[2490368]{0:T(1024)(128)(4,1)S(1)}, s32[]{:S(2)}) async-start(s8[6684672]{0:T(1024)(128)(4,1)} %bitcast.117), calls=%async_computation.1 | async-start | bytes 4980736
  302.1 17.0 %slice-start.2 = ((s8[6684672]{0:T(1024)(128)(4,1)}), s8[4194304]{0:T(1024)(128)(4,1)S(1)}, s32[]{:S(2)}) async-start(s8[6684672]{0:T(1024)(128)(4,1)} %bitcast.119), calls=%async_computation.2 | async-start | bytes 8388608
  305.0 11.5 %copy-start.10 = (bf16[16,64,768]{2,1,0:T(8,128)(2,1)S(1)}, bf16[16,64,768]{2,1,0:T(8,128)(2,1)}, u32[]{:S(2)}) copy-start(bf16[16,64,768]{2,1,0:T(8,128)(2,1)} %copy-done.9) | copy-start | bytes 4718596
  305.0 11.5 %copy-start.40 = (bf16[1024,768]{1,0:T(8,128)(2,1)S(1)}, bf16[1024,768]{1,0:T(8,128)(2,1)}, u32[]{:S(2)}) copy-start(bf16[1024,768]{1,0:T(8,128)(2,1)} %get-tuple-element.64) | copy-start | bytes 4718596
  305.0 14.1 %slice-start.3 = ((s8[6684672]{0:T(1024)(128)(4,1)}), s8[2490368]{0:T(1024)(128)(4,1)S(1)}, s32[]{:S(2)}) async-start(s8[6684672]{0:T(1024)(128)(4,1)} %bitcast.119), calls=%async_computation.3 | async-start | bytes 4980736
  316.5 11.5 %slice-start.4 = ((s8[6684672]{0:T(1024)(128)(4,1)}), s8[4194304]{0:T(1024)(128)(4,1)S(1)}, s32[]{:S(2)}) async-start(s8[6684672]{0:T(1024)(128)(4,1)} %bitcast.159), calls=%async_computation.4 | async-start | bytes 8388608
  319.1 8.9 %slice-start.5 = ((s8[6684672]{0:T(1024)(128)(4,1)}), s8[2490368]{0:T(1024)(128)(4,1)S(1)}, s32[]{:S(2)}) async-start(s8[6684672]{0:T(1024)(128)(4,1)} %bitcast.159), calls=%async_computation.5 | async-start | bytes 4980736
  328.0 6.6 %copy-start.15 = (bf16[1,1024,768]{2,1,0:T(8,128)(2,1)S(1)}, bf16[1,1024,768]{2,1,0:T(8,128)(2,1)}, u32[]{:S(2)}) copy-start(bf16[1,1024,768]{2,1,0:T(8,128)(2,1)} %param.18) | copy-start | bytes 4718596
  (24 other events, 71.3 us)

commit v4 on v3

--- a/solution.py
+++ b/solution.py
@@ -21,6 +21,10 @@
 MIB = 1 << 20
 MID_ROWS = 256
 MID_CHUNK = 768
+GAP = 0
+UNROLL = 4
+EARLY = 2
+PACE = (3,) * 12
 
 
 def lasting(microseconds):
@@ -429,11 +433,12 @@
 
 
 class Reducer:
-    def __init__(self, count, grads, out, scratch):
-        self.grads = grads
+    def __init__(self, count, unit, staged, out, scratch):
+        self.unit = unit
+        self.staged = staged
         self.out = out
         (
-            self.own,
+            self.ring,
             self.from_sib,
             self.from_far,
             self.from_pair,
@@ -465,21 +470,11 @@
         self.level = me // 2
         self.pair = me + 1 - 2 * self.side
 
-    def unit(self, u, quarter):
-        singles = len(self.grads) - 2
-        inner, outer = self.grads[-2:]
-        part, features = self.out.shape[1] * self.out.shape[2], self.out.shape[3]
-        if u < singles:
-            return self.grads[u].at[quarter]
-        u -= singles
-        across = inner.shape[2] // features
-        if u < across:
-            return inner.at[quarter, :, pl.ds(u * features, features)]
-        return outer.at[quarter, pl.ds((u - across) * part, part)]
-
     def load(self, u, slot):
         return pltpu.make_async_copy(
-            self.unit(u, (self.w, self.far)[slot]), self.own.at[u, slot], self.load_sem.at[u, slot]
+            self.unit(u, (self.w, self.far)[slot]),
+            self.ring.at[u % 2, slot],
+            self.load_sem.at[u, slot],
         )
 
     def remote(self, src, dst, send, recv, **device):
@@ -503,7 +498,7 @@
 
     def to_far(self, u):
         return self.remote(
-            self.own.at[u, 1],
+            self.from_sib.at[u, 1],
             self.from_far.at[u],
             self.far_s.at[u],
             self.far_r.at[u],
@@ -512,7 +507,7 @@
 
     def half(self, u, side):
         rows = self.out.shape[2]
-        return self.own.at[u, 0, pl.ds(pl.multiple_of(side * rows, rows), rows)]
+        return self.from_sib.at[u, 0, pl.ds(pl.multiple_of(side * rows, rows), rows)]
 
     def to_pair(self, u):
         return self.remote(
@@ -552,19 +547,26 @@
     def begin(self, u):
         for slot in (1, 0):
             self.to_sib(u, slot).start()
-            self.load(u, slot).start()
+            if u < min(2, self.staged):
+                self.load(u, slot).start()
 
     def join_sib(self, u):
         for slot in (1, 0):
-            self.load(u, slot).wait()
+            if u < self.staged:
+                self.load(u, slot).wait()
+                own = self.ring[u % 2, slot]
+            else:
+                own = self.unit(u, (self.w, self.far)[slot])[...]
             self.to_sib(u, slot).wait_recv()
-            self.own[u, slot] = add_bf16(self.own[u, slot], self.from_sib[u, slot])
+            self.from_sib[u, slot] = add_bf16(own, self.from_sib[u, slot])
             if slot == 1:
                 self.to_far(u).start()
+            if u + 2 < self.staged:
+                self.load(u + 2, slot).start()
 
     def join_far(self, u):
         self.to_far(u).wait_recv()
-        self.own[u, 0] = add_bf16(self.own[u, 0], self.from_far[u])
+        self.from_sib[u, 0] = add_bf16(self.from_sib[u, 0], self.from_far[u])
         self.to_pair(u).start()
 
     def join_pair(self, u):
@@ -595,21 +597,18 @@
                 self.widen(u).start()
             self.give_back(u, self.side).start()
 
-    def steps(self):
-        return self.units + 2 * self.top + 3
-
     def step(self, t):
-        lag = 0
-
         def unit(lag):
             u = t - lag
+            if u >= self.staged:
+                u = u - GAP if u >= self.staged + GAP else -1
             return u if 0 <= u < self.units else None
 
-        for stage in (self.join_sib, self.join_far, self.join_pair):
-            if unit(lag) is not None:
-                stage(unit(lag))
-            lag += 1
-        lag -= 1
+        if unit(0) is not None:
+            self.join_far(unit(0))
+        if unit(1) is not None:
+            self.join_pair(unit(1))
+        lag = 1
         for hop in range(self.top + 1):
             if unit(lag) is not None:
                 self.gather(unit(lag), hop)
@@ -619,6 +618,9 @@
                 self.spread_out(unit(lag), hop)
             lag += 1
 
+    def steps(self):
+        return self.units + GAP + 2 * self.top + 1
+
     def finish(self):
         for u in range(self.units):
             self.give_back(u, 1 - self.side).wait_recv()
@@ -642,21 +644,12 @@
     return (left.astype(jnp.float32) + right.astype(jnp.float32)).astype(jnp.bfloat16)
 
 
-def unit_count(grads):
-    inner, outer = grads[-2:]
-    features = outer.shape[2]
-    return len(grads) - 2 + inner.shape[2] // features + outer.shape[1] // (features // 4)
-
-
-def reducer_shapes(grads):
-    units = unit_count(grads)
-    features = grads[-1].shape[2]
-    part = features // 4
+def reducer_shapes(units, part, features):
     dma = pltpu.SemaphoreType.DMA
     kind = jnp.bfloat16
     out = jax.ShapeDtypeStruct((units, 2, part // 2, features), kind)
     scratch = [
-        pltpu.VMEM((units, 2, part, features), kind),
+        pltpu.VMEM((2, 2, part, features), kind),
         pltpu.VMEM((units, 2, part, features), kind),
         pltpu.VMEM((units, part, features), kind),
         pltpu.VMEM((units, part // 2, features), kind),
@@ -664,271 +657,555 @@
         dma((units, 2)),
         dma((units, 2)),
         dma((units, 2)),
-        dma((units,)),
-        dma((units,)),
-        dma((units,)),
-        dma((units,)),
-        dma((units,)),
-        dma((units,)),
-        dma((units,)),
-        dma((units,)),
-        dma((units,)),
-        dma((units,)),
+    ] + [dma((units,)) for _ in range(10)]
+    return out, scratch
+
+
+class Returner:
+    def __init__(self, count, capacity, far_ref, rim_ref, outs, small, sems):
+        self.count, self.capacity, self.small = count, capacity, small
+        self.far_ref, self.rim_ref = far_ref, rim_ref
+        self.back, self.rim, self.glob, self.small_out = outs
+        (
+            self.rand_s,
+            self.rand_r,
+            self.halo_s,
+            self.halo_r,
+            self.glob_s,
+            self.glob_r,
+            self.loc,
+            self.group_part,
+            self.ring_part,
+            self.group_s,
+            self.group_r,
+            self.ring_s,
+            self.ring_r,
+        ) = sems
+        self.me = lax.axis_index("ctx")
+        self.w = lax.axis_index("wsh")
+        self.last = count - 1
+        self.groups = small.shape[0]
+        self.is_source = jnp.logical_and(self.me >= 1, self.me <= self.last - 1)
+
+    def remote(self, src, dst, send, recv, **device):
+        return pltpu.make_async_remote_copy(
+            src_ref=src,
+            dst_ref=dst,
+            send_sem=send,
+            recv_sem=recv,
+            device_id=device,
+            device_id_type=MESH,
+        )
+
+    def random_copy(self, owner, k):
+        return self.remote(
+            self.far_ref.at[(owner - 1) * self.capacity + k],
+            self.back.at[self.me, k],
+            self.rand_s.at[owner, k],
+            self.rand_r.at[self.me, k],
+            ctx=owner,
+        )
+
+    def landed(self, sender, k):
+        return self.remote(
+            self.far_ref.at[k],
+            self.back.at[sender, k],
+            self.rand_s.at[sender, k],
+            self.rand_r.at[sender, k],
+            ctx=sender,
+        )
+
+    def own_random(self):
+        return pltpu.make_async_copy(
+            self.far_ref.at[pl.ds((self.me - 1) * self.capacity, self.capacity)],
+            self.back.at[self.me],
+            self.loc.at[0],
+        )
+
+    def halo_copy(self, side):
+        return self.remote(
+            self.rim_ref.at[side],
+            self.rim.at[1 - side],
+            self.halo_s.at[side],
+            self.halo_r.at[side],
+            ctx=self.me - 1 if side == 0 else self.me + 1,
+        )
+
+    def global_copy(self, which, sender):
+        return self.remote(
+            self.rim_ref.at[2 + which],
+            self.glob.at[sender],
+            self.glob_s.at[which],
+            self.glob_r.at[sender],
+            ctx=0 if which == 0 else self.last,
+        )
+
+    def own_global(self, which):
+        return pltpu.make_async_copy(
+            self.rim_ref.at[2 + which], self.glob.at[self.me], self.loc.at[1]
+        )
+
+    def group_copy(self, target, sender):
+        return self.remote(
+            self.small.at[target],
+            self.group_part.at[sender],
+            self.group_s.at[target],
+            self.group_r.at[sender],
+            wsh=target,
+        )
+
+    def ring_copy(self, target, sender):
+        return self.remote(
+            self.ring_part.at[self.me],
+            self.ring_part.at[sender],
+            self.ring_s.at[target],
+            self.ring_r.at[sender],
+            ctx=target,
+        )
+
+    def send_random(self, owner, slots):
+        @pl.when(owner != self.me)
+        def _():
+            for k in slots:
+                self.random_copy(owner, k).start()
+
+    def send_round(self, k):
+        @pl.loop(0, self.count - 2)
+        def _(i):
+            self.send_random(1 + (self.me + i) % (self.count - 2), (k,))
+
+    def keep_own(self):
+        @pl.when(self.is_source)
+        def _():
+            self.own_random().start()
+
+    def send_rims(self):
+        @pl.when(self.me > 0)
+        def _():
+            self.halo_copy(0).start()
+            self.global_copy(0, self.me).start()
+
+        @pl.when(self.me < self.last)
+        def _():
+            self.halo_copy(1).start()
+            self.global_copy(1, self.me).start()
+
+        for which, owner in ((0, 0), (1, self.last)):
+
+            @pl.when(self.me == owner)
+            def _():
+                self.own_global(which).start()
+
+    def send_small(self):
+        for delta in range(1, self.groups):
+            self.group_copy((self.w + delta) % self.groups, self.w).start()
+
+    def pass_small(self):
+        total = self.small[self.w]
+        for delta in range(1, self.groups):
+            sender = (self.w + delta) % self.groups
+            self.group_copy(self.w, sender).wait_recv()
+            total = total + self.group_part[sender]
+        self.ring_part[self.me] = total
+
+        @pl.loop(1, self.count)
+        def _(delta):
+            self.ring_copy((self.me + delta) % self.count, self.me).start()
+
+    def end_small(self):
+        @pl.loop(1, self.count)
+        def _(delta):
+            self.ring_copy(self.me, (self.me + delta) % self.count).wait_recv()
+
+        self.small_out[...] = jnp.sum(self.ring_part[...], axis=0)
+
+        @pl.loop(1, self.count)
+        def _(delta):
+            self.ring_copy((self.me + delta) % self.count, self.me).wait_send()
+
+        for delta in range(1, self.groups):
+            self.group_copy((self.w + delta) % self.groups, self.w).wait_send()
+
+    def finish(self):
+        @pl.when(self.is_source)
+        def _():
+            self.own_random().wait()
+
+            @pl.loop(0, self.count)
+            def _(sender):
+                @pl.when(sender != self.me)
+                def _():
+                    for k in range(self.capacity):
+                        self.landed(sender, k).wait_recv()
+
+        for which, owner in ((0, 0), (1, self.last)):
+
+            @pl.when(self.me == owner)
+            def _():
+                self.own_global(which).wait()
+
+                @pl.loop(0, self.count)
+                def _(sender):
+                    @pl.when(sender != self.me)
+                    def _():
+                        self.global_copy(which, sender).wait_recv()
+
+        @pl.when(self.me > 0)
+        def _():
+            self.halo_copy(0).wait_send()
+            self.halo_copy(1).wait_recv()
+            self.global_copy(0, self.me).wait_send()
+
+        @pl.when(self.me < self.last)
+        def _():
+            self.halo_copy(1).wait_send()
+            self.halo_copy(0).wait_recv()
+            self.global_copy(1, self.me).wait_send()
+
+        @pl.loop(1, self.last)
+        def _(owner):
+            @pl.when(owner != self.me)
+            def _():
+                for k in range(self.capacity):
+                    self.random_copy(owner, k).wait_send()
+
+
+def returner_shapes(count, capacity, tail, small):
+    kind = jnp.bfloat16
+    dma = pltpu.SemaphoreType.DMA
+    groups = small.shape[0]
+    outs = [
+        jax.ShapeDtypeStruct((count, capacity) + tail, kind),
+        jax.ShapeDtypeStruct((2,) + tail, kind),
+        jax.ShapeDtypeStruct((count,) + tail, kind),
+        jax.ShapeDtypeStruct(small.shape[1:], jnp.float32),
     ]
-    return out, scratch
-
-
-def return_kernel(count, capacity, weights, far_grad, small, *refs):
-    grads = refs[:weights]
-    back, rim, glob, small_out = refs[weights : weights + 4]
-    refs = refs[weights + 4 :]
-    reducer = None
-    if weights:
-        reducer = Reducer(count, grads, refs[0], refs[1 + 15 :])
-        refs = refs[1:]
-    rand_s, rand_r, halo_s, halo_r, glob_s, glob_r, loc, own_far, own_glob = refs[:9]
-    group_part, ring_part, group_s, group_r, ring_s, ring_r = refs[9:15]
-    me = lax.axis_index("ctx")
-    w = lax.axis_index("wsh")
-    last = count - 1
-    groups = small.shape[0]
-    is_source = jnp.logical_and(me >= 1, me <= last - 1)
-    greet(count, groups)
-
-    def random_copy(owner, sender, k):
-        return pltpu.make_async_remote_copy(
-            src_ref=far_grad.at[EXTRA + (owner - 1) * capacity + k],
-            dst_ref=back.at[sender, k],
-            send_sem=rand_s.at[owner, k],
-            recv_sem=rand_r.at[sender, k],
-            device_id={"ctx": owner},
-            device_id_type=MESH,
-        )
-
-    def landed(sender, k):
-        return pltpu.make_async_remote_copy(
-            src_ref=far_grad.at[EXTRA + k],
-            dst_ref=back.at[sender, k],
-            send_sem=rand_s.at[sender, k],
-            recv_sem=rand_r.at[sender, k],
-            device_id={"ctx": sender},
-            device_id_type=MESH,
-        )
-
-    def send_random(k):
-        @pl.loop(1, count)
-        def _(delta):
-            owner = (me + delta) % count
-
-            @pl.when(jnp.logical_and(owner >= 1, owner <= last - 1))
-            def _():
-                random_copy(owner, me, k).start()
-
-    def halo_copy(side):
-        return pltpu.make_async_remote_copy(
-            src_ref=far_grad.at[side],
-            dst_ref=rim.at[1 - side],
-            send_sem=halo_s.at[side],
-            recv_sem=halo_r.at[side],
-            device_id={"ctx": me - 1 if side == 0 else me + 1},
-            device_id_type=MESH,
-        )
-
-    def global_copy(which, sender):
-        return pltpu.make_async_remote_copy(
-            src_ref=far_grad.at[2 + which],
-            dst_ref=glob.at[sender],
-            send_sem=glob_s.at[which],
-            recv_sem=glob_r.at[sender],
-            device_id={"ctx": 0 if which == 0 else last},
-            device_id_type=MESH,
-        )
-
-    def group_copy(target, sender):
-        return pltpu.make_async_remote_copy(
-            src_ref=small.at[target],
-            dst_ref=group_part.at[sender],
-            send_sem=group_s.at[target],
-            recv_sem=group_r.at[sender],
-            device_id={"wsh": target},
-            device_id_type=MESH,
-        )
-
-    def ring_copy(target, sender):
-        return pltpu.make_async_remote_copy(
-            src_ref=ring_part.at[me],
-            dst_ref=ring_part.at[sender],
-            send_sem=ring_s.at[target],
-            recv_sem=ring_r.at[sender],
-            device_id={"ctx": target},
-            device_id_type=MESH,
-        )
-
-    for delta in range(1, groups):
-        group_copy((w + delta) % groups, w).start()
-
-    @pl.when(me > 0)
-    def _():
-        halo_copy(0).start()
-        global_copy(0, me).start()
-
-    @pl.when(me < last)
-    def _():
-        halo_copy(1).start()
-        global_copy(1, me).start()
-
-    if reducer:
-        for u in range(reducer.units):
-            reducer.begin(u)
-    else:
-        for k in range(capacity):
-            send_random(k)
-
-    total = small[w]
-    for delta in range(1, groups):
-        sender = (w + delta) % groups
-        group_copy(w, sender).wait_recv()
-        total = total + group_part[sender]
-    ring_part[me] = total
-
-    @pl.loop(1, count)
-    def _(delta):
-        ring_copy((me + delta) % count, me).start()
-
-    def own_random_in():
-        return pltpu.make_async_copy(
-            far_grad.at[pl.ds(EXTRA + (me - 1) * capacity, capacity)], own_far, loc.at[0]
-        )
-
-    def own_random_out():
-        return pltpu.make_async_copy(own_far, back.at[me], loc.at[1])
-
-    def own_global_in(which):
-        return pltpu.make_async_copy(far_grad.at[2 + which], own_glob, loc.at[2])
-
-    def own_global_out():
-        return pltpu.make_async_copy(own_glob, glob.at[me], loc.at[3])
-
-    @pl.when(is_source)
-    def _():
-        own_random_in().start()
-        own_random_in().wait()
-        own_random_out().start()
-        own_random_out().wait()
-
-    for which, owner in ((0, 0), (1, last)):
-
-        @pl.when(me == owner)
-        def _():
-            own_global_in(which).start()
-            own_global_in(which).wait()
-            own_global_out().start()
-            own_global_out().wait()
-
-    @pl.loop(1, count)
-    def _(delta):
-        ring_copy(me, (me + delta) % count).wait_recv()
-
-    small_out[...] = jnp.sum(ring_part[...], axis=0)
-
-    if reducer:
-        for t in range(reducer.steps()):
-            if t < capacity:
-                send_random(t)
-            reducer.step(t)
-        reducer.finish()
-
-    @pl.loop(1, count)
-    def _(delta):
-        ring_copy((me + delta) % count, me).wait_send()
-
-    for delta in range(1, groups):
-        group_copy((w + delta) % groups, w).wait_send()
-
-    @pl.when(is_source)
-    def _():
-        @pl.loop(0, count)
-        def _(sender):
-            @pl.when(sender != me)
-            def _():
-                for k in range(capacity):
-                    landed(sender, k).wait_recv()
-
-    for which, owner in ((0, 0), (1, last)):
-
-        @pl.when(me == owner)
-        def _():
-            @pl.loop(0, count)
-            def _(sender):
-                @pl.when(sender != me)
-                def _():
-                    global_copy(which, sender).wait_recv()
-
-    @pl.when(me > 0)
-    def _():
-        halo_copy(0).wait_send()
-        halo_copy(1).wait_recv()
-        global_copy(0, me).wait_send()
-
-    @pl.when(me < last)
-    def _():
-        halo_copy(1).wait_send()
-        halo_copy(0).wait_recv()
-        global_copy(1, me).wait_send()
-
-    @pl.loop(1, count)
-    def _(delta):
-        owner = (me + delta) % count
-
-        @pl.when(jnp.logical_and(owner >= 1, owner <= last - 1))
-        def _():
-            for k in range(capacity):
-                random_copy(owner, me, k).wait_send()
-
-
-def return_grads(far_grad, small, grads, count, capacity):
+    sems = [
+        dma((count, capacity)),
+        dma((count, capacity)),
+        dma((2,)),
+        dma((2,)),
+        dma((2,)),
+        dma((count,)),
+        dma((2,)),
+        pltpu.VMEM(small.shape, jnp.float32),
+        pltpu.VMEM((count,) + small.shape[1:], jnp.float32),
+        dma((groups,)),
+        dma((groups,)),
+        dma((count,)),
+        dma((count,)),
+    ]
+    return outs, sems
+
+
+HBM_SPEC = pl.BlockSpec(memory_space=pl.ANY)
+VMEM_SPEC = pl.BlockSpec(memory_space=pltpu.VMEM)
+RETURN_SPECS = [HBM_SPEC, HBM_SPEC, HBM_SPEC, VMEM_SPEC]
+
+
+def return_kernel(count, capacity, far_ref, rim_ref, small, *refs):
+    mover = Returner(count, capacity, far_ref, rim_ref, refs[:4], small, refs[4:])
+    greet(count, small.shape[0])
+    mover.send_small()
+    mover.send_rims()
+
+    for k in range(capacity):
+        mover.send_round(k)
+    mover.keep_own()
+    mover.pass_small()
+    mover.end_small()
+    mover.finish()
+
+
+def return_grads(far_grad, small, count, capacity):
     tail = far_grad.shape[1:]
-    kind = far_grad.dtype
-    groups = small.shape[0]
-    hbm = pl.BlockSpec(memory_space=pl.ANY)
-    vmem = pl.BlockSpec(memory_space=pltpu.VMEM)
-    sums, sum_scratch = reducer_shapes(grads) if grads else (None, [])
-    dma = pltpu.SemaphoreType.DMA
+    outs, sems = returner_shapes(count, capacity, tail, small)
     return pl.pallas_call(
-        functools.partial(return_kernel, count, capacity, len(grads)),
-        out_shape=[
-            jax.ShapeDtypeStruct((count, capacity) + tail, kind),
-            jax.ShapeDtypeStruct((2,) + tail, kind),
-            jax.ShapeDtypeStruct((count,) + tail, kind),
-            jax.ShapeDtypeStruct(small.shape[1:], jnp.float32),
-        ]
-        + ([sums] if grads else []),
-        in_specs=[hbm, vmem] + [hbm] * len(grads),
-        out_specs=[hbm, hbm, hbm, vmem] + ([vmem] if grads else []),
-        scratch_shapes=[
-            dma((count, capacity)),
-            dma((count, capacity)),
-            dma((2,)),
-            dma((2,)),
-            dma((2,)),
-            dma((count,)),
-            dma((4,)),
-            pltpu.VMEM((capacity,) + tail, kind),
-            pltpu.VMEM(tail, kind),
-            pltpu.VMEM(small.shape, jnp.float32),
-            pltpu.VMEM((count,) + small.shape[1:], jnp.float32),
-            dma((groups,)),
-            dma((groups,)),
-            dma((count,)),
-            dma((count,)),
-        ]
-        + sum_scratch,
+        functools.partial(return_kernel, count, capacity),
+        out_shape=outs,
+        in_specs=[VMEM_SPEC, VMEM_SPEC, VMEM_SPEC],
+        out_specs=RETURN_SPECS,
+        scratch_shapes=sems,
         compiler_params=pltpu.CompilerParams(
             collective_id=1, has_side_effects=True, vmem_limit_bytes=56 * MIB
         ),
+        name="return_grads",
+    )(far_grad[EXTRA:], far_grad[:EXTRA], small)
+
+
+def tail_kernel(
+    count,
+    capacity,
+    dq_hbm,
+    dk_hbm,
+    dv_hbm,
+    x_hbm,
+    stream_hbm,
+    outer_hbm,
+    inner_hbm,
+    wo_hbm,
+    wq_ref,
+    wk_ref,
+    wv_ref,
+    small_in,
+    *refs,
+):
+    outs, near_hbm, sums = refs[:4], refs[4], refs[5]
+    (
+        xbuf,
+        kbuf,
+        vbuf,
+        qbuf,
+        wq_sum,
+        wk_sum,
+        wv_sum,
+        shares,
+        sending,
+        rims,
+        stage,
+        small,
+        bias_sum,
+        load_sem,
+        q_sem,
+        stage_sem,
+    ) = refs[6:22]
+    returner_sems, reducer_scratch = refs[22:35], refs[35:]
+    blocks, _, features = dq_hbm.shape
+    length = blocks * BLK
+    near = blocks + EXTRA
+    chunk = capacity * BLK
+    part = features // 4
+    me = lax.axis_index("ctx")
+    sources = count - 2
+    mover = Returner(count, capacity, sending, rims, outs, small, returner_sems)
+    across = inner_hbm.shape[2] // features
+    stacked = outer_hbm.shape[1] // part
+    staged = stacked + across + 1
+
+    def unit(u, quarter):
+        if u < stacked:
+            return outer_hbm.at[quarter, pl.ds(u * part, part)]
+        if u < stacked + across:
+            return inner_hbm.at[quarter, :, pl.ds((u - stacked) * features, features)]
+        if u < staged:
+            return wo_hbm.at[quarter]
+        return shares.at[u - staged, quarter]
+
+    reducer = Reducer(count, unit, staged, sums, reducer_scratch)
+
+    def loads(at, slot, size):
+        here, there = pl.ds(at, size), pl.ds(0, size)
+        return [
+            pltpu.make_async_copy(src.at[here], dst.at[slot, there], load_sem.at[slot, n])
+            for n, (src, dst) in enumerate(((x_hbm, xbuf), (dk_hbm, kbuf), (dv_hbm, vbuf)))
+        ]
+
+    def far_loads(i, slot):
+        return loads(near + ((me + i) % sources) * capacity, slot, capacity)
+
+    def own_loads(n):
+        half = blocks // 2
+        return loads(n * half, n, half) + [
+            pltpu.make_async_copy(dq_hbm.at[pl.ds(n * half, half)], qbuf.at[n], q_sem.at[n])
+        ]
+
+    def start(copies):
+        for copy in copies:
+            copy.start()
+
+    def end(copies):
+        for copy in copies:
+            copy.wait()
+
+    def gather_weights(rows, key_grad, value_grad):
+        wk_sum[...] += tn(rows, key_grad)
+        wv_sum[...] += tn(rows, value_grad)
+        bias_sum[1:2] += jnp.sum(value_grad.astype(jnp.float32), axis=0, keepdims=True)
+
+    start(far_loads(0, 0))
+    greet(count, small.shape[0])
+    for u in range(staged):
+        reducer.begin(u)
+    bias_sum[...] = jnp.zeros_like(bias_sum)
+    wk_sum[...] = jnp.zeros_like(wk_sum)
+    wv_sum[...] = jnp.zeros_like(wv_sum)
+
+    for third in range(3):
+
+        @pl.loop(third * sources // 3, (third + 1) * sources // 3)
+        def _(i):
+            slot = i % 2
+            end(far_loads(i, slot))
+
+            @pl.when(i + 1 < sources)
+            def _():
+                start(far_loads(i + 1, 1 - slot))
+
+            key_grad = kbuf[slot].reshape(chunk, features)
+            value_grad = vbuf[slot].reshape(chunk, features)
+            row_grad = nt(key_grad, wk_ref[...]) + nt(value_grad, wv_ref[...])
+            s = 1 + (me + i) % sources
+            sending[pl.ds((s - 1) * capacity, capacity)] = row_grad.astype(sending.dtype).reshape(
+                capacity, BLK, features
+            )
+            mover.send_random(s, range(EARLY))
+            gather_weights(xbuf[slot].reshape(chunk, features), key_grad, value_grad)
+
+        for u in range(third * staged // 3, (third + 1) * staged // 3):
+            reducer.join_sib(u)
+    mover.keep_own()
+
+    rim_loads = loads(blocks, 0, EXTRA)
+    start(rim_loads)
+    end(rim_loads)
+    rim_rows = EXTRA * BLK
+    key_grad = kbuf[0, :EXTRA].reshape(rim_rows, features)
+    value_grad = vbuf[0, :EXTRA].reshape(rim_rows, features)
+    row_grad = nt(key_grad, wk_ref[...]) + nt(value_grad, wv_ref[...])
+    rims[...] = row_grad.astype(rims.dtype).reshape(EXTRA, BLK, features)
+    mover.send_rims()
+    gather_weights(xbuf[0, :EXTRA].reshape(rim_rows, features), key_grad, value_grad)
+
+    start(own_loads(0))
+    start(own_loads(1))
+    wq_sum[...] = jnp.zeros_like(wq_sum)
+    half = length // 2
+
+    def stage_load(n):
+        return pltpu.make_async_copy(
+            stream_hbm.at[pl.ds(n * half, half)], stage.at[n], stage_sem.at[0, n]
+        )
+
+    def stage_store(n):
+        return pltpu.make_async_copy(
+            stage.at[n], near_hbm.at[pl.ds(n * half, half)], stage_sem.at[1, n]
+        )
+
+    for n in range(2):
+        stage_load(n).start()
+        end(own_loads(n))
+
+    @pl.loop(0, 2)
+    def _(n):
+        rows = xbuf[n].reshape(half, features)
+        query_grad = qbuf[n].reshape(half, features)
+        gather_weights(rows, kbuf[n].reshape(half, features), vbuf[n].reshape(half, features))
+        wq_sum[...] += tn(rows, query_grad)
+        bias_sum[0:1] += jnp.sum(query_grad.astype(jnp.float32), axis=0, keepdims=True)
+
+    for u, total in ((0, wq_sum), (1, wk_sum), (2, wv_sum)):
+        for quarter in range(4):
+            shares[u, quarter] = total[quarter * part : (quarter + 1) * part].astype(shares.dtype)
+        reducer.begin(staged + u)
+    small[...] = small_in[...]
+    for quarter in range(4):
+        lanes = slice(quarter * part, (quarter + 1) * part)
+        small[quarter, 0:2, :part] = bias_sum[0:2, lanes]
+    mover.send_small()
+
+    ticks = iter(range(reducer.steps()))
+    waiting = list(range(EARLY * sources, capacity * sources))
+
+    def advance():
+        tick = next(ticks)
+        reducer.step(tick)
+        wave = PACE[tick] if tick < len(PACE) else 0
+        for n in waiting[:wave]:
+            mover.send_random(1 + (me + n % sources) % sources, (n // sources,))
+        del waiting[:wave]
+        return tick + 1
+
+    advance()
+    advance()
+    for u in range(staged, reducer.units):
+        reducer.join_sib(u)
+    mover.pass_small()
+
+    for n in range(2):
+        stage_load(n).wait()
+        stage[n] = (
+            stage[n]
+            + nt(qbuf[n].reshape(half, features), wq_ref[...])
+            + nt(kbuf[n].reshape(half, features), wk_ref[...])
+            + nt(vbuf[n].reshape(half, features), wv_ref[...])
+        )
+        stage_store(n).start()
+        advance()
+    while advance() < reducer.steps():
+        pass
+    for n in range(2):
+        stage_store(n).wait()
+    mover.end_small()
+    reducer.finish()
+    mover.finish()
+
+
+def backward_tail(
+    dq,
+    dk,
+    dv,
+    ext_rows,
+    stream_grad,
+    outer_grad,
+    inner_grad,
+    output_grad,
+    wq,
+    wk,
+    wv,
+    small,
+    count,
+    capacity,
+):
+    blocks, block_rows, features = dq.shape
+    tail = (block_rows, features)
+    far_slots = (count - 2) * capacity
+    part = features // 4
+    outs, sems = returner_shapes(count, capacity, tail, small)
+    units = outer_grad.shape[1] // part + inner_grad.shape[2] // features + 4
+    sums, sum_scratch = reducer_shapes(units, part, features)
+    kind = jnp.bfloat16
+    dma = pltpu.SemaphoreType.DMA
+    square = pltpu.VMEM((features, features), jnp.float32)
+    some = pltpu.VMEM((2, capacity) + tail, kind)
+    return pl.pallas_call(
+        functools.partial(tail_kernel, count, capacity),
+        out_shape=outs + [jax.ShapeDtypeStruct(stream_grad.shape, jnp.float32), sums],
+        in_specs=[HBM_SPEC] * 8 + [VMEM_SPEC] * 4,
+        out_specs=RETURN_SPECS + [HBM_SPEC, VMEM_SPEC],
+        scratch_shapes=[some] * 4
+        + [square] * 3
+        + [
+            pltpu.VMEM((3, 4, part, features), kind),
+            pltpu.VMEM((far_slots,) + tail, kind),
+            pltpu.VMEM((EXTRA,) + tail, kind),
+            pltpu.VMEM((2, blocks * block_rows // 2, features), jnp.float32),
+            pltpu.VMEM(small.shape, jnp.float32),
+            pltpu.VMEM((8, features), jnp.float32),
+            dma((2, 3)),
+            dma((2,)),
+            dma((2, 2)),
+        ]
+        + sems
+        + sum_scratch,
+        compiler_params=pltpu.CompilerParams(
+            collective_id=1, has_side_effects=True, vmem_limit_bytes=58 * MIB
+        ),
         cost_estimate=lasting(150),
-        name="return_grads",
-    )(far_grad, small, *grads)
+        name="backward_tail",
+    )(
+        dq,
+        dk,
+        dv,
+        ext_rows,
+        stream_grad,
+        outer_grad,
+        inner_grad,
+        output_grad,
+        wq,
+        wk,
+        wv,
+        small,
+    )
 
 
 def unpack_kernel(
@@ -1041,7 +1318,7 @@
     blocks = q_ref.shape[0]
     mask = head_mask()
 
-    @pl.loop(0, blocks)
+    @pl.loop(0, blocks, unroll=True)
     def _(b):
         query = spread_heads(q_ref[b] * HD**-0.5, mask)
         scores = mask_edges(nt(listed_rows(k_ref, index_ref, b), query), edge_ref, b, blocks)
@@ -1106,7 +1383,7 @@
     dk_ref[...] = jnp.zeros_like(dk_ref)
     dv_ref[...] = jnp.zeros_like(dv_ref)
 
-    @pl.loop(0, blocks)
+    @pl.loop(0, blocks, unroll=UNROLL)
     def _(b):
         query = spread_heads(q_ref[b] * HD**-0.5, mask)
         upstream = spread_heads(g_ref[b], mask)
@@ -1263,7 +1540,8 @@
     att_grad = stream_grad.astype(jnp.bfloat16)
     att_grad_ref[...] = att_grad
     tally(0, att_grad.astype(jnp.float32))
-    mixed_grad_ref[...] = nt(att_grad, wo_ref[...]).astype(jnp.bfloat16)
+    mixed_grad = nt(att_grad, wo_ref[...]).astype(jnp.bfloat16)
+    mixed_grad_ref[...] = mixed_grad
 
 
 def middle(mixed, rows, cotangent, vectors, inner_bias, wo, w1, w2):
@@ -1453,82 +1731,89 @@
     outer_weight_grad = outer_product(activated_bf, outer_grad_bf)
     square_sums = jnp.sum(middle_sums[6:8], axis=1)
 
+    fused = count == 8 and 3 * blocks_here == capacity * (count - 2)
+
+    def small_parts(query_row, value_row):
+        rows = jnp.concatenate([query_row, value_row, middle_sums[:6]], axis=0)
+        parts = jnp.concatenate(
+            [
+                jnp.transpose(rows.reshape(8, groups, part), (1, 0, 2)),
+                inner_bias_grad.reshape(groups, inner_parts, part),
+                jnp.broadcast_to(
+                    jnp.pad(square_sums, (0, part - 2)).reshape(1, 1, part), (groups, 1, part)
+                ),
+            ],
+            axis=1,
+        )
+        return jnp.pad(parts, ((0, 0), (0, (-parts.shape[1]) % 8), (0, (-part) % 128)))
+
+    mixed_grad_blocks = mixed_grad_bf.reshape(blocks_here, BLK, features)
     dq_blocks, dk_blocks, dv_blocks = attend_back(
-        query_blocks,
-        mixed_grad_bf.reshape(blocks_here, BLK, features),
-        key_blocks,
-        value_blocks,
-        log_total,
-        index,
-        edge,
+        query_blocks, mixed_grad_blocks, key_blocks, value_blocks, log_total, index, edge
     )
-    dq = dq_blocks.reshape(length, features)
-    dk = dk_blocks.reshape(slots * BLK, features)
-    dv = dv_blocks.reshape(slots * BLK, features)
-    far_grad = (
-        (back_product(dk[length:], full_key) + back_product(dv[length:], full_value))
-        .astype(jnp.bfloat16)
-        .reshape(slots - blocks_here, BLK, features)
-    )
-    query_bias_grad = column_sum(dq)
-    value_bias_grad = column_sum(dv)
-    weight_grads = tuple(
-        grad.astype(jnp.bfloat16).reshape(groups, -1, grad.shape[-1])
-        for grad in (
-            outer_product(token_rows, dq),
-            outer_product(ext_flat, dk),
-            outer_product(ext_flat, dv),
-            output_weight_grad,
-            inner_weight_grad,
-            outer_weight_grad,
-        )
-    )
-    vector_grads = jnp.concatenate(
-        [query_bias_grad[None], value_bias_grad[None], middle_sums[:6]], axis=0
-    )
-    small_grads = jnp.concatenate(
-        [
-            jnp.transpose(vector_grads.reshape(8, groups, part), (1, 0, 2)),
-            inner_bias_grad.reshape(groups, inner_parts, part),
-            jnp.broadcast_to(
-                jnp.pad(square_sums, (0, part - 2)).reshape(1, 1, part), (groups, 1, part)
-            ),
-        ],
-        axis=1,
-    )
-    small_grads = jnp.pad(
-        small_grads, ((0, 0), (0, (-small_grads.shape[1]) % 8), (0, (-part) % 128))
-    )
-    chained = count == 8
-    back, rim, glob, small_sums, *chain_sums = return_grads(
-        far_grad, small_grads, weight_grads if chained else (), count, capacity
-    )
-    near_grad = (
-        stream_grad
-        + back_product(dq, full_query)
-        + back_product(dk[:length], full_key)
-        + back_product(dv[:length], full_value)
-    ).reshape(blocks_here, BLK, features)
-    tokens_grad = unpack_grads(near_grad, back, rim, glob, picked, filled, edge)
-
-    if chained:
-        units = chain_sums[0].reshape(-1, part, features).astype(jnp.float32)
+    if fused:
+        empty = jnp.zeros((1, features), jnp.float32)
+        back, rim, glob, small_sums, near_grad, unit_sums = backward_tail(
+            dq_blocks,
+            dk_blocks,
+            dv_blocks,
+            ext_rows,
+            stream_grad,
+            outer_weight_grad.astype(jnp.bfloat16).reshape(groups, -1, features),
+            inner_weight_grad.astype(jnp.bfloat16).reshape(groups, part, -1),
+            output_weight_grad.astype(jnp.bfloat16).reshape(groups, part, features),
+            full_query,
+            full_key,
+            full_value,
+            small_parts(empty, empty),
+            count,
+            capacity,
+        )
+        stacked = full_outer.shape[0] // features
         across = full_inner.shape[1] // features
-        sums = [units[i] for i in range(4)] + [
-            jnp.concatenate([units[4 + i] for i in range(across)], axis=1),
-            units[4 + across :].reshape(-1, features),
+        units = unit_sums.reshape(-1, part, features).astype(jnp.float32)
+        sums = [units[stacked + across + i] for i in (1, 2, 3, 0)] + [
+            jnp.concatenate([units[stacked + i] for i in range(across)], axis=1),
+            units[:stacked].reshape(-1, features),
         ]
     else:
+        dq = dq_blocks.reshape(length, features)
+        dk = dk_blocks.reshape(slots * BLK, features)
+        dv = dv_blocks.reshape(slots * BLK, features)
+        far_grad = (
+            (back_product(dk[length:], full_key) + back_product(dv[length:], full_value))
+            .astype(jnp.bfloat16)
+            .reshape(slots - blocks_here, BLK, features)
+        )
+        back, rim, glob, small_sums = return_grads(
+            far_grad, small_parts(column_sum(dq)[None], column_sum(dv)[None]), count, capacity
+        )
+        near_grad = (
+            stream_grad
+            + back_product(dq, full_query)
+            + back_product(dk[:length], full_key)
+            + back_product(dv[:length], full_value)
+        )
         sums = lax.psum(
             tuple(
                 lax.psum_scatter(
-                    grad.reshape(-1, grad.shape[-1]), "wsh", scatter_dimension=0, tiled=True
+                    grad.astype(jnp.bfloat16), "wsh", scatter_dimension=0, tiled=True
                 )
-                for grad in weight_grads
+                for grad in (
+                    outer_product(token_rows, dq),
+                    outer_product(ext_flat, dk),
+                    outer_product(ext_flat, dv),
+                    output_weight_grad,
+                    inner_weight_grad,
+                    outer_weight_grad,
+                )
             ),
             "ctx",
         )
         sums = [total.astype(jnp.float32) for total in sums]
+    tokens_grad = unpack_grads(
+        near_grad.reshape(blocks_here, BLK, features), back, rim, glob, picked, filled, edge
+    )
     element_count = count * groups * length * features
     stream_rms = jnp.sqrt(small_sums[8 + inner_parts, :2] / element_count)
     (

time: 569 us -> 497 us (0.87)
  matrix products: 79.7 us -> 40.2 us
  Pallas kernels: 437 us -> 416 us
  local copies, waits for them, and re-layouts: 32 us -> 23.6 us
    pallas_call x1, Pallas kernels: 37.6 us -> 13.5 us  [attend(): pl.pallas_call(forward_kernel, out_shape=[jax.ShapeDtypeStruct(queries.sh...]
    dot_general x5 -> x0, matrix products: 22.7 us -> none  [back_product(): jnp.einsum('tb,ab->ta', upstream, weight, preferred_element_type=jnp.floa...]
    dot_general x6 -> x3, matrix products: 36.6 us -> 18.1 us  [outer_product(): jnp.einsum('ta,tb->ab', left, right, preferred_element_type=jnp.float32)]
    pallas_call x1, Pallas kernels: 196 us -> 210 us  [backward_tail(): pl.pallas_call(functools.partial(tail_kernel, count, capacity), out_shape...]
    pallas_call x1, Pallas kernels: 44.6 us -> 33.9 us  [attend_back(): pl.pallas_call(backward_kernel, out_shape=[jax.ShapeDtypeStruct(queries.s...]
    slice x6 -> x2, local copies, waits for them, and re-layouts: 14.1 us -> 4.87 us  [the longest x1 3.26 us: shards(): units[stacked + i]]
    unnamed x100 -> x70, local copies, waits for them, and re-layouts: 12.4 us -> 12.6 us
where the time goes in v4:
time: 497 us; the launch traced here: 488 us
  Pallas kernels  416 us (84%)
  matrix products  40.2 us (8%)
  local copies, waits for them, and re-layouts  23.6 us (5%)
  other arithmetic  6.76 us (1%)
    pallas_call x1, Pallas kernels, backward_tail(): pl.pallas_call(functools.partial(tail_kernel, count, capacity), out_shape...  210 us
    pallas_call x1, Pallas kernels, spread(): pl.pallas_call(functools.partial(spread_kernel, count, capacity), out_sha...  112 us
    pallas_call x1, Pallas kernels, middle(): pl.pallas_call(functools.partial(mid_kernel, MID_CHUNK), grid=(length //...  38.1 us
    pallas_call x1, Pallas kernels, attend_back(): pl.pallas_call(backward_kernel, out_shape=[jax.ShapeDtypeStruct(queries.s...  33.9 us
    dot_general x3, matrix products, outer_product(): jnp.einsum('ta,tb->ab', left, right, preferred_element_type=jnp.float32)  18.1 us
    pallas_call x1, Pallas kernels, attend(): pl.pallas_call(forward_kernel, out_shape=[jax.ShapeDtypeStruct(queries.sh...  13.5 us
    unnamed x70, local copies, waits for them, and re-layouts  12.6 us

profile of v4, /device:TPU:0, one launch (start us, length us, event | category | flops | bytes accessed | tf_op | source)
XLA Modules:
  0.0 487.8 jit_solution(15866850735310625028)
XLA Ops:
  2.8 5.4 %pack_blocks.1 = bf16[64,64,768]{2,1,0:T(8,128)(2,1)} custom-call(s32[64]{0:T(128)} %reshape.302.picked_ref, bf16[16,64,768]{2,1,0:T(8,128)(2,1)} %bitcast.91), custom_call_target="tpu_custom_call" | custom-call | tf_op jit(solution)/shard_map/pack_blocks/pallas_call | solution.py:90
  9.1 111.7 %spread_rows.1 = (bf16[68,64,768]{2,1,0:T(8,128)(2,1)}, bf16[2,8,64,768]{3,2,1,0:T(8,128)(2,1)}, bf16[4,192,768]{2,1,0:T(8,128)(2,1)}, bf16[4,192,768]{2,1,0:T(8...) custom-call(bf16[8,8,64,768]{3,2,1,0:T(8,128)(2,1)} %bitcast.84, ...), custom_call_target="tpu_custom_call" | custom-call | flops 109999996928 | bytes 110000000 | tf_op jit(solution)/shard_map/spread_rows/pallas_call | solution.py:400
  121.8 9.7 %add_convert_fusion = bf16[4352,768]{1,0:T(8,128)(2,1)} fusion(bf16[4352,768]{1,0:T(8,128)(2,1)} %bitcast.114, bf16[768,768]{1,0:T(8,128)(2,1)} %bitcast.127, f32[768]{0:T(1024)S(1)} %add.102), kind=kOutput, calls=%fused_computation | convolution fusion | flops 5140512768 | bytes 14552064 | tf_op jit(solution)/shard_map/dot_general | solution.py:1700
  131.6 2.8 fusion
  135.1 9.6 %convolution_convert_fusion = bf16[4352,768]{1,0:T(8,128)(2,1)} fusion(bf16[4352,768]{1,0:T(8,128)(2,1)} %bitcast.115, bf16[768,768]{1,0:T(8,128)(2,1)} %bitcast.125), kind=kOutput, calls=%fused_computation.1 | convolution fusion | flops 5137170432 | bytes 14548992 | tf_op jit(solution)/shard_map/dot_general | solution.py:1698
  145.1 2.9 copy-done.7
  148.0 13.5 %attend.1 = (bf16[16,64,768]{2,1,0:T(8,128)(2,1)S(1)}, f32[16,1,768]{2,1,0:T(1,128)S(1)}) custom-call(s32[128]{0:T(128)S(1)} %reshape.301.index_ref, s32[2]{0:T(128)S(1)} %add_convert_fusion.2.edge_ref, bf16[16,64,768]{2,1,0:T(8,128)(2,1)S(1)} %bitcast.77, bf16[68,64,768]{2,1,0:T(8,128)(2,1)S(1)} %bitcast.80, bf16[68,64,768]{2,1,0:T(8,128)(2,1)} %bitcast.116), custom_call_target="tpu_custom_call" | custom-call | flops 36999999488 | bytes 37000000 | tf_op jit(solution)/shard_map/attend/pallas_call | solution.py:1339
  161.6 1.1 copy-done.9
  164.0 38.1 %middle.1 = (bf16[1024,768]{1,0:T(8,128)(2,1)}, f32[1024,768]{1,0:T(8,128)}, bf16[1024,768]{1,0:T(8,128)(2,1)}, bf16[1024,768]{1,0:T(8,128)(2,1)}, bf16[1024,307...) custom-call(bf16[1024,768]{1,0:T(8,128)(2,1)} %bitcast.82, ...), custom_call_target="tpu_custom_call" | custom-call | flops 49999998976 | bytes 50000000 | tf_op jit(solution)/shard_map/middle/pallas_call | solution.py:1559
  203.5 1.4 reduce.7
  205.0 0.9 slice_reduce_fusion
  206.5 4.0 convolution_convert_fusion.3
  210.5 7.0 %convolution_convert_fusion.1 = bf16[768,3072]{1,0:T(8,128)(2,1)} fusion(bf16[1024,768]{1,0:T(8,128)(2,1)S(1)} %copy-done.29, bf16[1024,3072]{1,0:T(8,128)(2,1)S(1)} %copy-done.28), kind=kOutput, calls=%fused_computation.2 | convolution fusion | flops 4834197504 | bytes 12582912 | tf_op jit(solution)/shard_map/ta,tb->ab/dot_general | solution.py:1604
  217.5 7.1 %convolution_convert_fusion.2 = bf16[3072,768]{1,0:T(8,128)(2,1)} fusion(bf16[1024,3072]{1,0:T(8,128)(2,1)S(1)} %bitcast.132, bf16[1024,768]{1,0:T(8,128)(2,1)S(1)} %copy-done.30), kind=kOutput, calls=%fused_computation.3 | convolution fusion | flops 4834197504 | bytes 12582912 | tf_op jit(solution)/shard_map/ta,tb->ab/dot_general | solution.py:1604
  224.6 33.9 %attend_back.1 = (bf16[16,64,768]{2,1,0:T(8,128)(2,1)S(1)}, bf16[68,64,768]{2,1,0:T(8,128)(2,1)}, bf16[68,64,768]{2,1,0:T(8,128)(2,1)}) custom-call(s32[128]{0:T(128)S(1)} %reshape.301.index_ref, s32[2]{0:T(128)S(1)} %add_convert_fusion.2.edge_ref, bf16[16,64,768]{2,1,0:T(8,128)(2,1)S(1)} %bitcast.78, bf16[16,64,768]{2,1,0:T(8,128)(2,1)S(1)} %bitcast.81, ...), custom_call_target="tpu_custom_call" | custom-call | flops 44000002048 | bytes 44000000 | tf_op jit(solution)/shard_map/attend_back/pallas_call | solution.py:1421
  258.5 1.1 copy-done.11
  259.7 210.1 %backward_tail.1 = (bf16[8,8,64,768]{3,2,1,0:T(8,128)(2,1)}, bf16[2,64,768]{2,1,0:T(8,128)(2,1)}, bf16[8,64,768]{2,1,0:T(8,128)(2,1)}, f32[16,256]{1,0:T(8,128)}...) custom-call(bf16[16,64,768]{2,1,0:T(8,128)(2,1)} %copy-done.11, bf16[68,64,768]{2,1,0:T(8,128)(2,1)} %get-tuple-element.60.dk_hbm, ...), custom_call_target="tpu_custom_call" | custom-call | flops 149999992832 | bytes 150000000 | tf_op jit(solution)/shard_map/backward_tail/pallas_call | solution.py:1170
  469.8 3.3 fusion.8
  473.0 1.7 pad_maximum_fusion
  474.7 1.2 copy-done.12
  475.9 1.6 slice.123
  478.7 2.8 copy-done
  481.4 1.1 copy-done.2
  482.6 3.0 unpack_grads.1
  (107 shorter events, 11.3 us)
Async XLA Ops:
  1.6 6.7 %copy-start.17 = (pred[8,48]{1,0:T(8,128)(4,1)}, pred[8,48]{1,0:T(8,128)(4,1)S(1)}, u32[]{:S(2)}) copy-start(pred[8,48]{1,0:T(8,128)(4,1)S(1)} %get-tuple-element.76) | copy-start | bytes 1156
  1.9 142.8 %copy-start.14 = (s32[8,48]{1,0:T(8,128)}, s32[8,48]{1,0:T(8,128)S(1)}, u32[]{:S(2)}) copy-start(s32[8,48]{1,0:T(8,128)S(1)} %convert_reduce_fusion) | copy-start | bytes 4612
  2.7 5.5 %copy-start.19 = (bf16[768]{0:T(1024)(128)(2,1)S(1)}, bf16[768]{0:T(1024)(128)(2,1)}, u32[]{:S(2)}) copy-start(bf16[768]{0:T(1024)(128)(2,1)} %param.31) | copy-start | bytes 4612
  2.7 5.5 %copy-start.20 = (bf16[192]{0:T(256)(128)(2,1)S(1)}, bf16[192]{0:T(256)(128)(2,1)}, u32[]{:S(2)}) copy-start(bf16[192]{0:T(256)(128)(2,1)} %param.22) | copy-start | bytes 1156
  2.7 5.5 %copy-start.21 = (bf16[192]{0:T(256)(128)(2,1)S(1)}, bf16[192]{0:T(256)(128)(2,1)}, u32[]{:S(2)}) copy-start(bf16[192]{0:T(256)(128)(2,1)} %param.25) | copy-start | bytes 1156
  2.7 5.6 %copy-start.22 = (bf16[192]{0:T(256)(128)(2,1)S(1)}, bf16[192]{0:T(256)(128)(2,1)}, u32[]{:S(2)}) copy-start(bf16[192]{0:T(256)(128)(2,1)} %param.27) | copy-start | bytes 1156
  2.8 5.6 %copy-start.23 = (bf16[192]{0:T(256)(128)(2,1)S(1)}, bf16[192]{0:T(256)(128)(2,1)}, u32[]{:S(2)}) copy-start(bf16[192]{0:T(256)(128)(2,1)} %param.28) | copy-start | bytes 1156
  2.8 5.6 %copy-start.24 = (bf16[192]{0:T(256)(128)(2,1)S(1)}, bf16[192]{0:T(256)(128)(2,1)}, u32[]{:S(2)}) copy-start(bf16[192]{0:T(256)(128)(2,1)} %param.29) | copy-start | bytes 1156
  2.8 5.6 %copy-start.25 = (bf16[192]{0:T(256)(128)(2,1)S(1)}, bf16[192]{0:T(256)(128)(2,1)}, u32[]{:S(2)}) copy-start(bf16[192]{0:T(256)(128)(2,1)} %param.33) | copy-start | bytes 1156
  2.8 5.5 %copy-start.26 = (bf16[192]{0:T(256)(128)(2,1)S(1)}, bf16[192]{0:T(256)(128)(2,1)}, u32[]{:S(2)}) copy-start(bf16[192]{0:T(256)(128)(2,1)} %param.34) | copy-start | bytes 1156
  2.8 5.5 %copy-start.27 = (bf16[192]{0:T(256)(128)(2,1)S(1)}, bf16[192]{0:T(256)(128)(2,1)}, u32[]{:S(2)}) copy-start(bf16[192]{0:T(256)(128)(2,1)} %param.35) | copy-start | bytes 1156
  121.8 9.7 %copy-start.13 = (bf16[1,1024,768]{2,1,0:T(8,128)(2,1)S(1)}, bf16[1,1024,768]{2,1,0:T(8,128)(2,1)}, u32[]{:S(2)}) copy-start(bf16[1,1024,768]{2,1,0:T(8,128)(2,1)} %param.18) | copy-start | bytes 4718596
  145.1 2.9 copy-start.7
  148.0 76.6 %copy-start.5 = (s32[2]{0:T(128)}, s32[2]{0:T(128)S(1)}, u32[]{:S(2)}) copy-start(s32[2]{0:T(128)S(1)} %add_convert_fusion.2.edge_ref) | copy-start | bytes 28
  164.0 42.5 %copy-start.10 = (bf16[16,64,768]{2,1,0:T(8,128)(2,1)S(1)}, bf16[16,64,768]{2,1,0:T(8,128)(2,1)}, u32[]{:S(2)}) copy-start(bf16[16,64,768]{2,1,0:T(8,128)(2,1)} %copy-done.9) | copy-start | bytes 4718596
  205.8 4.7 copy-start.29
  206.5 4.0 copy-start.28
  206.5 11.0 %slice-start = ((s8[6291456]{0:T(1024)(128)(4,1)}), s8[4194304]{0:T(1024)(128)(4,1)S(1)}, s32[]{:S(2)}) async-start(s8[6291456]{0:T(1024)(128)(4,1)} %bitcast.131), calls=%async_computation | async-start | bytes 8388608
  210.5 7.0 %slice-start.1 = ((s8[6291456]{0:T(1024)(128)(4,1)}), s8[2097152]{0:T(1024)(128)(4,1)S(1)}, s32[]{:S(2)}) async-start(s8[6291456]{0:T(1024)(128)(4,1)} %bitcast.131), calls=%async_computation.1 | async-start | bytes 4194304
  210.5 7.0 %copy-start.30 = (bf16[1024,768]{1,0:T(8,128)(2,1)S(1)}, bf16[1024,768]{1,0:T(8,128)(2,1)}, u32[]{:S(2)}) copy-start(bf16[1024,768]{1,0:T(8,128)(2,1)} %get-tuple-element.64) | copy-start | bytes 4718596
  217.5 7.1 %copy-start.8 = (bf16[1024,768]{1,0:T(8,128)(2,1)S(1)}, bf16[1024,768]{1,0:T(8,128)(2,1)}, u32[]{:S(2)}) copy-start(bf16[1024,768]{1,0:T(8,128)(2,1)} %get-tuple-element.57) | copy-start | bytes 4718596
  473.0 2.9 copy-start.12
  478.6 2.8 copy-start
  482.6 3.0 copy-start.16
  (9 other events, 17.8 us)

commit v5 on v4

--- a/solution.py
+++ b/solution.py
@@ -22,9 +22,8 @@
 MID_ROWS = 256
 MID_CHUNK = 768
 GAP = 0
-UNROLL = 4
-EARLY = 2
-PACE = (3,) * 12
+EARLY = 4
+PACE = (2,) * 12
 
 
 def lasting(microseconds):
@@ -1383,7 +1382,7 @@
     dk_ref[...] = jnp.zeros_like(dk_ref)
     dv_ref[...] = jnp.zeros_like(dv_ref)
 
-    @pl.loop(0, blocks, unroll=UNROLL)
+    @pl.loop(0, blocks, unroll=True)
     def _(b):
         query = spread_heads(q_ref[b] * HD**-0.5, mask)
         upstream = spread_heads(g_ref[b], mask)
@@ -1439,6 +1438,31 @@
         cost_estimate=lasting(44),
         name="attend_back",
     )(index, edge, queries, upstream, keys, values, log_total)
+
+
+def project_kernel(rows_ref, wk_ref, wv_ref, bias_ref, k_ref, v_ref):
+    count, block_rows, features = rows_ref.shape
+    rows = rows_ref[...].reshape(count * block_rows, features)
+    k_ref[...] = nn(rows, wk_ref[...]).astype(k_ref.dtype).reshape(k_ref.shape)
+    values = nn(rows, wv_ref[...]) + bias_ref[...]
+    v_ref[...] = values.astype(v_ref.dtype).reshape(v_ref.shape)
+
+
+def project(rows, wk, wv, bias):
+    slots = rows.shape[0]
+    step = max(n for n in range(1, 21) if slots % n == 0)
+    by_row = pl.BlockSpec((step,) + rows.shape[1:], lambda i: (i, 0, 0))
+    whole = pl.BlockSpec(wk.shape, lambda i: (0, 0))
+    return pl.pallas_call(
+        project_kernel,
+        grid=(slots // step,),
+        out_shape=[jax.ShapeDtypeStruct(rows.shape, jnp.bfloat16)] * 2,
+        in_specs=[by_row, whole, whole, pl.BlockSpec(bias.shape, lambda i: (0, 0))],
+        out_specs=[by_row, by_row],
+        compiler_params=pltpu.CompilerParams(vmem_limit_bytes=40 * MIB),
+        cost_estimate=lasting(13),
+        name="project",
+    )(rows, wk, wv, bias)
 
 
 def layer_norm(hidden, gain, shift):
@@ -1695,13 +1719,8 @@
     queries_bf = (
         jnp.dot(token_rows, full_query, preferred_element_type=jnp.float32) + vectors[0]
     ).astype(jnp.bfloat16)
-    keys_bf = jnp.dot(ext_flat, full_key, preferred_element_type=jnp.float32).astype(jnp.bfloat16)
-    values_bf = (
-        jnp.dot(ext_flat, full_value, preferred_element_type=jnp.float32) + vectors[1]
-    ).astype(jnp.bfloat16)
     query_blocks = queries_bf.reshape(blocks_here, BLK, features)
-    key_blocks = keys_bf.reshape(slots, BLK, features)
-    value_blocks = values_bf.reshape(slots, BLK, features)
+    key_blocks, value_blocks = project(ext_rows, full_key, full_value, vectors[1:2])
     mixed_blocks, log_total = attend(query_blocks, key_blocks, value_blocks, index, edge)
     mixed_bf = mixed_blocks.reshape(length, features)
 

time: 497 us -> 481 us (0.968)
  matrix products: 40.2 us -> 20.9 us
  local copies, waits for them, and re-layouts: 23.6 us -> 28.9 us
    dot_general x2 -> x0, matrix products: 19.3 us -> none  [the longest x1 9.66 us: shards(): jnp.dot(ext_flat, full_value, preferred_element_type=jnp.float32)]
    pallas_call x0 -> x1, Pallas kernels: none -> 14 us  [project(): pl.pallas_call(project_kernel, grid=(slots // step,), out_shape=[jax.Shap...]
    pallas_call x1, Pallas kernels: 210 us -> 198 us  [backward_tail(): pl.pallas_call(functools.partial(tail_kernel, count, capacity), out_shape...]
    unnamed x70 -> x76, local copies, waits for them, and re-layouts: 12.6 us -> 17.9 us
where the time goes in v5:
time: 481 us; the launch traced here: 474 us
  Pallas kernels  415 us (86%)
  local copies, waits for them, and re-layouts  28.9 us (6%)
  matrix products  20.9 us (4%)
  other arithmetic  6.76 us (1%)
    pallas_call x1, Pallas kernels, backward_tail(): pl.pallas_call(functools.partial(tail_kernel, count, capacity), out_shape...  198 us
    pallas_call x1, Pallas kernels, spread(): pl.pallas_call(functools.partial(spread_kernel, count, capacity), out_sha...  112 us
    pallas_call x1, Pallas kernels, middle(): pl.pallas_call(functools.partial(mid_kernel, MID_CHUNK), grid=(length //...  38.1 us
    pallas_call x1, Pallas kernels, attend_back(): pl.pallas_call(backward_kernel, out_shape=[jax.ShapeDtypeStruct(queries.s...  31.3 us
    dot_general x3, matrix products, outer_product(): jnp.einsum('ta,tb->ab', left, right, preferred_element_type=jnp.float32)  18 us
    unnamed x76, local copies, waits for them, and re-layouts  17.9 us
    pallas_call x1, Pallas kernels, project(): pl.pallas_call(project_kernel, grid=(slots // step,), out_shape=[jax.Shap...  14 us
    pallas_call x1, Pallas kernels, attend(): pl.pallas_call(forward_kernel, out_shape=[jax.ShapeDtypeStruct(queries.sh...  13.6 us

profile of v5, /device:TPU:0, one launch (start us, length us, event | category | flops | bytes accessed | tf_op | source)
XLA Modules:
  0.0 473.5 jit_solution(5963845587407334617)
XLA Ops:
  2.8 5.5 %pack_blocks.1 = bf16[64,64,768]{2,1,0:T(8,128)(2,1)} custom-call(s32[64]{0:T(128)} %reshape.292.picked_ref, bf16[16,64,768]{2,1,0:T(8,128)(2,1)} %bitcast.86), custom_call_target="tpu_custom_call" | custom-call | tf_op jit(solution)/shard_map/pack_blocks/pallas_call | solution.py:89
  9.1 111.7 %spread_rows.1 = (bf16[68,64,768]{2,1,0:T(8,128)(2,1)}, bf16[2,8,64,768]{3,2,1,0:T(8,128)(2,1)}, bf16[4,192,768]{2,1,0:T(8,128)(2,1)}, bf16[4,192,768]{2,1,0:T(8...) custom-call(bf16[8,8,64,768]{3,2,1,0:T(8,128)(2,1)} %bitcast.79, ...), custom_call_target="tpu_custom_call" | custom-call | flops 109999996928 | bytes 110000000 | tf_op jit(solution)/shard_map/spread_rows/pallas_call | solution.py:399
  121.9 1.3 copy-done.10
  123.1 1.3 copy-done.11
  124.4 14.0 %project.1 = (bf16[68,64,768]{2,1,0:T(8,128)(2,1)S(1)}, bf16[68,64,768]{2,1,0:T(8,128)(2,1)}) custom-call(bf16[68,64,768]{2,1,0:T(8,128)(2,1)} %get-tuple-element.51.rows_ref.x_hbm, bf16[768,768]{1,0:T(8,128)(2,1)S(1)} %bitcast.76, bf16[768,768]{1,0:T(8,128)(2,1)S(1)} %bitcast.78, f32[1,768]{1,0:T(1,128)S(1)} %slice.91.bias_ref), custom_call_target="tpu_custom_call" | custom-call | flops 12999999488 | bytes 13000000 | tf_op jit(solution)/shard_map/project/pallas_call | solution.py:1456
  138.4 2.7 copy-done.12
  141.2 2.9 fusion
  145.2 2.9 copy-done.13
  148.1 13.6 %attend.1 = (bf16[16,64,768]{2,1,0:T(8,128)(2,1)S(1)}, f32[16,1,768]{2,1,0:T(1,128)S(1)}) custom-call(s32[128]{0:T(128)S(1)} %reshape.291.index_ref, s32[2]{0:T(128)S(1)} %add_convert_fusion.1.edge_ref, bf16[16,64,768]{2,1,0:T(8,128)(2,1)S(1)} %bitcast.70, bf16[68,64,768]{2,1,0:T(8,128)(2,1)S(1)} %copy-done.13, bf16[68,64,768]{2,1,0:T(8,128)(2,1)} %get-tuple-element.55.v_ref), custom_call_target="tpu_custom_call" | custom-call | flops 36999999488 | bytes 37000000 | tf_op jit(solution)/shard_map/attend/pallas_call | solution.py:1338
  161.7 1.1 copy-done.8
  164.2 38.1 %middle.1 = (bf16[1024,768]{1,0:T(8,128)(2,1)}, f32[1024,768]{1,0:T(8,128)}, bf16[1024,768]{1,0:T(8,128)(2,1)}, bf16[1024,768]{1,0:T(8,128)(2,1)}, bf16[1024,307...) custom-call(bf16[1024,768]{1,0:T(8,128)(2,1)} %bitcast.73, ...), custom_call_target="tpu_custom_call" | custom-call | flops 49999998976 | bytes 50000000 | tf_op jit(solution)/shard_map/middle/pallas_call | solution.py:1583
  203.6 1.4 reduce.7
  206.7 4.1 convolution_convert_fusion.2
  210.7 6.8 %convolution_convert_fusion = bf16[768,3072]{1,0:T(8,128)(2,1)} fusion(bf16[1024,768]{1,0:T(8,128)(2,1)S(1)} %copy-done.32, bf16[1024,3072]{1,0:T(8,128)(2,1)S(1)} %copy-done.31), kind=kOutput, calls=%fused_computation | convolution fusion | flops 4834197504 | bytes 12582912 | tf_op jit(solution)/shard_map/ta,tb->ab/dot_general | solution.py:1628
  217.6 7.1 %convolution_convert_fusion.1 = bf16[3072,768]{1,0:T(8,128)(2,1)} fusion(bf16[1024,3072]{1,0:T(8,128)(2,1)S(1)} %bitcast.119, bf16[1024,768]{1,0:T(8,128)(2,1)S(1)} %copy-done.33), kind=kOutput, calls=%fused_computation.1 | convolution fusion | flops 4834197504 | bytes 12582912 | tf_op jit(solution)/shard_map/ta,tb->ab/dot_general | solution.py:1628
  224.7 31.3 %attend_back.1 = (bf16[16,64,768]{2,1,0:T(8,128)(2,1)S(1)}, bf16[68,64,768]{2,1,0:T(8,128)(2,1)}, bf16[68,64,768]{2,1,0:T(8,128)(2,1)}) custom-call(s32[128]{0:T(128)S(1)} %reshape.291.index_ref, s32[2]{0:T(128)S(1)} %add_convert_fusion.1.edge_ref, bf16[16,64,768]{2,1,0:T(8,128)(2,1)S(1)} %bitcast.71, bf16[16,64,768]{2,1,0:T(8,128)(2,1)S(1)} %bitcast.72, ...), custom_call_target="tpu_custom_call" | custom-call | flops 44000002048 | bytes 44000000 | tf_op jit(solution)/shard_map/attend_back/pallas_call | solution.py:1420
  256.0 1.1 copy-done.14
  257.1 198.3 %backward_tail.1 = (bf16[8,8,64,768]{3,2,1,0:T(8,128)(2,1)}, bf16[2,64,768]{2,1,0:T(8,128)(2,1)}, bf16[8,64,768]{2,1,0:T(8,128)(2,1)}, f32[16,256]{1,0:T(8,128)}...) custom-call(bf16[16,64,768]{2,1,0:T(8,128)(2,1)} %copy-done.14, bf16[68,64,768]{2,1,0:T(8,128)(2,1)} %get-tuple-element.64.dk_hbm, ...), custom_call_target="tpu_custom_call" | custom-call | flops 149999992832 | bytes 150000000 | tf_op jit(solution)/shard_map/backward_tail/pallas_call | solution.py:1169
  455.4 3.3 fusion.8
  458.7 1.7 pad_maximum_fusion
  460.4 1.2 copy-done.15
  461.6 1.6 slice.126
  464.3 2.8 copy-done
  468.2 3.0 unpack_grads.1
  (112 shorter events, 13.3 us)
Async XLA Ops:
  1.6 6.7 %copy-start.19 = (pred[8,48]{1,0:T(8,128)(4,1)}, pred[8,48]{1,0:T(8,128)(4,1)S(1)}, u32[]{:S(2)}) copy-start(pred[8,48]{1,0:T(8,128)(4,1)S(1)} %get-tuple-element.80) | copy-start | bytes 1156
  1.9 142.9 %copy-start.16 = (s32[8,48]{1,0:T(8,128)}, s32[8,48]{1,0:T(8,128)S(1)}, u32[]{:S(2)}) copy-start(s32[8,48]{1,0:T(8,128)S(1)} %convert_reduce_fusion) | copy-start | bytes 4612
  2.7 5.5 %copy-start.21 = (bf16[768]{0:T(1024)(128)(2,1)S(1)}, bf16[768]{0:T(1024)(128)(2,1)}, u32[]{:S(2)}) copy-start(bf16[768]{0:T(1024)(128)(2,1)} %param.31) | copy-start | bytes 4612
  2.7 5.6 %copy-start.22 = (bf16[192]{0:T(256)(128)(2,1)S(1)}, bf16[192]{0:T(256)(128)(2,1)}, u32[]{:S(2)}) copy-start(bf16[192]{0:T(256)(128)(2,1)} %param.22) | copy-start | bytes 1156
  2.7 5.6 %copy-start.23 = (bf16[192]{0:T(256)(128)(2,1)S(1)}, bf16[192]{0:T(256)(128)(2,1)}, u32[]{:S(2)}) copy-start(bf16[192]{0:T(256)(128)(2,1)} %param.25) | copy-start | bytes 1156
  2.7 5.6 %copy-start.24 = (bf16[192]{0:T(256)(128)(2,1)S(1)}, bf16[192]{0:T(256)(128)(2,1)}, u32[]{:S(2)}) copy-start(bf16[192]{0:T(256)(128)(2,1)} %param.27) | copy-start | bytes 1156
  2.8 5.6 %copy-start.25 = (bf16[192]{0:T(256)(128)(2,1)S(1)}, bf16[192]{0:T(256)(128)(2,1)}, u32[]{:S(2)}) copy-start(bf16[192]{0:T(256)(128)(2,1)} %param.28) | copy-start | bytes 1156
  2.8 5.6 %copy-start.26 = (bf16[192]{0:T(256)(128)(2,1)S(1)}, bf16[192]{0:T(256)(128)(2,1)}, u32[]{:S(2)}) copy-start(bf16[192]{0:T(256)(128)(2,1)} %param.29) | copy-start | bytes 1156
  2.8 5.6 %copy-start.27 = (bf16[192]{0:T(256)(128)(2,1)S(1)}, bf16[192]{0:T(256)(128)(2,1)}, u32[]{:S(2)}) copy-start(bf16[192]{0:T(256)(128)(2,1)} %param.33) | copy-start | bytes 1156
  2.8 5.6 %copy-start.28 = (bf16[192]{0:T(256)(128)(2,1)S(1)}, bf16[192]{0:T(256)(128)(2,1)}, u32[]{:S(2)}) copy-start(bf16[192]{0:T(256)(128)(2,1)} %param.34) | copy-start | bytes 1156
  2.8 5.6 %copy-start.29 = (bf16[192]{0:T(256)(128)(2,1)S(1)}, bf16[192]{0:T(256)(128)(2,1)}, u32[]{:S(2)}) copy-start(bf16[192]{0:T(256)(128)(2,1)} %param.35) | copy-start | bytes 1156
  124.4 16.8 %copy-start.30 = (bf16[4,192,768]{2,1,0:T(8,128)(2,1)S(1)}, bf16[4,192,768]{2,1,0:T(8,128)(2,1)}, u32[]{:S(2)}) copy-start(bf16[4,192,768]{2,1,0:T(8,128)(2,1)} %get-tuple-element.49) | copy-start | bytes 3538948
  145.2 2.9 copy-start.13
  148.1 76.6 %copy-start.5 = (s32[2]{0:T(128)}, s32[2]{0:T(128)S(1)}, u32[]{:S(2)}) copy-start(s32[2]{0:T(128)S(1)} %add_convert_fusion.1.edge_ref) | copy-start | bytes 28
  164.2 42.5 %copy-start.9 = (bf16[16,64,768]{2,1,0:T(8,128)(2,1)S(1)}, bf16[16,64,768]{2,1,0:T(8,128)(2,1)}, u32[]{:S(2)}) copy-start(bf16[16,64,768]{2,1,0:T(8,128)(2,1)} %copy-done.8) | copy-start | bytes 4718596
  206.0 4.7 copy-start.32
  206.7 4.1 copy-start.31
  206.7 10.9 %slice-start = ((s8[6291456]{0:T(1024)(128)(4,1)}), s8[4194304]{0:T(1024)(128)(4,1)S(1)}, s32[]{:S(2)}) async-start(s8[6291456]{0:T(1024)(128)(4,1)} %bitcast.118), calls=%async_computation | async-start | bytes 8388608
  210.7 6.8 %slice-start.1 = ((s8[6291456]{0:T(1024)(128)(4,1)}), s8[2097152]{0:T(1024)(128)(4,1)S(1)}, s32[]{:S(2)}) async-start(s8[6291456]{0:T(1024)(128)(4,1)} %bitcast.118), calls=%async_computation.1 | async-start | bytes 4194304
  210.7 6.8 %copy-start.33 = (bf16[1024,768]{1,0:T(8,128)(2,1)S(1)}, bf16[1024,768]{1,0:T(8,128)(2,1)}, u32[]{:S(2)}) copy-start(bf16[1024,768]{1,0:T(8,128)(2,1)} %get-tuple-element.68) | copy-start | bytes 4718596
  217.6 7.1 %copy-start.7 = (bf16[1024,768]{1,0:T(8,128)(2,1)S(1)}, bf16[1024,768]{1,0:T(8,128)(2,1)}, u32[]{:S(2)}) copy-start(bf16[1024,768]{1,0:T(8,128)(2,1)} %get-tuple-element.61) | copy-start | bytes 4718596
  458.7 2.9 copy-start.15
  464.3 2.8 copy-start
  468.2 3.0 copy-start.18
  (12 other events, 23.1 us)

commit v6 on v5

--- a/solution.py
+++ b/solution.py
@@ -1261,7 +1261,7 @@
             out_specs=pl.BlockSpec(base.shape, lambda i, *t: (0, 0, 0)),
             scratch_shapes=[pltpu.VMEM(base.shape, jnp.float32)],
         ),
-        compiler_params=pltpu.CompilerParams(vmem_limit_bytes=32 * MIB),
+        compiler_params=pltpu.CompilerParams(vmem_limit_bytes=58 * MIB),
         name="unpack_grads",
     )(picked, filled, edge, base, back, rim, glob)
 
@@ -1354,7 +1354,7 @@
                 pl.BlockSpec((blocks, 1, LANES), column),
             ],
         ),
-        compiler_params=pltpu.CompilerParams(vmem_limit_bytes=40 * MIB),
+        compiler_params=pltpu.CompilerParams(vmem_limit_bytes=58 * MIB),
         cost_estimate=lasting(37),
         name="attend",
     )(index, edge, queries, keys, values)
@@ -1434,7 +1434,7 @@
                 pltpu.VMEM((blocks + EXTRA, block_rows, LANES), jnp.float32),
             ],
         ),
-        compiler_params=pltpu.CompilerParams(vmem_limit_bytes=48 * MIB),
+        compiler_params=pltpu.CompilerParams(vmem_limit_bytes=58 * MIB),
         cost_estimate=lasting(44),
         name="attend_back",
     )(index, edge, queries, upstream, keys, values, log_total)
@@ -1459,7 +1459,7 @@
         out_shape=[jax.ShapeDtypeStruct(rows.shape, jnp.bfloat16)] * 2,
         in_specs=[by_row, whole, whole, pl.BlockSpec(bias.shape, lambda i: (0, 0))],
         out_specs=[by_row, by_row],
-        compiler_params=pltpu.CompilerParams(vmem_limit_bytes=40 * MIB),
+        compiler_params=pltpu.CompilerParams(vmem_limit_bytes=58 * MIB),
         cost_estimate=lasting(13),
         name="project",
     )(rows, wk, wv, bias)

time: 481 us -> 477 us (level)
  local copies, waits for them, and re-layouts: 28.9 us -> 16.2 us
  Pallas kernels: 415 us -> 423 us
    unnamed x76 -> x48, local copies, waits for them, and re-layouts: 17.9 us -> 2.7 us
    pallas_call x1, Pallas kernels: 3.04 us -> 8.65 us  [unpack_grads(): pl.pallas_call(functools.partial(unpack_kernel, capacity), out_shape=jax....]
where the time goes in v6:
time: 477 us; the launch traced here: 469 us
  Pallas kernels  423 us (89%)
  matrix products  20.7 us (4%)
  local copies, waits for them, and re-layouts  16.2 us (3%)
  other arithmetic  7.27 us (2%)
    pallas_call x1, Pallas kernels, backward_tail(): pl.pallas_call(functools.partial(tail_kernel, count, capacity), out_shape...  198 us
    pallas_call x1, Pallas kernels, spread(): pl.pallas_call(functools.partial(spread_kernel, count, capacity), out_sha...  112 us
    pallas_call x1, Pallas kernels, middle(): pl.pallas_call(functools.partial(mid_kernel, MID_CHUNK), grid=(length //...  38.1 us
    pallas_call x1, Pallas kernels, attend_back(): pl.pallas_call(backward_kernel, out_shape=[jax.ShapeDtypeStruct(queries.s...  31.3 us
    dot_general x3, matrix products, outer_product(): jnp.einsum('ta,tb->ab', left, right, preferred_element_type=jnp.float32)  18 us
    pallas_call x1, Pallas kernels, attend(): pl.pallas_call(forward_kernel, out_shape=[jax.ShapeDtypeStruct(queries.sh...  14.9 us
    pallas_call x1, Pallas kernels, project(): pl.pallas_call(project_kernel, grid=(slots // step,), out_shape=[jax.Shap...  14.7 us

profile of v6, /device:TPU:0, one launch (start us, length us, event | category | flops | bytes accessed | tf_op | source)
XLA Modules:
  0.0 468.7 jit_solution(8823944422782294090)
XLA Ops:
  0.7 0.8 copy.42
  2.8 5.4 %pack_blocks.1 = bf16[64,64,768]{2,1,0:T(8,128)(2,1)} custom-call(s32[64]{0:T(128)} %reshape.292.picked_ref, bf16[16,64,768]{2,1,0:T(8,128)(2,1)} %bitcast.79), custom_call_target="tpu_custom_call" | custom-call | tf_op jit(solution)/shard_map/pack_blocks/pallas_call | solution.py:89
  9.0 111.7 %spread_rows.1 = (bf16[68,64,768]{2,1,0:T(8,128)(2,1)}, bf16[2,8,64,768]{3,2,1,0:T(8,128)(2,1)}, bf16[4,192,768]{2,1,0:T(8,128)(2,1)}, bf16[4,192,768]{2,1,0:T(8...) custom-call(bf16[8,8,64,768]{3,2,1,0:T(8,128)(2,1)} %bitcast.69, ...), custom_call_target="tpu_custom_call" | custom-call | flops 109999996928 | bytes 110000000 | tf_op jit(solution)/shard_map/spread_rows/pallas_call | solution.py:399
  120.7 0.8 convert_bitcast_fusion
  122.3 14.7 %project.1 = (bf16[68,64,768]{2,1,0:T(8,128)(2,1)}, bf16[68,64,768]{2,1,0:T(8,128)(2,1)}) custom-call(bf16[68,64,768]{2,1,0:T(8,128)(2,1)} %get-tuple-element.51.rows_ref.x_hbm, bf16[768,768]{1,0:T(8,128)(2,1)} %bitcast.112, bf16[768,768]{1,0:T(8,128)(2,1)} %bitcast.114, f32[1,768]{1,0:T(1,128)} %slice.91.bias_ref), custom_call_target="tpu_custom_call" | custom-call | flops 12999999488 | bytes 13000000 | tf_op jit(solution)/shard_map/project/pallas_call | solution.py:1456
  137.1 2.8 fusion
  139.9 1.6 copy.44
  142.9 14.9 %attend.1 = (bf16[16,64,768]{2,1,0:T(8,128)(2,1)}, f32[16,1,768]{2,1,0:T(1,128)}) custom-call(s32[128]{0:T(128)} %reshape.291.index_ref, s32[2]{0:T(128)} %add_convert_fusion.1.edge_ref, bf16[16,64,768]{2,1,0:T(8,128)(2,1)} %bitcast.77, bf16[68,64,768]{2,1,0:T(8,128)(2,1)} %get-tuple-element.54.k_ref, bf16[68,64,768]{2,1,0:T(8,128)(2,1)} %get-tuple-element.55.v_ref), custom_call_target="tpu_custom_call" | custom-call | flops 36999999488 | bytes 37000000 | tf_op jit(solution)/shard_map/attend/pallas_call | solution.py:1338
  157.8 0.7 reshape.301.vec_ref
  159.1 38.1 %middle.1 = (bf16[1024,768]{1,0:T(8,128)(2,1)}, f32[1024,768]{1,0:T(8,128)}, bf16[1024,768]{1,0:T(8,128)(2,1)}, bf16[1024,768]{1,0:T(8,128)(2,1)}, bf16[1024,307...) custom-call(bf16[1024,768]{1,0:T(8,128)(2,1)} %bitcast.108, ...), custom_call_target="tpu_custom_call" | custom-call | flops 49999998976 | bytes 50000000 | tf_op jit(solution)/shard_map/middle/pallas_call | solution.py:1583
  197.2 0.7 concatenate.18
  198.6 1.4 reduce.7
  200.1 0.9 slice_reduce_fusion
  201.6 4.0 convolution_convert_fusion.2
  205.6 6.8 %convolution_convert_fusion = bf16[768,3072]{1,0:T(8,128)(2,1)} fusion(bf16[1024,768]{1,0:T(8,128)(2,1)S(1)} %copy-done.18, bf16[1024,3072]{1,0:T(8,128)(2,1)S(1)} %copy-done.17), kind=kOutput, calls=%fused_computation | convolution fusion | flops 4834197504 | bytes 12582912 | tf_op jit(solution)/shard_map/ta,tb->ab/dot_general | solution.py:1628
  212.5 7.1 %convolution_convert_fusion.1 = bf16[3072,768]{1,0:T(8,128)(2,1)} fusion(bf16[1024,3072]{1,0:T(8,128)(2,1)S(1)} %bitcast.119, bf16[1024,768]{1,0:T(8,128)(2,1)S(1)} %copy-done.19), kind=kOutput, calls=%fused_computation.1 | convolution fusion | flops 4834197504 | bytes 12582912 | tf_op jit(solution)/shard_map/ta,tb->ab/dot_general | solution.py:1628
  219.6 31.3 %attend_back.1 = (bf16[16,64,768]{2,1,0:T(8,128)(2,1)}, bf16[68,64,768]{2,1,0:T(8,128)(2,1)}, bf16[68,64,768]{2,1,0:T(8,128)(2,1)}) custom-call(s32[128]{0:T(128)} %reshape.291.index_ref, s32[2]{0:T(128)} %add_convert_fusion.1.edge_ref, bf16[16,64,768]{2,1,0:T(8,128)(2,1)} %bitcast.78, bf16[16,64,768]{2,1,0:T(8,128)(2,1)} %bitcast.107, ...), custom_call_target="tpu_custom_call" | custom-call | flops 44000002048 | bytes 44000000 | tf_op jit(solution)/shard_map/attend_back/pallas_call | solution.py:1420
  250.9 198.3 %backward_tail.1 = (bf16[8,8,64,768]{3,2,1,0:T(8,128)(2,1)}, bf16[2,64,768]{2,1,0:T(8,128)(2,1)}, bf16[8,64,768]{2,1,0:T(8,128)(2,1)}, f32[16,256]{1,0:T(8,128)}...) custom-call(bf16[16,64,768]{2,1,0:T(8,128)(2,1)} %get-tuple-element.63.dq_hbm, ...), custom_call_target="tpu_custom_call" | custom-call | flops 149999992832 | bytes 150000000 | tf_op jit(solution)/shard_map/backward_tail/pallas_call | solution.py:1169
  449.2 3.3 fusion.8
  452.5 1.7 pad_maximum_fusion
  454.2 1.2 copy-done
  455.3 1.6 slice.126
  457.8 8.6 %unpack_grads.1 = bf16[16,64,768]{2,1,0:T(8,128)(2,1)} custom-call(s32[64]{0:T(128)} %reshape.292.picked_ref, s32[64]{0:T(128)} %reshape.317.filled_ref, s32[2]{0:T(128)} %add_convert_fusion.1.edge_ref, f32[16,64,768]{2,1,0:T(8,128)} %bitcast.70, bf16[8,8,64,768]{3,2,1,0:T(8,128)(2,1)} %get-tuple-element.75.back_ref, ...), custom_call_target="tpu_custom_call" | custom-call | tf_op jit(solution)/shard_map/unpack_grads/pallas_call | solution.py:1249
  467.0 0.7 reshape.314
  (84 shorter events, 8.2 us)
Async XLA Ops:
  1.6 6.6 %copy-start.5 = (pred[8,48]{1,0:T(8,128)(4,1)}, pred[8,48]{1,0:T(8,128)(4,1)S(1)}, u32[]{:S(2)}) copy-start(pred[8,48]{1,0:T(8,128)(4,1)S(1)} %get-tuple-element.80) | copy-start | bytes 1156
  1.9 139.6 %copy-start.2 = (s32[8,48]{1,0:T(8,128)}, s32[8,48]{1,0:T(8,128)S(1)}, u32[]{:S(2)}) copy-start(s32[8,48]{1,0:T(8,128)S(1)} %convert_reduce_fusion) | copy-start | bytes 4612
  2.7 5.5 %copy-start.7 = (bf16[768]{0:T(1024)(128)(2,1)S(1)}, bf16[768]{0:T(1024)(128)(2,1)}, u32[]{:S(2)}) copy-start(bf16[768]{0:T(1024)(128)(2,1)} %param.31) | copy-start | bytes 4612
  2.7 5.5 %copy-start.8 = (bf16[192]{0:T(256)(128)(2,1)S(1)}, bf16[192]{0:T(256)(128)(2,1)}, u32[]{:S(2)}) copy-start(bf16[192]{0:T(256)(128)(2,1)} %param.22) | copy-start | bytes 1156
  2.7 5.5 %copy-start.9 = (bf16[192]{0:T(256)(128)(2,1)S(1)}, bf16[192]{0:T(256)(128)(2,1)}, u32[]{:S(2)}) copy-start(bf16[192]{0:T(256)(128)(2,1)} %param.25) | copy-start | bytes 1156
  2.7 5.5 %copy-start.10 = (bf16[192]{0:T(256)(128)(2,1)S(1)}, bf16[192]{0:T(256)(128)(2,1)}, u32[]{:S(2)}) copy-start(bf16[192]{0:T(256)(128)(2,1)} %param.27) | copy-start | bytes 1156
  2.8 5.5 %copy-start.11 = (bf16[192]{0:T(256)(128)(2,1)S(1)}, bf16[192]{0:T(256)(128)(2,1)}, u32[]{:S(2)}) copy-start(bf16[192]{0:T(256)(128)(2,1)} %param.28) | copy-start | bytes 1156
  2.8 5.5 %copy-start.12 = (bf16[192]{0:T(256)(128)(2,1)S(1)}, bf16[192]{0:T(256)(128)(2,1)}, u32[]{:S(2)}) copy-start(bf16[192]{0:T(256)(128)(2,1)} %param.29) | copy-start | bytes 1156
  2.8 5.5 %copy-start.13 = (bf16[192]{0:T(256)(128)(2,1)S(1)}, bf16[192]{0:T(256)(128)(2,1)}, u32[]{:S(2)}) copy-start(bf16[192]{0:T(256)(128)(2,1)} %param.33) | copy-start | bytes 1156
  2.8 5.5 %copy-start.14 = (bf16[192]{0:T(256)(128)(2,1)S(1)}, bf16[192]{0:T(256)(128)(2,1)}, u32[]{:S(2)}) copy-start(bf16[192]{0:T(256)(128)(2,1)} %param.34) | copy-start | bytes 1156
  2.8 5.5 %copy-start.15 = (bf16[192]{0:T(256)(128)(2,1)S(1)}, bf16[192]{0:T(256)(128)(2,1)}, u32[]{:S(2)}) copy-start(bf16[192]{0:T(256)(128)(2,1)} %param.35) | copy-start | bytes 1156
  122.3 14.8 %copy-start.1 = (bf16[1,1024,768]{2,1,0:T(8,128)(2,1)S(1)}, bf16[1,1024,768]{2,1,0:T(8,128)(2,1)}, u32[]{:S(2)}) copy-start(bf16[1,1024,768]{2,1,0:T(8,128)(2,1)} %param.18) | copy-start | bytes 4718596
  159.1 42.5 %copy-start.16 = (bf16[16,64,768]{2,1,0:T(8,128)(2,1)S(1)}, bf16[16,64,768]{2,1,0:T(8,128)(2,1)}, u32[]{:S(2)}) copy-start(bf16[16,64,768]{2,1,0:T(8,128)(2,1)} %get-tuple-element.56) | copy-start | bytes 4718596
  201.0 4.7 copy-start.18
  201.6 4.0 copy-start.17
  201.6 10.9 %slice-start = ((s8[6291456]{0:T(1024)(128)(4,1)}), s8[4194304]{0:T(1024)(128)(4,1)S(1)}, s32[]{:S(2)}) async-start(s8[6291456]{0:T(1024)(128)(4,1)} %bitcast.118), calls=%async_computation | async-start | bytes 8388608
  205.6 6.9 %slice-start.1 = ((s8[6291456]{0:T(1024)(128)(4,1)}), s8[2097152]{0:T(1024)(128)(4,1)S(1)}, s32[]{:S(2)}) async-start(s8[6291456]{0:T(1024)(128)(4,1)} %bitcast.118), calls=%async_computation.1 | async-start | bytes 4194304
  205.6 6.9 %copy-start.19 = (bf16[1024,768]{1,0:T(8,128)(2,1)S(1)}, bf16[1024,768]{1,0:T(8,128)(2,1)}, u32[]{:S(2)}) copy-start(bf16[1024,768]{1,0:T(8,128)(2,1)} %get-tuple-element.68) | copy-start | bytes 4718596
  452.5 2.9 copy-start
  455.3 1.6 copy-start.3
  455.3 1.6 copy-start.6
  457.8 8.7 %copy-start.4 = (f32[16,256]{1,0:T(8,128)S(1)}, f32[16,256]{1,0:T(8,128)}, u32[]{:S(2)}) copy-start(f32[16,256]{1,0:T(8,128)} %get-tuple-element.79) | copy-start | bytes 49156
